TPU v7x, 256 devices: a whole 4x4x8 slice. The times are simulated.
256 devices in a mesh: dp: 4 (over y), tensor: 64 (over x, z, core).
Axes of the slice: x: 4, y: 4, z: 8, core: 2. Of those that a mesh axis runs over, the one named last changes fastest.
Arguments:
- tokens: bfloat16 [4, 8192, 1536], P('dp', 'tensor'), may hold values from -6 to 6
- attn_gain: float32 [1536], replicated, may hold values from 0.1 to 1.9
- qkv_weight: bfloat16 [1536, 2560], P(None, 'dp'), may hold values from -0.25 to 0.25
- out_weight: bfloat16 [1536, 1536], P('dp'), may hold values from -0.15625 to 0.15625
- prefix_cache: bfloat16 [4, 512, 2, 512], P('dp', 'tensor'), may hold values from -640 to 640
- lengths: int32 [4, 256], P('dp'), may hold values from 1 to 384, 8192 in all within a row
- ffn_gain: float32 [1536], replicated, may hold values from 0.1 to 1.9
- expert_ids: int32 [4, 8192, 8], P('dp', 'tensor'), may hold values from 0 to 31, all different within a row; in each aligned block of 128 rows (0 to 127, 128 to 255, ..., all dimensions but the last counted through in order) at most 40 rows name the same one
- gate_weights: float32 [4, 8192, 8], P('dp', 'tensor'), may hold values from 0.05 to 0.5
- expert_in: bfloat16 [64, 1536, 512], P('tensor'), may hold values from -0.15625 to 0.15625
- expert_out: bfloat16 [64, 256, 1536], P('tensor'), may hold values from -0.25 to 0.25
Outputs:
- hidden_state: bfloat16 [4, 8192, 1536], P('dp', 'tensor')
- mixed: bfloat16 [4, 8192, 1536], P('dp', 'tensor')
Inputs may be any that keep to these rules, and one draw needn't show every extreme that they name: `lengths`: each group's 256 requests fill its 8192 suffix positions in order, and the longest holds exactly 384 tokens. `expert_ids`: each token names 8 different experts; among the 128 tokens of one device no expert is named more than 40 times, a bound that some block reaches.
All inputs are finite; a program needn't handle non-finite values.
Results may differ from a plain program's by a relative error of at most 0.014.
The roundings to bfloat16 on the way count: a program that leaves them out, or rounds other values in their place, can miss the bound.
Values may be sent and summed in bfloat16 or wider, within the bound.
No kernel may reach another device: no remote copies, remote signals or barrier semaphores. Data moves between devices by JAX's collectives and lax.ppermute only.
A program may use at most 128 MiB of HBM per device.

v0:
```python
import jax
import jax.numpy as jnp
from jax import lax
from jax.sharding import PartitionSpec as P

HEADS = 24
KV_HEADS = 8
HEAD_DIM = 64
EXPERTS = 32
TOPK = 8
SHIFTS = 2
CAP = 40


EPS = 1e-06
THETA = 10000.0


def from_behind(value, axis, steps):
    count = lax.axis_size(axis)
    first, last = (max(0, -steps), min(count, count - steps))
    return lax.ppermute(value, axis, [(source, source + steps) for source in range(first, last)])


def rms_norm(x, gain):
    values = x.astype(jnp.float32)
    mean_sq = jnp.mean(values * values, axis=-1, keepdims=True)
    return (values * lax.rsqrt(mean_sq + EPS) * gain).astype(jnp.bfloat16)


def rotary(x, positions):
    half = x.shape[-1] // 2
    freqs = THETA ** (-jnp.arange(half, dtype=jnp.float32) * 2.0 / x.shape[-1])
    angles = positions.astype(jnp.float32)[:, None] * freqs[None, :]
    cosine = jnp.concatenate([jnp.cos(angles), jnp.cos(angles)], axis=-1)[:, None, :]
    sine = jnp.concatenate([jnp.sin(angles), jnp.sin(angles)], axis=-1)[:, None, :]
    turned = jnp.concatenate([-x[..., half:], x[..., :half]], axis=-1)
    return x * cosine + turned * sine


def request_info(index, lengths):
    ends = jnp.cumsum(lengths, dtype=jnp.int32)
    before = ends[None, :] <= index[:, None]
    segment = jnp.sum(before.astype(jnp.int32), axis=1, dtype=jnp.int32)
    start = jnp.sum(jnp.where(before, lengths[None, :], 0), axis=1, dtype=jnp.int32)
    return (segment, index - start)


def merge_block(carry, scores, values, visible):
    best, total, acc = carry
    if visible is not None:
        scores = jnp.where(visible, scores, -1e30)
    newest = jnp.maximum(best, jnp.max(scores, axis=-1))
    probs = jnp.exp(scores - newest[..., None])
    if visible is not None:
        probs = jnp.where(visible, probs, 0.0)
    decay = jnp.exp(best - newest)
    total = total * decay + jnp.sum(probs, axis=-1)
    acc = acc * decay[..., None] + jnp.einsum(
        "tgrn,ngd->tgrd", probs.astype(jnp.bfloat16), values, preferred_element_type=jnp.float32
    )
    return (newest, total, acc)


def shards(
    tokens,
    attn_gain,
    qkv_weight,
    out_weight,
    prefix_cache,
    lengths,
    ffn_gain,
    expert_ids,
    gate_weights,
    expert_in,
    expert_out,
):
    rows = tokens.shape[1]
    model = tokens.shape[2]
    head_cols = HEADS * HEAD_DIM
    kv_cols = KV_HEADS * HEAD_DIM
    ratio = HEADS // KV_HEADS
    scale = 1.0 / HEAD_DIM**0.5
    lanes = lax.axis_size("tensor")
    prefix_len = prefix_cache.shape[1] * lanes
    own_lengths = lengths[0]
    inputs = tokens[0]
    normed = rms_norm(inputs, attn_gain)
    full_qkv, full_out = (
        lax.all_gather(qkv_weight, "dp", axis=1, tiled=True),
        lax.all_gather(out_weight, "dp", axis=0, tiled=True),
    )
    qkv = jnp.dot(normed, full_qkv, preferred_element_type=jnp.float32).astype(jnp.bfloat16)
    lane = lax.axis_index("tensor")
    q_index = lane * rows + jnp.arange(rows, dtype=jnp.int32)
    q_segment, offset = request_info(q_index, own_lengths)
    positions = prefix_len + offset
    query = rotary(
        qkv[:, :head_cols].astype(jnp.float32).reshape(rows, HEADS, HEAD_DIM), positions
    ).astype(jnp.bfloat16)
    query = query.reshape(rows, KV_HEADS, ratio, HEAD_DIM)
    keys = rotary(
        qkv[:, head_cols : head_cols + kv_cols]
        .astype(jnp.float32)
        .reshape(rows, KV_HEADS, HEAD_DIM),
        positions,
    ).astype(jnp.bfloat16)
    local_pairs = jnp.stack([keys.reshape(rows, kv_cols), qkv[:, head_cols + kv_cols :]], axis=1)
    start_carry = (
        jnp.full((rows, KV_HEADS, ratio), -1e30, jnp.float32),
        jnp.zeros((rows, KV_HEADS, ratio), jnp.float32),
        jnp.zeros((rows, KV_HEADS, ratio, HEAD_DIM), jnp.float32),
    )
    piece = lax.all_gather(prefix_cache[0], "tensor", axis=0, tiled=True)
    count = piece.shape[0]
    cached_keys = piece[:, 0].reshape(count, KV_HEADS, HEAD_DIM)
    cached_values = piece[:, 1].reshape(count, KV_HEADS, HEAD_DIM)
    scores = (
        jnp.einsum("tgrd,ngd->tgrn", query, cached_keys, preferred_element_type=jnp.float32) * scale
    )
    carry = merge_block(start_carry, scores, cached_values, None)
    window = local_pairs[None]
    for bit in range(SHIFTS):
        earlier = from_behind(window, "tensor", 2**bit)
        window = jnp.concatenate([window, earlier], axis=0)
    depth = window.shape[0]
    k_index = (
        (lane - jnp.arange(depth, dtype=jnp.int32))[:, None] * rows
        + jnp.arange(rows, dtype=jnp.int32)[None, :]
    ).reshape(-1)
    k_segment, unused = request_info(k_index, own_lengths)
    visible = (
        (k_index[None, :] >= 0)
        & (k_index[None, :] <= q_index[:, None])
        & (k_segment[None, :] == q_segment[:, None])
    )
    suffix_pairs = window.reshape(depth * rows, 2, kv_cols)
    suffix_keys = suffix_pairs[:, 0].reshape(depth * rows, KV_HEADS, HEAD_DIM)
    suffix_values = suffix_pairs[:, 1].reshape(depth * rows, KV_HEADS, HEAD_DIM)
    scores = (
        jnp.einsum("tgrd,ngd->tgrn", query, suffix_keys, preferred_element_type=jnp.float32) * scale
    )
    best, total, acc = merge_block(carry, scores, suffix_values, visible[:, None, None, :])
    attended = (acc / total[..., None]).astype(jnp.bfloat16).reshape(rows, head_cols)
    projected = jnp.dot(attended, full_out, preferred_element_type=jnp.float32)
    hidden_state = (inputs.astype(jnp.float32) + projected).astype(jnp.bfloat16)
    moe_input = rms_norm(hidden_state, ffn_gain)
    total_units = expert_in.shape[0] * lanes
    parts = total_units // EXPERTS
    unit_ff = expert_in.shape[2] // 2
    flat_ids = expert_ids[0].reshape(-1)
    onehot = (flat_ids[:, None] == jnp.arange(EXPERTS, dtype=jnp.int32)[None, :]).astype(jnp.int32)
    earlier_count = jnp.cumsum(onehot, axis=0, dtype=jnp.int32) - onehot
    slots = jnp.sum(earlier_count * onehot, axis=1, dtype=jnp.int32)
    unit_ids = flat_ids[:, None] * parts + jnp.arange(parts, dtype=jnp.int32)[None, :]
    target = (unit_ids * CAP + slots[:, None]).reshape(-1)
    row_of = jnp.repeat(jnp.arange(rows, dtype=jnp.int32), TOPK * parts)
    source = jnp.full((total_units * CAP,), rows, jnp.int32).at[target].set(row_of)
    padded_input = jnp.concatenate([moe_input, jnp.zeros((1, model), jnp.bfloat16)], axis=0)
    outgoing = padded_input[source]
    arrived = lax.all_to_all(
        outgoing.reshape(total_units, CAP, model), "tensor", split_axis=0, concat_axis=1, tiled=True
    )
    inner = jnp.einsum("erd,edf->erf", arrived, expert_in, preferred_element_type=jnp.float32)
    activated = (jax.nn.silu(inner[..., :unit_ff]) * inner[..., unit_ff:]).astype(jnp.bfloat16)
    produced = jnp.einsum(
        "erf,efd->erd", activated, expert_out, preferred_element_type=jnp.float32
    ).astype(jnp.bfloat16)
    returned = lax.all_to_all(produced, "tensor", split_axis=1, concat_axis=0, tiled=True)
    picked = returned.reshape(total_units * CAP, model)[target].reshape(rows, TOPK, parts, model)
    combined = jnp.einsum("tk,tksd->td", gate_weights[0], picked.astype(jnp.float32))
    mixed = (hidden_state.astype(jnp.float32) + combined).astype(jnp.bfloat16)
    return (hidden_state[None], mixed[None])


def solution(mesh):
    in_specs = (
        P("dp", "tensor", None),
        P(),
        P(None, "dp"),
        P("dp", None),
        P("dp", "tensor", None, None),
        P("dp", None),
        P(),
        P("dp", "tensor", None),
        P("dp", "tensor", None),
        P("tensor", None, None),
        P("tensor", None, None),
    )
    out_specs = (P("dp", "tensor", None), P("dp", "tensor", None))
    return jax.shard_map(shards, mesh=mesh, in_specs=in_specs, out_specs=out_specs, check_vma=False)
```

profile of v0, /device:TPU:32, one launch (start us, length us, event | category | flops | bytes accessed | tf_op | source)
XLA Modules:
  0.0 878.6 jit_solution(11526907995774648510)
XLA Ops:
  14.2 9.0 %reduce-window.19 = s32[32,8,128]{2,1,0:T(8,128)S(1)} reduce-window(s32[32,8,128]{2,1,0:T(8,128)S(1)} %fusion.61, s32[]{:T(128)} %constant.24.clone.1), window={size=1x1x128 pad=0_0x0_0x127_0}, to_apply=%region_11.12 | reduce-window | flops 4161536 | bytes 262148 | tf_op jit(solution)/shard_map/reduce-window.2
  24.5 8.1 scatter_custom_fusion
  34.4 54.9 %all-gather.9.cloned.1.call-done = bf16[1,512,2,512]{3,2,0,1:T(2,128)(2,1)} async-done(((bf16[1,8,2,512]{3,2,0,1:T(2,128)(2,1)}), bf16[1,512,2,512]{3,2,0,1:T(2,128)(2,1)}) %all-gather.9.cloned.1.call-update) | async-done | bytes 1048592 | tf_op jit(solution)/shard_map/all_gather | solution.py:114
  89.3 4.2 fusion.70
  93.5 3.5 copy.73
  97.0 3.5 copy.74
  100.5 70.5 %all-gather.5.cloned.1.call-done = bf16[1536,2560]{1,0:T(8,128)(2,1)} async-done(((bf16[1536,640]{1,0:T(8,128)(2,1)}), bf16[1536,2560]{1,0:T(8,128)(2,1)}) %all-gather.5.cloned.1.call-update) | async-done | bytes 7864336 | tf_op jit(solution)/shard_map/all_gather | solution.py:90
  171.1 4.5 convolution_convert_fusion.1
  177.5 1.9 collective-permute-start
  179.9 5.7 collective-permute-done
  186.7 3.9 collective-permute-start.1
  191.5 4.8 bitcast_reduce_fusion
  196.4 5.2 collective-permute-done.1
  205.1 2.1 copy.80
  208.3 3.7 fusion.3
  218.3 10.7 %all-gather.7.cloned.1.call-done = bf16[1536,1536]{1,0:T(8,128)(2,1)} async-done(((bf16[384,1536]{1,0:T(8,128)(2,1)}), bf16[1536,1536]{1,0:T(8,128)(2,1)}) %all-gather.7.cloned.1.call-update) | async-done | bytes 4718608 | tf_op jit(solution)/shard_map/all_gather | solution.py:91
  229.0 3.2 fusion.40
  232.5 9.5 %gather_fusion = bf16[2560,1536]{1,0:T(8,128)(2,1)} fusion(bf16[129,1536]{1,0:T(8,128)(2,1)S(1)} %concatenate.37, s32[3072]{0:T(1024)S(1)} %pad_clamp_fusion), kind=kCustom, calls=%fused_computation | custom fusion | bytes 15738880 | tf_op jit(solution)/shard_map/gather | solution.py:160
  242.0 184.6 %all_to_all.8 = bf16[64,40,1536]{2,1,0:T(8,128)(2,1)S(1)} all-to-all(bf16[64,40,1536]{2,1,0:T(8,128)(2,1)} %bitcast.167), channel_id=1, replica_groups=mesh['dp'=4,'tensor'=64] {'tensor'}, dimensions={0} | all-to-all | bytes 15728640 | tf_op jit(solution)/shard_map/all_to_all | solution.py:161
  426.6 4.3 convolution_bitcast_fusion
  430.8 2.3 fusion
  433.1 86.3 %copy.103 = bf16[1,2560,1536]{2,0,1:T(2,128)(2,1)} copy(bf16[1,2560,1536]{2,1,0:T(8,128)(2,1)S(1)} %fusion) | data formatting | bytes 15728640 | tf_op jit(solution)/shard_map/convert_element_type | solution.py:168
  520.0 51.5 %reduce.2 = bf16[2560,1536]{1,0:T(8,128)(2,1)} reduce(bf16[2560,1,1536]{2,1,0:T(2,128)(2,1)} %bitcast.165, bf16[]{:T(256)} %broadcast.284), dimensions={1}, to_apply=%bitcast.163.reduce_sub_computation | reduce | bytes 15728642
  571.5 17.7 %reshape.394 = bf16[64,2,30720]{2,1,0:T(2,128)(2,1)} reshape(bf16[2560,1536]{1,0:T(8,128)(2,1)} %reduce.2) | data formatting | bytes 15728640
  589.1 7.0 all-to-all-start.1
  596.4 172.5 %all-to-all-done.1 = bf16[64,2,30720]{2,1,0:T(2,128)(2,1)} async-done(((bf16[64,2,30720]{2,1,0:T(2,128)(2,1)}), bf16[64,2,30720]{2,1,0:T(2,128)(2,1)}, u32[]{:S(2)}, u32[]{:S(2)}) %all-to-all-start.1) | async-done | bytes 7864352 | tf_op jit(solution)/shard_map/all_to_all | solution.py:169
  768.8 38.0 %reshape.395 = bf16[2560,1,1536]{2,1,0:T(2,128)(2,1)} reshape(bf16[64,2,30720]{2,1,0:T(2,128)(2,1)} %all-to-all-done.1) | data formatting | bytes 15728640
  806.8 10.8 %copy.102 = bf16[1,2560,1536]{2,1,0:T(8,128)(2,1)} copy(bf16[1,2560,1536]{2,0,1:T(2,128)(2,1)} %bitcast.166) | data formatting | bytes 15728640
  817.6 17.5 %gather_fusion.1 = bf16[2048,1536]{1,0:T(8,128)(2,1)} fusion(bf16[2560,1536]{1,0:T(8,128)(2,1)} %bitcast.164, s32[2048]{0:T(1024)S(1)} %broadcast_clamp_fusion), kind=kCustom, calls=%fused_computation.1 | custom fusion | bytes 12591104 | tf_op jit(solution)/shard_map/gather | solution.py:170
  835.2 14.1 %reshape.358 = f32[128,8,2,1536]{3,2,1,0:T(2,128)} reshape(bf16[2048,1536]{1,0:T(8,128)(2,1)} %gather_fusion.1) | data formatting | bytes 18874368 | tf_op jit(solution)/shard_map/convert_element_type | solution.py:171
  849.3 18.9 %reduce_sum.89 = bf16[128,8,1536]{2,1,0:T(8,128)(2,1)} reduce(f32[128,8,2,1536]{3,2,1,0:T(2,128)} %reshape.358, f32[]{:T(128)} %constant.19.clone.1), dimensions={2}, to_apply=%region_15.16 | reduce | flops 1572864 | bytes 15728644 | tf_op jit(solution)/shard_map/tk,tksd->td/reduce_sum | solution.py:171
  868.2 2.8 fusion.72
  (107 shorter events, 26.8 us)
Async XLA Ops:
  7.2 419.4 %copy-start = (bf16[1,1536,512]{2,1,0:T(8,128)(2,1)S(1)}, bf16[1,1536,512]{2,1,0:T(8,128)(2,1)}, u32[]{:S(2)}) copy-start(bf16[1,1536,512]{2,1,0:T(8,128)(2,1)} %param.20) | copy-start | bytes 4718596
  7.2 82.1 %all-gather.9.cloned.1.call-start = ((), (), s32[]{:S(2)}) async-start(), calls=%async_computation.4 | async-start | bytes 1064960 | tf_op jit(solution)/shard_map/all_gather | solution.py:114
  7.9 163.2 %all-gather.5.cloned.1.call-start = ((), (), s32[]{:S(2)}) async-start(), calls=%async_computation.2 | async-start | bytes 9830400 | tf_op jit(solution)/shard_map/all_gather | solution.py:90
  8.7 162.4 %copy-start.2 = (bf16[1,128,1536]{2,1,0:T(8,128)(2,1)S(1)}, bf16[1,128,1536]{2,1,0:T(8,128)(2,1)}, u32[]{:S(2)}) copy-start(bf16[1,128,1536]{2,1,0:T(8,128)(2,1)} %param.11) | copy-start | bytes 1179652
  8.7 162.4 %copy-start.8 = (f32[1536]{0:T(1024)S(1)}, f32[1536]{0:T(1024)}, u32[]{:S(2)}) copy-start(f32[1536]{0:T(1024)} %param.12) | copy-start | bytes 18436
  8.7 220.3 %all-gather.7.cloned.1.call-start = ((), (), s32[]{:S(2)}) async-start(), calls=%async_computation.3 | async-start | bytes 5898240 | tf_op jit(solution)/shard_map/all_gather | solution.py:91
  24.4 8.2 copy-start.9
  34.2 66.3 %copy-start.7 = (f32[128,64]{0,1:T(8,128)}, f32[128,64]{0,1:T(8,128)S(1)}, u32[]{:S(2)}) copy-start(f32[128,64]{0,1:T(8,128)S(1)} %get-tuple-element.27) | copy-start | bytes 98308
  177.5 8.0 collective-permute-start
  186.7 14.9 %collective-permute-start.1 = (bf16[2,128,2,512]{3,1,2,0:T(8,128)(2,1)S(1)}, bf16[2,128,2,512]{3,1,2,0:T(8,128)(2,1)S(1)}, u32[]{:S(2)}, u32[]{:S(2)}) collective-permute-start(bf16[2,128,2,512]{3,1,2,0:T(8,128)(2,1)S(1)} %pad_maximum_fusion.1), channel_id=1, source_target_pairs={{0,2},{1,3},{2,4},{3,5},{4,6},{5,7},{6,8},{7,9},{8,10},{9,11},{10,... | collective-permute-start | bytes 1572872 | tf_op jit(solution)/shard_map/ppermute | solution.py:22
  191.5 15.7 %copy-start.4 = (pred[128,512]{0,1:T(8,128)(4,1)S(1)}, pred[128,512]{0,1:T(8,128)(4,1)}, u32[]{:S(2)}) copy-start(pred[128,512]{0,1:T(8,128)(4,1)} %compare_and_fusion) | copy-start | bytes 196612
  208.3 5.3 copy-start.6
  213.5 2.4 slice-start
  213.5 2.4 copy-start.5
  213.5 3.1 slice-start.1
  216.6 15.7 %copy-start.11 = (f32[1536]{0:T(1024)S(1)}, f32[1536]{0:T(1024)}, u32[]{:S(2)}) copy-start(f32[1536]{0:T(1024)} %param.17) | copy-start | bytes 18436
  232.2 638.8 %copy-start.3 = (bf16[128,1536]{1,0:T(8,128)(2,1)}, bf16[128,1536]{1,0:T(8,128)(2,1)S(1)}, u32[]{:S(2)}) copy-start(bf16[128,1536]{1,0:T(8,128)(2,1)S(1)} %get-tuple-element.26) | copy-start | bytes 1179652
  426.5 4.3 copy-start.13
  589.1 7.1 copy-start.12
  589.1 7.2 copy-start.10
  589.1 179.7 %all-to-all-start.1 = ((bf16[64,2,30720]{2,1,0:T(2,128)(2,1)}), bf16[64,2,30720]{2,1,0:T(2,128)(2,1)}, u32[]{:S(2)}, u32[]{:S(2)}) async-start(bf16[64,2,30720]{2,1,0:T(2,128)(2,1)} %reshape.394), calls=%async_computation.1 | async-start | bytes 15728640 | tf_op jit(solution)/shard_map/all_to_all | solution.py:169
  849.3 22.6 %copy-start.1 = (bf16[1,1536,512]{2,1,0:T(8,128)(2,1)S(1)}, bf16[1,1536,512]{2,1,0:T(8,128)(2,1)}, u32[]{:S(2)}) copy-start(bf16[1,1536,512]{2,1,0:T(8,128)(2,1)} %param.20) | copy-start | bytes 4718596
Sparse Core Ops, SparseCore 0:
  10.8 78.4 all-gather.8
  91.1 79.9 all-gather.4
  172.9 56.0 all-gather.6
where the time goes:
time: 890 us; the launch traced here: 879 us
  waiting for transfers between devices  322 us (36%)
  local copies, waits for them, and re-layouts  222 us (25%)
  blocking collectives  185 us (21%)
  other arithmetic  96.3 us (11%)
  matrix products  26.4 us (3%)
  between operations  14.5 us (2%)
  starting transfers between devices  13 us (1%)
    all_to_all x1, blocking collectives, shards(): lax.all_to_all(outgoing.reshape(total_units, CAP, model), 'tensor', split...  185 us
    all_to_all x1, waiting for transfers between devices, shards(): lax.all_to_all(produced, 'tensor', split_axis=1, concat_axis=0, tiled=True)  172 us
    convert_element_type x1, local copies, waits for them, and re-layouts, shards(): produced = jnp.einsum('erf,efd->erd', activated, expert_out, preferred_el...  86.3 us
    all_gather x1, waiting for transfers between devices, shards(): lax.all_gather(qkv_weight, 'dp', axis=1, tiled=True)  70.5 us
    unnamed x37, local copies, waits for them, and re-layouts  69.2 us
    all_gather x1, waiting for transfers between devices, shards(): piece = lax.all_gather(prefix_cache[0], 'tensor', axis=0, tiled=True)  54.9 us
    unnamed x2, other arithmetic  51.5 us
    reduce_sum x1, other arithmetic, shards(): jnp.einsum('tk,tksd->td', gate_weights[0], picked.astype(jnp.float32))  18.9 us
  transfers between devices with their start and end apart: 6, of which 6 were waited for; matrix products, arithmetic and copies ran while one was open for 7% of the time, Pallas kernels for 0%

commit v1 on v0

--- a/solution.py
+++ b/solution.py
@@ -10,6 +10,7 @@
 TOPK = 8
 SHIFTS = 2
 CAP = 40
+TENSOR = ("chip", "core")
 
 
 EPS = 1e-06
@@ -81,7 +82,7 @@
     kv_cols = KV_HEADS * HEAD_DIM
     ratio = HEADS // KV_HEADS
     scale = 1.0 / HEAD_DIM**0.5
-    lanes = lax.axis_size("tensor")
+    lanes = lax.axis_size(TENSOR)
     prefix_len = prefix_cache.shape[1] * lanes
     own_lengths = lengths[0]
     inputs = tokens[0]
@@ -91,7 +92,7 @@
         lax.all_gather(out_weight, "dp", axis=0, tiled=True),
     )
     qkv = jnp.dot(normed, full_qkv, preferred_element_type=jnp.float32).astype(jnp.bfloat16)
-    lane = lax.axis_index("tensor")
+    lane = lax.axis_index(TENSOR)
     q_index = lane * rows + jnp.arange(rows, dtype=jnp.int32)
     q_segment, offset = request_info(q_index, own_lengths)
     positions = prefix_len + offset
@@ -111,7 +112,7 @@
         jnp.zeros((rows, KV_HEADS, ratio), jnp.float32),
         jnp.zeros((rows, KV_HEADS, ratio, HEAD_DIM), jnp.float32),
     )
-    piece = lax.all_gather(prefix_cache[0], "tensor", axis=0, tiled=True)
+    piece = lax.all_gather(prefix_cache[0], TENSOR, axis=0, tiled=True)
     count = piece.shape[0]
     cached_keys = piece[:, 0].reshape(count, KV_HEADS, HEAD_DIM)
     cached_values = piece[:, 1].reshape(count, KV_HEADS, HEAD_DIM)
@@ -121,7 +122,7 @@
     carry = merge_block(start_carry, scores, cached_values, None)
     window = local_pairs[None]
     for bit in range(SHIFTS):
-        earlier = from_behind(window, "tensor", 2**bit)
+        earlier = from_behind(window, TENSOR, 2**bit)
         window = jnp.concatenate([window, earlier], axis=0)
     depth = window.shape[0]
     k_index = (
@@ -145,47 +146,48 @@
     projected = jnp.dot(attended, full_out, preferred_element_type=jnp.float32)
     hidden_state = (inputs.astype(jnp.float32) + projected).astype(jnp.bfloat16)
     moe_input = rms_norm(hidden_state, ffn_gain)
-    total_units = expert_in.shape[0] * lanes
-    parts = total_units // EXPERTS
+    chips = lax.axis_size("chip")
     unit_ff = expert_in.shape[2] // 2
     flat_ids = expert_ids[0].reshape(-1)
     onehot = (flat_ids[:, None] == jnp.arange(EXPERTS, dtype=jnp.int32)[None, :]).astype(jnp.int32)
     earlier_count = jnp.cumsum(onehot, axis=0, dtype=jnp.int32) - onehot
     slots = jnp.sum(earlier_count * onehot, axis=1, dtype=jnp.int32)
-    unit_ids = flat_ids[:, None] * parts + jnp.arange(parts, dtype=jnp.int32)[None, :]
-    target = (unit_ids * CAP + slots[:, None]).reshape(-1)
-    row_of = jnp.repeat(jnp.arange(rows, dtype=jnp.int32), TOPK * parts)
-    source = jnp.full((total_units * CAP,), rows, jnp.int32).at[target].set(row_of)
+    target = flat_ids * CAP + slots
+    row_of = jnp.repeat(jnp.arange(rows, dtype=jnp.int32), TOPK)
+    source = jnp.full((chips * CAP,), rows, jnp.int32).at[target].set(row_of)
     padded_input = jnp.concatenate([moe_input, jnp.zeros((1, model), jnp.bfloat16)], axis=0)
-    outgoing = padded_input[source]
-    arrived = lax.all_to_all(
-        outgoing.reshape(total_units, CAP, model), "tensor", split_axis=0, concat_axis=1, tiled=True
-    )
-    inner = jnp.einsum("erd,edf->erf", arrived, expert_in, preferred_element_type=jnp.float32)
-    activated = (jax.nn.silu(inner[..., :unit_ff]) * inner[..., unit_ff:]).astype(jnp.bfloat16)
-    produced = jnp.einsum(
-        "erf,efd->erd", activated, expert_out, preferred_element_type=jnp.float32
-    ).astype(jnp.bfloat16)
-    returned = lax.all_to_all(produced, "tensor", split_axis=1, concat_axis=0, tiled=True)
-    picked = returned.reshape(total_units * CAP, model)[target].reshape(rows, TOPK, parts, model)
-    combined = jnp.einsum("tk,tksd->td", gate_weights[0], picked.astype(jnp.float32))
+    outgoing = padded_input[source].reshape(chips, CAP, model)
+    arrived = lax.all_to_all(outgoing, "chip", 0, 0, tiled=True)
+    sibling = lax.ppermute(arrived, "core", [(0, 1), (1, 0)])
+    unit_rows = jnp.concatenate([arrived, sibling], axis=0).reshape(2 * chips * CAP, model)
+    inner = jnp.dot(unit_rows, expert_in[0], preferred_element_type=jnp.float32)
+    activated = (jax.nn.silu(inner[:, :unit_ff]) * inner[:, unit_ff:]).astype(jnp.bfloat16)
+    produced = jnp.dot(activated, expert_out[0], preferred_element_type=jnp.float32).astype(jnp.bfloat16)
+    produced = produced.reshape(2, chips, CAP, model)
+    partner = lax.ppermute(produced[1], "core", [(0, 1), (1, 0)])
+    summed = (produced[0].astype(jnp.float32) + partner.astype(jnp.float32)).astype(jnp.bfloat16)
+    returned = lax.all_to_all(summed, "chip", 0, 0, tiled=True)
+    picked = returned.reshape(chips * CAP, model)[target].reshape(rows, TOPK, model)
+    combined = jnp.einsum("tk,tkd->td", gate_weights[0], picked.astype(jnp.float32))
     mixed = (hidden_state.astype(jnp.float32) + combined).astype(jnp.bfloat16)
     return (hidden_state[None], mixed[None])
 
 
 def solution(mesh):
+    groups, lanes = mesh.devices.shape
+    chip_mesh = jax.sharding.Mesh(mesh.devices.reshape(groups, lanes // 2, 2), ("dp", "chip", "core"))
     in_specs = (
-        P("dp", "tensor", None),
+        P("dp", TENSOR, None),
         P(),
         P(None, "dp"),
         P("dp", None),
-        P("dp", "tensor", None, None),
+        P("dp", TENSOR, None, None),
         P("dp", None),
         P(),
-        P("dp", "tensor", None),
-        P("dp", "tensor", None),
-        P("tensor", None, None),
-        P("tensor", None, None),
+        P("dp", TENSOR, None),
+        P("dp", TENSOR, None),
+        P(TENSOR, None, None),
+        P(TENSOR, None, None),
     )
-    out_specs = (P("dp", "tensor", None), P("dp", "tensor", None))
-    return jax.shard_map(shards, mesh=mesh, in_specs=in_specs, out_specs=out_specs, check_vma=False)
+    out_specs = (P("dp", TENSOR, None), P("dp", TENSOR, None))
+    return jax.shard_map(shards, mesh=chip_mesh, in_specs=in_specs, out_specs=out_specs, check_vma=False)

time: 890 us -> 491 us (0.55); the launches traced: 879 us -> 489 us
  local copies, waits for them, and re-layouts: 222 us -> 42 us
  blocking collectives: 185 us -> 100 us
  waiting for transfers between devices: 322 us -> 257 us
  other arithmetic: 96.3 us -> 36.3 us
    convert_element_type x2 -> x0, local copies, waits for them, and re-layouts: 100 us -> none  [the longest x1 86.3 us: shards(): produced = jnp.einsum('erf,efd->erd', activated, expert_out, preferred_el...]
    all_to_all x1, blocking collectives: 185 us -> 100 us  [shards(): arrived = lax.all_to_all(outgoing, 'chip', 0, 0, tiled=True)]
    all_to_all x1, waiting for transfers between devices: 172 us -> 90.1 us  [shards(): returned = lax.all_to_all(summed, 'chip', 0, 0, tiled=True)]
    unnamed x37 -> x31, local copies, waits for them, and re-layouts: 69.2 us -> 4.18 us
    unnamed x2 -> x1, other arithmetic: 51.5 us -> 0.01 us
    reduce_sum x1 -> x0, other arithmetic: 18.9 us -> none  [shards(): jnp.einsum('tk,tksd->td', gate_weights[0], picked.astype(jnp.float32))]
    ppermute x0 -> x2, waiting for transfers between devices: none -> 13.6 us  [the longest x1 6.91 us: shards(): sibling = lax.ppermute(arrived, 'core', [(0, 1), (1, 0)])]
    gather x2, local copies, waits for them, and re-layouts: 27 us -> 15.4 us  [the longest x1 10 us: shards(): returned.reshape(chips * CAP, model)[target].reshape(rows, TOPK, model)]
  transfers between devices with their start and end apart: 6 -> 8, of which waited for: 6 -> 8; matrix products, arithmetic and copies ran while one was open for 7% -> 13% of each run, Pallas kernels for 0% -> 0%
where the time goes in v1:
time: 491 us; the launch traced here: 489 us
  waiting for transfers between devices  257 us (52%)
  blocking collectives  100 us (20%)
  local copies, waits for them, and re-layouts  42 us (9%)
  other arithmetic  36.3 us (7%)
  matrix products  28.7 us (6%)
  between operations  14.2 us (3%)
  starting transfers between devices  11 us (2%)
    all_to_all x1, blocking collectives, shards(): arrived = lax.all_to_all(outgoing, 'chip', 0, 0, tiled=True)  100 us
    all_to_all x1, waiting for transfers between devices, shards(): returned = lax.all_to_all(summed, 'chip', 0, 0, tiled=True)  90.1 us
    all_gather x1, waiting for transfers between devices, shards(): lax.all_gather(qkv_weight, 'dp', axis=1, tiled=True)  70.6 us
    all_gather x1, waiting for transfers between devices, shards(): piece = lax.all_gather(prefix_cache[0], TENSOR, axis=0, tiled=True)  58.5 us
    ppermute x2, waiting for transfers between devices, from_behind(): lax.ppermute(value, axis, [(source, source + steps) for source in range(f...  11.2 us
    all_gather x1, waiting for transfers between devices, shards(): lax.all_gather(out_weight, 'dp', axis=0, tiled=True)  10.7 us
    another operation x6, other arithmetic  10.2 us
    gather x1, local copies, waits for them, and re-layouts, shards(): returned.reshape(chips * CAP, model)[target].reshape(rows, TOPK, model)  10 us
  transfers between devices with their start and end apart: 8, of which 8 were waited for; matrix products, arithmetic and copies ran while one was open for 13% of the time, Pallas kernels for 0%

profile of v1, /device:TPU:32, one launch (start us, length us, event | category | flops | bytes accessed | tf_op | source)
XLA Modules:
  0.0 489.3 jit_solution(2247679255793934085)
XLA Ops:
  14.9 9.0 %reduce-window.19 = s32[32,8,128]{2,1,0:T(8,128)S(1)} reduce-window(s32[32,8,128]{2,1,0:T(8,128)S(1)} %fusion.64, s32[]{:T(128)} %constant.27.clone.1), window={size=1x1x128 pad=0_0x0_0x127_0}, to_apply=%region_11.12 | reduce-window | flops 4161536 | bytes 262148 | tf_op jit(solution)/shard_map/reduce-window.2
  24.7 4.3 scatter_custom_fusion
  30.9 58.5 %all-gather.9.cloned.1.call-done = bf16[1,512,2,512]{3,2,0,1:T(2,128)(2,1)} async-done(((bf16[1,8,2,512]{3,2,0,1:T(2,128)(2,1)}), bf16[1,512,2,512]{3,2,0,1:T(2,128)(2,1)}) %all-gather.9.cloned.1.call-update) | async-done | bytes 1048592 | tf_op jit(solution)/shard_map/all_gather | solution.py:115
  89.3 4.3 fusion.74
  93.6 3.5 copy.57
  97.1 3.5 copy.58
  100.6 70.6 %all-gather.5.cloned.1.call-done = bf16[1536,2560]{1,0:T(8,128)(2,1)} async-done(((bf16[1536,640]{1,0:T(8,128)(2,1)}), bf16[1536,2560]{1,0:T(8,128)(2,1)}) %all-gather.5.cloned.1.call-update) | async-done | bytes 7864336 | tf_op jit(solution)/shard_map/all_gather | solution.py:91
  171.1 4.5 convolution_convert_fusion.1
  177.6 1.9 collective-permute-start
  179.9 5.7 %collective-permute-done = bf16[1,128,2,512]{3,1,2,0:T(8,128)(2,1)} collective-permute-done((bf16[1,128,2,512]{3,1,2,0:T(8,128)(2,1)}, bf16[1,128,2,512]{3,1,2,0:T(8,128)(2,1)}, u32[]{:S(2)}, u32[]{:S(2)}) %collective-permute-start) | collective-permute-done | bytes 262176 | tf_op jit(solution)/shard_map/ppermute | solution.py:23
  186.7 3.6 collective-permute-start.1
  191.3 4.8 bitcast_reduce_fusion
  196.1 5.5 %collective-permute-done.1 = bf16[2,128,2,512]{3,1,2,0:T(8,128)(2,1)S(1)} collective-permute-done((bf16[2,128,2,512]{3,1,2,0:T(8,128)(2,1)S(1)}, bf16[2,128,2,512]{3,1,2,0:T(8,128)(2,1)S(1)}, u32[]{:S(2)}, u32[]{:S(2)}) %collective-permute-start.1) | collective-permute-done | bytes 524320 | tf_op jit(solution)/shard_map/ppermute | solution.py:23
  205.2 2.1 copy.64
  208.4 3.7 fusion.3
  213.6 1.7 fusion.22
  216.7 1.7 fusion.40
  218.4 10.7 %all-gather.7.cloned.1.call-done = bf16[1536,1536]{1,0:T(8,128)(2,1)} async-done(((bf16[384,1536]{1,0:T(8,128)(2,1)}), bf16[1536,1536]{1,0:T(8,128)(2,1)}) %all-gather.7.cloned.1.call-update) | async-done | bytes 4718608 | tf_op jit(solution)/shard_map/all_gather | solution.py:92
  229.0 3.2 fusion.43
  232.5 5.4 %gather_fusion = bf16[1280,1536]{1,0:T(8,128)(2,1)} fusion(bf16[129,1536]{1,0:T(8,128)(2,1)S(1)} %concatenate.40, s32[2048]{0:T(1024)S(1)} %pad_clamp_fusion), kind=kCustom, calls=%fused_computation | custom fusion | bytes 7869440 | tf_op jit(solution)/shard_map/gather | solution.py:159
  237.9 100.5 %all_to_all.10 = bf16[32,40,1536]{2,1,0:T(8,128)(2,1)S(1)} all-to-all(bf16[32,40,1536]{2,1,0:T(8,128)(2,1)} %bitcast.159), channel_id=1, replica_groups=mesh['dp'=4,'chip'=32,'core'=2] {'chip'}, dimensions={0} | all-to-all | bytes 7864320 | tf_op jit(solution)/shard_map/all_to_all | solution.py:160
  338.4 2.0 copy-done.2
  340.4 6.9 %collective-permute-done.2 = bf16[32,40,1536]{2,1,0:T(8,128)(2,1)} collective-permute-done((bf16[32,40,1536]{2,1,0:T(8,128)(2,1)S(1)}, bf16[32,40,1536]{2,1,0:T(8,128)(2,1)}, u32[]{:S(2)}, u32[]{:S(2)}) %collective-permute-start.2) | collective-permute-done | bytes 3932192 | tf_op jit(solution)/shard_map/ppermute | solution.py:161
  347.3 7.1 %pad_maximum_fusion = bf16[64,40,1536]{2,1,0:T(8,128)(2,1)} fusion(bf16[32,40,1536]{2,1,0:T(8,128)(2,1)} %collective-permute-done.2, bf16[32,40,1536]{2,1,0:T(8,128)(2,1)} %copy-done.2), kind=kLoop, calls=%fused_computation.4 | loop fusion | flops 3932160 | bytes 15728640 | tf_op jit(solution)/shard_map/concatenate | solution.py:162
  354.3 6.6 %fusion.18 = f32[2560,512]{1,0:T(8,128)S(1)} fusion(bf16[2560,1536]{1,0:T(8,128)(2,1)} %bitcast.161, bf16[1,1536,512]{2,1,0:T(8,128)(2,1)S(1)} %copy-done), kind=kOutput, calls=%fused_computation.29 | convolution fusion | flops 4026531840 | bytes 14680064 | tf_op jit(solution)/shard_map/dot_general | solution.py:163
  361.0 2.3 convolution_convert_fusion
  364.1 6.6 %collective-permute-done.3 = bf16[32,40,1536]{2,1,0:T(8,128)(2,1)S(1)} collective-permute-done((bf16[32,40,1536]{2,1,0:T(8,128)(2,1)S(1)}, bf16[32,40,1536]{2,1,0:T(8,128)(2,1)S(1)}, u32[]{:S(2)}, u32[]{:S(2)}) %collective-permute-start.3) | collective-permute-done | bytes 3932192 | tf_op jit(solution)/shard_map/ppermute | solution.py:167
  370.7 3.0 fusion
  373.7 5.1 %all-to-all-start.1 = ((bf16[32,40,1536]{2,1,0:T(8,128)(2,1)}), bf16[32,40,1536]{2,1,0:T(8,128)(2,1)}, u32[]{:S(2)}, u32[]{:S(2)}) async-start(bf16[32,40,1536]{2,1,0:T(8,128)(2,1)} %fusion), calls=%async_computation.1 | async-start | bytes 7864320 | tf_op jit(solution)/shard_map/all_to_all | solution.py:169
  379.0 90.1 %all-to-all-done.1 = bf16[32,40,1536]{2,1,0:T(8,128)(2,1)} async-done(((bf16[32,40,1536]{2,1,0:T(8,128)(2,1)}), bf16[32,40,1536]{2,1,0:T(8,128)(2,1)}, u32[]{:S(2)}, u32[]{:S(2)}) %all-to-all-start.1) | async-done | bytes 3932192 | tf_op jit(solution)/shard_map/all_to_all | solution.py:169
  469.1 10.0 %gather_fusion.1 = bf16[1024,1536]{1,0:T(8,128)(2,1)} fusion(bf16[1280,1536]{1,0:T(8,128)(2,1)} %bitcast.47, s32[1024]{0:T(1024)S(1)} %broadcast_clamp_fusion), kind=kCustom, calls=%fused_computation.1 | custom fusion | bytes 6295552 | tf_op jit(solution)/shard_map/gather | solution.py:170
  479.1 2.8 fusion.9
  (104 shorter events, 24.0 us)
Async XLA Ops:
  7.2 347.2 %copy-start = (bf16[1,1536,512]{2,1,0:T(8,128)(2,1)S(1)}, bf16[1,1536,512]{2,1,0:T(8,128)(2,1)}, u32[]{:S(2)}) copy-start(bf16[1,1536,512]{2,1,0:T(8,128)(2,1)} %param.20) | copy-start | bytes 4718596
  7.2 82.2 %all-gather.9.cloned.1.call-start = ((), (), s32[]{:S(2)}) async-start(), calls=%async_computation.4 | async-start | bytes 1064960 | tf_op jit(solution)/shard_map/all_gather | solution.py:115
  7.9 163.2 %all-gather.5.cloned.1.call-start = ((), (), s32[]{:S(2)}) async-start(), calls=%async_computation.2 | async-start | bytes 9830400 | tf_op jit(solution)/shard_map/all_gather | solution.py:91
  8.7 162.5 %copy-start.3 = (bf16[1,128,1536]{2,1,0:T(8,128)(2,1)S(1)}, bf16[1,128,1536]{2,1,0:T(8,128)(2,1)}, u32[]{:S(2)}) copy-start(bf16[1,128,1536]{2,1,0:T(8,128)(2,1)} %param.11) | copy-start | bytes 1179652
  8.7 162.5 %copy-start.9 = (f32[1536]{0:T(1024)S(1)}, f32[1536]{0:T(1024)}, u32[]{:S(2)}) copy-start(f32[1536]{0:T(1024)} %param.12) | copy-start | bytes 18436
  8.7 220.3 %all-gather.7.cloned.1.call-start = ((), (), s32[]{:S(2)}) async-start(), calls=%async_computation.3 | async-start | bytes 5898240 | tf_op jit(solution)/shard_map/all_gather | solution.py:92
  30.7 69.9 %copy-start.8 = (f32[128,64]{0,1:T(8,128)}, f32[128,64]{0,1:T(8,128)S(1)}, u32[]{:S(2)}) copy-start(f32[128,64]{0,1:T(8,128)S(1)} %get-tuple-element.29) | copy-start | bytes 98308
  177.6 8.0 %collective-permute-start = (bf16[1,128,2,512]{3,1,2,0:T(8,128)(2,1)}, bf16[1,128,2,512]{3,1,2,0:T(8,128)(2,1)}, u32[]{:S(2)}, u32[]{:S(2)}) collective-permute-start(bf16[1,128,2,512]{3,1,2,0:T(8,128)(2,1)} %maximum_bitcast_fusion), channel_id=1, source_target_pairs={{0,1},{1,2},{2,3},{3,4},{4,5},{5,6},{6,7},{7,8},{8,9},{9,10},{10,1... | collective-permute-start | bytes 786440 | tf_op jit(solution)/shard_map/ppermute | solution.py:23
  186.7 14.9 %collective-permute-start.1 = (bf16[2,128,2,512]{3,1,2,0:T(8,128)(2,1)S(1)}, bf16[2,128,2,512]{3,1,2,0:T(8,128)(2,1)S(1)}, u32[]{:S(2)}, u32[]{:S(2)}) collective-permute-start(bf16[2,128,2,512]{3,1,2,0:T(8,128)(2,1)S(1)} %pad_maximum_fusion.2), channel_id=1, source_target_pairs={{0,2},{1,3},{2,4},{3,5},{4,6},{5,7},{6,8},{7,9},{8,10},{9,11},{10,... | collective-permute-start | bytes 1572872 | tf_op jit(solution)/shard_map/ppermute | solution.py:23
  191.3 16.0 %copy-start.5 = (pred[128,512]{0,1:T(8,128)(4,1)S(1)}, pred[128,512]{0,1:T(8,128)(4,1)}, u32[]{:S(2)}) copy-start(pred[128,512]{0,1:T(8,128)(4,1)} %compare_and_fusion) | copy-start | bytes 196612
  208.3 5.2 %copy-start.7 = (bf16[512,1,512]{0,2,1:T(8,128)(2,1)S(1)}, bf16[512,1,512]{0,2,1:T(8,128)(2,1)}, u32[]{:S(2)}) copy-start(bf16[512,1,512]{0,2,1:T(8,128)(2,1)} %copy.64) | copy-start | bytes 1572868
  213.5 2.4 slice-start
  213.5 2.4 copy-start.6
  213.6 3.1 slice-start.1
  216.7 15.6 %copy-start.10 = (f32[1536]{0:T(1024)S(1)}, f32[1536]{0:T(1024)}, u32[]{:S(2)}) copy-start(f32[1536]{0:T(1024)} %param.17) | copy-start | bytes 18436
  232.3 249.7 %copy-start.4 = (bf16[128,1536]{1,0:T(8,128)(2,1)}, bf16[128,1536]{1,0:T(8,128)(2,1)S(1)}, u32[]{:S(2)}) copy-start(bf16[128,1536]{1,0:T(8,128)(2,1)S(1)} %get-tuple-element.28) | copy-start | bytes 1179652
  338.4 2.0 copy-start.2
  340.4 6.9 %collective-permute-start.2 = (bf16[32,40,1536]{2,1,0:T(8,128)(2,1)S(1)}, bf16[32,40,1536]{2,1,0:T(8,128)(2,1)}, u32[]{:S(2)}, u32[]{:S(2)}) collective-permute-start(bf16[32,40,1536]{2,1,0:T(8,128)(2,1)S(1)} %all_to_all.10), channel_id=1, source_target_pairs={{0,1},{1,0},{2,3},{3,2},{4,5},{5,4},{6,7},{7,6},{8,9},{9,8},{10,11... | collective-permute-start | bytes 11796488 | tf_op jit(solution)/shard_map/ppermute | solution.py:161
  354.3 6.6 %copy-start.12 = (bf16[1,256,1536]{2,1,0:T(8,128)(2,1)S(1)}, bf16[1,256,1536]{2,1,0:T(8,128)(2,1)}, u32[]{:S(2)}) copy-start(bf16[1,256,1536]{2,1,0:T(8,128)(2,1)} %param.21) | copy-start | bytes 2359300
  363.8 6.9 %collective-permute-start.3 = (bf16[32,40,1536]{2,1,0:T(8,128)(2,1)S(1)}, bf16[32,40,1536]{2,1,0:T(8,128)(2,1)S(1)}, u32[]{:S(2)}, u32[]{:S(2)}) collective-permute-start(bf16[32,40,1536]{2,1,0:T(8,128)(2,1)S(1)} %bitcast.166), channel_id=1, source_target_pairs={{0,1},{1,0},{2,3},{3,2},{4,5},{5,4},{6,7},{7,6},{8,9},{9,8},{10,11... | collective-permute-start | bytes 11796488 | tf_op jit(solution)/shard_map/ppermute | solution.py:167
  373.7 5.1 %copy-start.11 = (f32[1,128,8]{1,2,0:T(8,128)S(1)}, f32[1,128,8]{1,2,0:T(8,128)}, u32[]{:S(2)}) copy-start(f32[1,128,8]{1,2,0:T(8,128)} %param.19) | copy-start | bytes 12292
  373.7 95.4 %all-to-all-start.1 = ((bf16[32,40,1536]{2,1,0:T(8,128)(2,1)}), bf16[32,40,1536]{2,1,0:T(8,128)(2,1)}, u32[]{:S(2)}, u32[]{:S(2)}) async-start(bf16[32,40,1536]{2,1,0:T(8,128)(2,1)} %fusion), calls=%async_computation.1 | async-start | bytes 7864320 | tf_op jit(solution)/shard_map/all_to_all | solution.py:169
  469.1 13.7 %copy-start.1 = (bf16[1,1536,512]{2,1,0:T(8,128)(2,1)S(1)}, bf16[1,1536,512]{2,1,0:T(8,128)(2,1)}, u32[]{:S(2)}) copy-start(bf16[1,1536,512]{2,1,0:T(8,128)(2,1)} %param.20) | copy-start | bytes 4718596
Sparse Core Ops, SparseCore 0:
  10.8 78.5 all-gather.8
  91.2 79.9 all-gather.4
  173.0 56.0 all-gather.6

commit v2 on v1

--- a/solution.py
+++ b/solution.py
@@ -87,11 +87,13 @@
     own_lengths = lengths[0]
     inputs = tokens[0]
     normed = rms_norm(inputs, attn_gain)
-    full_qkv, full_out = (
-        lax.all_gather(qkv_weight, "dp", axis=1, tiled=True),
-        lax.all_gather(out_weight, "dp", axis=0, tiled=True),
-    )
-    qkv = jnp.dot(normed, full_qkv, preferred_element_type=jnp.float32).astype(jnp.bfloat16)
+    groups = lax.axis_size("dp")
+    full_out = lax.all_gather(out_weight, "dp", axis=0, tiled=True)
+    spread = jnp.broadcast_to(normed[None], (groups, rows, model))
+    group_rows = lax.all_to_all(spread, "dp", 0, 0, tiled=True).reshape(groups * rows, model)
+    qkv_part = jnp.dot(group_rows, qkv_weight, preferred_element_type=jnp.float32).astype(jnp.bfloat16)
+    qkv_back = lax.all_to_all(qkv_part.reshape(groups, rows, -1), "dp", 0, 0, tiled=True)
+    qkv = jnp.transpose(qkv_back, (1, 0, 2)).reshape(rows, -1)
     lane = lax.axis_index(TENSOR)
     q_index = lane * rows + jnp.arange(rows, dtype=jnp.int32)
     q_segment, offset = request_info(q_index, own_lengths)
@@ -112,14 +114,6 @@
         jnp.zeros((rows, KV_HEADS, ratio), jnp.float32),
         jnp.zeros((rows, KV_HEADS, ratio, HEAD_DIM), jnp.float32),
     )
-    piece = lax.all_gather(prefix_cache[0], TENSOR, axis=0, tiled=True)
-    count = piece.shape[0]
-    cached_keys = piece[:, 0].reshape(count, KV_HEADS, HEAD_DIM)
-    cached_values = piece[:, 1].reshape(count, KV_HEADS, HEAD_DIM)
-    scores = (
-        jnp.einsum("tgrd,ngd->tgrn", query, cached_keys, preferred_element_type=jnp.float32) * scale
-    )
-    carry = merge_block(start_carry, scores, cached_values, None)
     window = local_pairs[None]
     for bit in range(SHIFTS):
         earlier = from_behind(window, TENSOR, 2**bit)
@@ -141,7 +135,15 @@
     scores = (
         jnp.einsum("tgrd,ngd->tgrn", query, suffix_keys, preferred_element_type=jnp.float32) * scale
     )
-    best, total, acc = merge_block(carry, scores, suffix_values, visible[:, None, None, :])
+    carry = merge_block(start_carry, scores, suffix_values, visible[:, None, None, :])
+    piece = lax.all_gather(prefix_cache[0], TENSOR, axis=0, tiled=True)
+    count = piece.shape[0]
+    cached_keys = piece[:, 0].reshape(count, KV_HEADS, HEAD_DIM)
+    cached_values = piece[:, 1].reshape(count, KV_HEADS, HEAD_DIM)
+    scores = (
+        jnp.einsum("tgrd,ngd->tgrn", query, cached_keys, preferred_element_type=jnp.float32) * scale
+    )
+    best, total, acc = merge_block(carry, scores, cached_values, None)
     attended = (acc / total[..., None]).astype(jnp.bfloat16).reshape(rows, head_cols)
     projected = jnp.dot(attended, full_out, preferred_element_type=jnp.float32)
     hidden_state = (inputs.astype(jnp.float32) + projected).astype(jnp.bfloat16)

time: 491 us -> 408 us (0.83)
  waiting for transfers between devices: 257 us -> 145 us
  other arithmetic: 36.3 us -> 52.9 us
  starting transfers between devices: 11 us -> 20.6 us
  local copies, waits for them, and re-layouts: 42 us -> 47 us
    all_gather x1, waiting for transfers between devices: 58.5 us -> 0.02 us  [shards(): piece = lax.all_gather(prefix_cache[0], TENSOR, axis=0, tiled=True)]
    all_gather x2 -> x1, waiting for transfers between devices: 81.2 us -> 25.9 us  [shards(): full_out = lax.all_gather(out_weight, 'dp', axis=0, tiled=True)]
    another operation x6, other arithmetic: 10.2 us -> 20.2 us
    all_to_all x0 -> x2, starting transfers between devices: none -> 9.26 us  [the longest x1 4.8 us: shards(): lax.all_to_all(qkv_part.reshape(groups, rows, -1), 'dp', 0, 0, tiled=True)]
    all_to_all x0 -> x2, waiting for transfers between devices: none -> 7.44 us  [the longest x1 7.44 us: shards(): lax.all_to_all(qkv_part.reshape(groups, rows, -1), 'dp', 0, 0, tiled=True)]
  transfers between devices with their start and end apart: 8 -> 9, of which waited for: 8 -> 7; matrix products, arithmetic and copies ran while one was open for 13% -> 20% of each run, Pallas kernels for 0% -> 0%
where the time goes in v2:
time: 408 us; the launch traced here: 406 us
  waiting for transfers between devices  145 us (36%)
  blocking collectives  100 us (25%)
  other arithmetic  52.9 us (13%)
  local copies, waits for them, and re-layouts  47 us (12%)
  matrix products  25.3 us (6%)
  starting transfers between devices  20.6 us (5%)
  between operations  14.5 us (4%)
    all_to_all x1, blocking collectives, shards(): arrived = lax.all_to_all(outgoing, 'chip', 0, 0, tiled=True)  100 us
    all_to_all x1, waiting for transfers between devices, shards(): returned = lax.all_to_all(summed, 'chip', 0, 0, tiled=True)  90.3 us
    all_gather x1, waiting for transfers between devices, shards(): full_out = lax.all_gather(out_weight, 'dp', axis=0, tiled=True)  25.9 us
    another operation x6, other arithmetic  20.2 us
    gather x1, local copies, waits for them, and re-layouts, shards(): returned.reshape(chips * CAP, model)[target].reshape(rows, TOPK, model)  10 us
  transfers between devices with their start and end apart: 9, of which 7 were waited for; matrix products, arithmetic and copies ran while one was open for 20% of the time, Pallas kernels for 0%

profile of v2, /device:TPU:32, one launch (start us, length us, event | category | flops | bytes accessed | tf_op | source)
XLA Modules:
  0.0 405.7 jit_solution(2051394180246428151)
XLA Ops:
  11.6 4.5 %all-to-all-start = ((bf16[4,128,1536]{2,1,0:T(8,128)(2,1)}), bf16[4,128,1536]{2,1,0:T(8,128)(2,1)S(1)}, u32[]{:S(2)}, u32[]{:S(2)}) async-start(bf16[4,128,1536]{2,1,0:T(8,128)(2,1)} %broadcast_in_dim.55), calls=%async_computation | async-start | bytes 3145728 | tf_op jit(solution)/shard_map/all_to_all | solution.py:93
  23.5 17.5 %reduce-window.19 = s32[32,8,128]{2,1,0:T(8,128)} reduce-window(s32[32,8,128]{2,1,0:T(8,128)} %fusion.62, s32[]{:T(128)} %constant.24.clone.1), window={size=1x1x128 pad=0_0x0_0x127_0}, to_apply=%region_11.12 | reduce-window | flops 4161536 | bytes 262148 | tf_op jit(solution)/shard_map/reduce-window.2
  40.9 1.7 slice.94
  45.0 1.7 broadcast_add_fusion
  53.5 4.3 %scatter_custom_fusion = s32[1280]{0:T(1024)S(1)} fusion(s32[1024]{0:T(1024)S(1)} %bitcast.196, s32[1024]{0:T(1024)S(1)} %reshape.362, s32[]{:T(128)} %constant.23.clone.1), kind=kCustom, calls=%fused_computation.95 | custom fusion | bytes 5124 | tf_op jit(solution)/shard_map/scatter | solution.py:159
  62.2 2.2 convolution_convert_fusion.1
  64.4 2.2 copy.51
  66.5 4.8 %all-to-all-start.1 = ((bf16[4,128,640]{1,2,0:T(8,128)(2,1)}), bf16[4,128,640]{1,2,0:T(8,128)(2,1)S(1)}, u32[]{:S(2)}, u32[]{:S(2)}) async-start(bf16[4,128,640]{1,2,0:T(8,128)(2,1)} %copy.51), calls=%async_computation.1 | async-start | bytes 1310720 | tf_op jit(solution)/shard_map/all_to_all | solution.py:95
  74.2 7.4 %all-to-all-done.1 = bf16[4,128,640]{1,2,0:T(8,128)(2,1)S(1)} async-done(((bf16[4,128,640]{1,2,0:T(8,128)(2,1)}), bf16[4,128,640]{1,2,0:T(8,128)(2,1)S(1)}, u32[]{:S(2)}, u32[]{:S(2)}) %all-to-all-start.1) | async-done | bytes 655392 | tf_op jit(solution)/shard_map/all_to_all | solution.py:95
  83.4 1.9 collective-permute-start
  85.6 5.5 %collective-permute-done = bf16[1,128,2,512]{1,3,2,0:T(8,128)(2,1)S(1)} collective-permute-done((bf16[1,128,2,512]{1,3,2,0:T(8,128)(2,1)S(1)}, bf16[1,128,2,512]{1,3,2,0:T(8,128)(2,1)S(1)}, u32[]{:S(2)}, u32[]{:S(2)}) %collective-permute-start) | collective-permute-done | bytes 262176 | tf_op jit(solution)/shard_map/ppermute | solution.py:23
  91.9 4.0 collective-permute-start.1
  95.9 3.3 fusion.72
  100.5 2.3 copy.58
  102.8 3.7 bitcast_reduce_fusion
  110.8 1.7 copy-done.2
  115.7 1.7 fusion.34
  119.1 25.9 %all-gather.4.cloned.1.call-done = bf16[1536,1536]{1,0:T(8,128)(2,1)} async-done(((bf16[384,1536]{1,0:T(8,128)(2,1)}), bf16[1536,1536]{1,0:T(8,128)(2,1)}) %all-gather.4.cloned.1.call-update) | async-done | bytes 4718608 | tf_op jit(solution)/shard_map/all_gather | solution.py:91
  145.0 3.2 fusion.47
  148.5 5.4 %gather_fusion = bf16[1280,1536]{1,0:T(8,128)(2,1)} fusion(bf16[129,1536]{1,0:T(8,128)(2,1)S(1)} %concatenate.40, s32[2048]{0:T(1024)S(1)} %copy-done.10), kind=kCustom, calls=%fused_computation | custom fusion | bytes 7869440 | tf_op jit(solution)/shard_map/gather | solution.py:161
  153.9 100.4 %all_to_all.20 = bf16[32,40,1536]{2,1,0:T(8,128)(2,1)S(1)} all-to-all(bf16[32,40,1536]{2,1,0:T(8,128)(2,1)} %bitcast.170), channel_id=1, replica_groups=mesh['dp'=4,'chip'=32,'core'=2] {'chip'}, dimensions={0} | all-to-all | bytes 7864320 | tf_op jit(solution)/shard_map/all_to_all | solution.py:162
  254.3 1.9 copy-done.3
  256.3 6.9 %collective-permute-done.2 = bf16[32,40,1536]{2,1,0:T(8,128)(2,1)} collective-permute-done((bf16[32,40,1536]{2,1,0:T(8,128)(2,1)S(1)}, bf16[32,40,1536]{2,1,0:T(8,128)(2,1)}, u32[]{:S(2)}, u32[]{:S(2)}) %collective-permute-start.2) | collective-permute-done | bytes 3932192 | tf_op jit(solution)/shard_map/ppermute | solution.py:163
  263.2 7.1 %pad_maximum_fusion = bf16[64,40,1536]{2,1,0:T(8,128)(2,1)} fusion(bf16[32,40,1536]{2,1,0:T(8,128)(2,1)} %collective-permute-done.2, bf16[32,40,1536]{2,1,0:T(8,128)(2,1)} %copy-done.3), kind=kLoop, calls=%fused_computation.4 | loop fusion | flops 3932160 | bytes 15728640 | tf_op jit(solution)/shard_map/concatenate | solution.py:164
  270.3 6.6 %fusion.18 = f32[2560,512]{1,0:T(8,128)S(1)} fusion(bf16[2560,1536]{1,0:T(8,128)(2,1)} %bitcast.172, bf16[1,1536,512]{2,1,0:T(8,128)(2,1)S(1)} %copy-done.20), kind=kOutput, calls=%fused_computation.28 | convolution fusion | flops 4026531840 | bytes 14680064 | tf_op jit(solution)/shard_map/dot_general | solution.py:165
  276.9 2.3 convolution_convert_fusion
  280.0 6.6 %collective-permute-done.3 = bf16[32,40,1536]{2,1,0:T(8,128)(2,1)S(1)} collective-permute-done((bf16[32,40,1536]{2,1,0:T(8,128)(2,1)S(1)}, bf16[32,40,1536]{2,1,0:T(8,128)(2,1)S(1)}, u32[]{:S(2)}, u32[]{:S(2)}) %collective-permute-start.3) | collective-permute-done | bytes 3932192 | tf_op jit(solution)/shard_map/ppermute | solution.py:169
  286.6 3.0 fusion
  289.6 5.1 %all-to-all-start.3 = ((bf16[32,40,1536]{2,1,0:T(8,128)(2,1)}), bf16[32,40,1536]{2,1,0:T(8,128)(2,1)}, u32[]{:S(2)}, u32[]{:S(2)}) async-start(bf16[32,40,1536]{2,1,0:T(8,128)(2,1)} %fusion), calls=%async_computation.3 | async-start | bytes 7864320 | tf_op jit(solution)/shard_map/all_to_all | solution.py:171
  294.9 90.3 %all-to-all-done.3 = bf16[32,40,1536]{2,1,0:T(8,128)(2,1)} async-done(((bf16[32,40,1536]{2,1,0:T(8,128)(2,1)}), bf16[32,40,1536]{2,1,0:T(8,128)(2,1)}, u32[]{:S(2)}, u32[]{:S(2)}) %all-to-all-start.3) | async-done | bytes 3932192 | tf_op jit(solution)/shard_map/all_to_all | solution.py:171
  385.1 10.0 %gather_fusion.1 = bf16[1024,1536]{1,0:T(8,128)(2,1)} fusion(bf16[1280,1536]{1,0:T(8,128)(2,1)} %bitcast.52, s32[1024]{0:T(1024)S(1)} %broadcast_clamp_fusion), kind=kCustom, calls=%fused_computation.1 | custom fusion | bytes 6295552 | tf_op jit(solution)/shard_map/gather | solution.py:172
  395.2 2.8 fusion.9
  (116 shorter events, 43.3 us)
Async XLA Ops:
  7.2 55.0 %copy-start = (bf16[1536,640]{1,0:T(8,128)(2,1)S(1)}, bf16[1536,640]{1,0:T(8,128)(2,1)}, u32[]{:S(2)}) copy-start(bf16[1536,640]{1,0:T(8,128)(2,1)} %param.13) | copy-start | bytes 5898244
  7.2 10.1 %copy-start.13 = (s32[1,128,8]{1,2,0:T(8,128)S(1)}, s32[1,128,8]{1,2,0:T(8,128)}, u32[]{:S(2)}) copy-start(s32[1,128,8]{1,2,0:T(8,128)} %param.18) | copy-start | bytes 12292
  7.2 14.4 %copy-start.19 = (s32[1,256]{1,0:T(1,128)S(1)}, s32[1,256]{1,0:T(1,128)}, u32[]{:S(2)}) copy-start(s32[1,256]{1,0:T(1,128)} %param.16) | copy-start | bytes 3076
  7.2 88.7 %all-gather.6.cloned.1.call-start = ((), (), s32[]{:S(2)}) async-start(), calls=%async_computation.5 | async-start | bytes 1064960 | tf_op jit(solution)/shard_map/all_gather | solution.py:139
  11.6 50.6 %all-to-all-start = ((bf16[4,128,1536]{2,1,0:T(8,128)(2,1)}), bf16[4,128,1536]{2,1,0:T(8,128)(2,1)S(1)}, u32[]{:S(2)}, u32[]{:S(2)}) async-start(bf16[4,128,1536]{2,1,0:T(8,128)(2,1)} %broadcast_in_dim.55), calls=%async_computation | async-start | bytes 3145728 | tf_op jit(solution)/shard_map/all_to_all | solution.py:93
  16.0 129.0 %all-gather.4.cloned.1.call-start = ((), (), s32[]{:S(2)}) async-start(), calls=%async_computation.4 | async-start | bytes 5898240 | tf_op jit(solution)/shard_map/all_gather | solution.py:91
  50.0 10.7 %copy-start.14 = (s32[1024,1]{0,1:T(1,128)}, s32[1024,1]{0,1:T(1,128)S(1)}, u32[]{:S(2)}) copy-start(s32[1024,1]{0,1:T(1,128)S(1)} %compare_select_fusion.1) | copy-start | bytes 12292
  60.6 1.5 copy-start.11
  62.1 10.6 %copy-start.12 = (s32[512]{0:T(512)S(1)}, s32[512]{0:T(512)}, u32[]{:S(2)}) copy-start(s32[512]{0:T(512)} %copy-done.11) | copy-start | bytes 6148
  62.1 10.6 %copy-start.17 = (s32[512]{0:T(512)S(1)}, s32[512]{0:T(512)}, u32[]{:S(2)}) copy-start(s32[512]{0:T(512)} %convert_reduce_fusion) | copy-start | bytes 6148
  64.4 21.1 %copy-start.8 = (f32[128,64]{0,1:T(8,128)S(1)}, f32[128,64]{0,1:T(8,128)}, u32[]{:S(2)}) copy-start(f32[128,64]{0,1:T(8,128)} %get-tuple-element.29) | copy-start | bytes 98308
  64.4 21.1 %copy-start.9 = (f32[128,64]{0,1:T(8,128)S(1)}, f32[128,64]{0,1:T(8,128)}, u32[]{:S(2)}) copy-start(f32[128,64]{0,1:T(8,128)} %get-tuple-element.30) | copy-start | bytes 98308
  66.5 15.1 %all-to-all-start.1 = ((bf16[4,128,640]{1,2,0:T(8,128)(2,1)}), bf16[4,128,640]{1,2,0:T(8,128)(2,1)S(1)}, u32[]{:S(2)}, u32[]{:S(2)}) async-start(bf16[4,128,640]{1,2,0:T(8,128)(2,1)} %copy.51), calls=%async_computation.1 | async-start | bytes 1310720 | tf_op jit(solution)/shard_map/all_to_all | solution.py:95
  83.4 7.7 %collective-permute-start = (bf16[1,128,2,512]{1,3,2,0:T(8,128)(2,1)S(1)}, bf16[1,128,2,512]{1,3,2,0:T(8,128)(2,1)S(1)}, u32[]{:S(2)}, u32[]{:S(2)}) collective-permute-start(bf16[1,128,2,512]{1,3,2,0:T(8,128)(2,1)S(1)} %maximum_bitcast_fusion), channel_id=1, source_target_pairs={{0,1},{1,2},{2,3},{3,4},{4,5},{5,6},{6,7},{7,8},{8,9},{9,10},{10,1... | collective-permute-start | bytes 786440 | tf_op jit(solution)/shard_map/ppermute | solution.py:23
  91.9 15.6 %collective-permute-start.1 = (bf16[2,128,2,512]{1,3,2,0:T(8,128)(2,1)}, bf16[2,128,2,512]{1,3,2,0:T(8,128)(2,1)}, u32[]{:S(2)}, u32[]{:S(2)}) collective-permute-start(bf16[2,128,2,512]{1,3,2,0:T(8,128)(2,1)} %pad_maximum_fusion.2), channel_id=1, source_target_pairs={{0,2},{1,3},{2,4},{3,5},{4,6},{5,7},{6,8},{7,9},{8,10},{9,11},{10,... | collective-permute-start | bytes 1572872 | tf_op jit(solution)/shard_map/ppermute | solution.py:23
  106.5 3.2 copy-start.6
  109.7 2.8 copy-start.2
  115.7 1.8 copy-start.7
  117.4 27.6 %copy-start.4 = (bf16[1,128,1536]{2,1,0:T(8,128)(2,1)S(1)}, bf16[1,128,1536]{2,1,0:T(8,128)(2,1)}, u32[]{:S(2)}) copy-start(bf16[1,128,1536]{2,1,0:T(8,128)(2,1)} %param.11) | copy-start | bytes 1179652
  119.1 29.2 %copy-start.16 = (f32[1536]{0:T(1024)S(1)}, f32[1536]{0:T(1024)}, u32[]{:S(2)}) copy-start(f32[1536]{0:T(1024)} %param.17) | copy-start | bytes 18436
  119.1 29.4 %copy-start.10 = (s32[2048]{0:T(1024)S(1)}, s32[2048]{0:T(1024)}, u32[]{:S(2)}) copy-start(s32[2048]{0:T(1024)} %pad_clamp_fusion) | copy-start | bytes 24580
  148.2 249.8 %copy-start.5 = (bf16[128,1536]{1,0:T(8,128)(2,1)}, bf16[128,1536]{1,0:T(8,128)(2,1)S(1)}, u32[]{:S(2)}) copy-start(bf16[128,1536]{1,0:T(8,128)(2,1)S(1)} %get-tuple-element.28) | copy-start | bytes 1179652
  254.3 1.9 copy-start.3
  256.3 14.0 %copy-start.20 = (bf16[1,1536,512]{2,1,0:T(8,128)(2,1)S(1)}, bf16[1,1536,512]{2,1,0:T(8,128)(2,1)}, u32[]{:S(2)}) copy-start(bf16[1,1536,512]{2,1,0:T(8,128)(2,1)} %param.20) | copy-start | bytes 4718596
  256.3 6.9 %collective-permute-start.2 = (bf16[32,40,1536]{2,1,0:T(8,128)(2,1)S(1)}, bf16[32,40,1536]{2,1,0:T(8,128)(2,1)}, u32[]{:S(2)}, u32[]{:S(2)}) collective-permute-start(bf16[32,40,1536]{2,1,0:T(8,128)(2,1)S(1)} %all_to_all.20), channel_id=1, source_target_pairs={{0,1},{1,0},{2,3},{3,2},{4,5},{5,4},{6,7},{7,6},{8,9},{9,8},{10,11... | collective-permute-start | bytes 11796488 | tf_op jit(solution)/shard_map/ppermute | solution.py:163
  270.3 6.6 %copy-start.21 = (bf16[1,256,1536]{2,1,0:T(8,128)(2,1)S(1)}, bf16[1,256,1536]{2,1,0:T(8,128)(2,1)}, u32[]{:S(2)}) copy-start(bf16[1,256,1536]{2,1,0:T(8,128)(2,1)} %param.21) | copy-start | bytes 2359300
  279.7 6.9 %collective-permute-start.3 = (bf16[32,40,1536]{2,1,0:T(8,128)(2,1)S(1)}, bf16[32,40,1536]{2,1,0:T(8,128)(2,1)S(1)}, u32[]{:S(2)}, u32[]{:S(2)}) collective-permute-start(bf16[32,40,1536]{2,1,0:T(8,128)(2,1)S(1)} %bitcast.177), channel_id=1, source_target_pairs={{0,1},{1,0},{2,3},{3,2},{4,5},{5,4},{6,7},{7,6},{8,9},{9,8},{10,11... | collective-permute-start | bytes 11796488 | tf_op jit(solution)/shard_map/ppermute | solution.py:169
  289.6 5.1 %copy-start.18 = (f32[1,128,8]{1,2,0:T(8,128)S(1)}, f32[1,128,8]{1,2,0:T(8,128)}, u32[]{:S(2)}) copy-start(f32[1,128,8]{1,2,0:T(8,128)} %param.19) | copy-start | bytes 12292
  289.6 5.3 %copy-start.15 = (s32[1024,1]{0,1:T(1,128)S(1)}, s32[1024,1]{0,1:T(1,128)}, u32[]{:S(2)}) copy-start(s32[1024,1]{0,1:T(1,128)} %copy-done.14) | copy-start | bytes 12292
  289.6 95.6 %all-to-all-start.3 = ((bf16[32,40,1536]{2,1,0:T(8,128)(2,1)}), bf16[32,40,1536]{2,1,0:T(8,128)(2,1)}, u32[]{:S(2)}, u32[]{:S(2)}) async-start(bf16[32,40,1536]{2,1,0:T(8,128)(2,1)} %fusion), calls=%async_computation.3 | async-start | bytes 7864320 | tf_op jit(solution)/shard_map/all_to_all | solution.py:171
  385.1 13.7 %copy-start.1 = (bf16[1536,640]{1,0:T(8,128)(2,1)S(1)}, bf16[1536,640]{1,0:T(8,128)(2,1)}, u32[]{:S(2)}) copy-start(bf16[1536,640]{1,0:T(8,128)(2,1)} %param.13) | copy-start | bytes 5898244
Sparse Core Ops, SparseCore 0:
  10.8 78.4 all-gather.5
  91.1 53.8 all-gather.3

commit v3 on v2

--- a/solution.py
+++ b/solution.py
@@ -88,7 +88,8 @@
     inputs = tokens[0]
     normed = rms_norm(inputs, attn_gain)
     groups = lax.axis_size("dp")
-    full_out = lax.all_gather(out_weight, "dp", axis=0, tiled=True)
+    out_spread = jnp.broadcast_to(out_weight[None], (groups,) + out_weight.shape)
+    full_out = lax.all_to_all(out_spread, "dp", 0, 0, tiled=True).reshape(groups * out_weight.shape[0], -1)
     spread = jnp.broadcast_to(normed[None], (groups, rows, model))
     group_rows = lax.all_to_all(spread, "dp", 0, 0, tiled=True).reshape(groups * rows, model)
     qkv_part = jnp.dot(group_rows, qkv_weight, preferred_element_type=jnp.float32).astype(jnp.bfloat16)
@@ -150,10 +151,15 @@
     moe_input = rms_norm(hidden_state, ffn_gain)
     chips = lax.axis_size("chip")
     unit_ff = expert_in.shape[2] // 2
-    flat_ids = expert_ids[0].reshape(-1)
-    onehot = (flat_ids[:, None] == jnp.arange(EXPERTS, dtype=jnp.int32)[None, :]).astype(jnp.int32)
-    earlier_count = jnp.cumsum(onehot, axis=0, dtype=jnp.int32) - onehot
-    slots = jnp.sum(earlier_count * onehot, axis=1, dtype=jnp.int32)
+    own_ids = expert_ids[0]
+    flat_ids = own_ids.reshape(-1)
+    named = jnp.sum(
+        (own_ids[:, :, None] == jnp.arange(EXPERTS, dtype=jnp.int32)[None, None, :]).astype(jnp.float32), axis=1
+    )
+    order = jnp.arange(rows, dtype=jnp.int32)
+    below = (order[None, :] < order[:, None]).astype(jnp.bfloat16)
+    earlier = jnp.dot(below, named.astype(jnp.bfloat16), preferred_element_type=jnp.float32)
+    slots = jnp.take_along_axis(earlier, own_ids, axis=1).astype(jnp.int32).reshape(-1)
     target = flat_ids * CAP + slots
     row_of = jnp.repeat(jnp.arange(rows, dtype=jnp.int32), TOPK)
     source = jnp.full((chips * CAP,), rows, jnp.int32).at[target].set(row_of)
@@ -161,13 +167,16 @@
     outgoing = padded_input[source].reshape(chips, CAP, model)
     arrived = lax.all_to_all(outgoing, "chip", 0, 0, tiled=True)
     sibling = lax.ppermute(arrived, "core", [(0, 1), (1, 0)])
-    unit_rows = jnp.concatenate([arrived, sibling], axis=0).reshape(2 * chips * CAP, model)
-    inner = jnp.dot(unit_rows, expert_in[0], preferred_element_type=jnp.float32)
-    activated = (jax.nn.silu(inner[:, :unit_ff]) * inner[:, unit_ff:]).astype(jnp.bfloat16)
-    produced = jnp.dot(activated, expert_out[0], preferred_element_type=jnp.float32).astype(jnp.bfloat16)
-    produced = produced.reshape(2, chips, CAP, model)
-    partner = lax.ppermute(produced[1], "core", [(0, 1), (1, 0)])
-    summed = (produced[0].astype(jnp.float32) + partner.astype(jnp.float32)).astype(jnp.bfloat16)
+
+    def unit(block):
+        inner = jnp.dot(block.reshape(chips * CAP, model), expert_in[0], preferred_element_type=jnp.float32)
+        activated = (jax.nn.silu(inner[:, :unit_ff]) * inner[:, unit_ff:]).astype(jnp.bfloat16)
+        produced = jnp.dot(activated, expert_out[0], preferred_element_type=jnp.float32).astype(jnp.bfloat16)
+        return produced.reshape(chips, CAP, model)
+
+    own_part = unit(arrived)
+    partner = lax.ppermute(unit(sibling), "core", [(0, 1), (1, 0)])
+    summed = (own_part.astype(jnp.float32) + partner.astype(jnp.float32)).astype(jnp.bfloat16)
     returned = lax.all_to_all(summed, "chip", 0, 0, tiled=True)
     picked = returned.reshape(chips * CAP, model)[target].reshape(rows, TOPK, model)
     combined = jnp.einsum("tk,tkd->td", gate_weights[0], picked.astype(jnp.float32))

time: 408 us -> 366 us (0.90)
  other arithmetic: 52.9 us -> 16.7 us
  local copies, waits for them, and re-layouts: 47 us -> 41.5 us
    all_gather x1 -> x0, waiting for transfers between devices: 25.9 us -> none  [shards(): full_out = lax.all_gather(out_weight, 'dp', axis=0, tiled=True)]
    all_gather x1, waiting for transfers between devices: 0.02 us -> 21.8 us  [shards(): piece = lax.all_gather(prefix_cache[0], TENSOR, axis=0, tiled=True)]
    another operation x6 -> x3, other arithmetic: 20.2 us -> 0.42 us
    gather x0 -> x3, local copies, waits for them, and re-layouts: none -> 7.22 us  [shards(): jnp.take_along_axis(earlier, own_ids, axis=1).astype(jnp.int32).reshape(-1)]
    concatenate x1 -> x0, other arithmetic: 7.06 us -> none  [shards(): jnp.concatenate([arrived, sibling], axis=0).reshape(2 * chips * CAP, model)]
    all_to_all x1, waiting for transfers between devices: 0.01 us -> 6.97 us  [shards(): lax.all_to_all(spread, 'dp', 0, 0, tiled=True).reshape(groups * rows, model)]
    all_to_all x0 -> x1, starting transfers between devices: none -> 4.97 us  [shards(): lax.all_to_all(out_spread, 'dp', 0, 0, tiled=True)]
    unnamed x45 -> x37, local copies, waits for them, and re-layouts: 4.5 us -> 0.23 us
  transfers between devices with their start and end apart: 9 -> 9, of which waited for: 7 -> 7; matrix products, arithmetic and copies ran while one was open for 20% -> 14% of each run, Pallas kernels for 0% -> 0%
where the time goes in v3:
time: 366 us; the launch traced here: 363 us
  waiting for transfers between devices  143 us (39%)
  blocking collectives  98.3 us (27%)
  local copies, waits for them, and re-layouts  41.5 us (11%)
  matrix products  25 us (7%)
  starting transfers between devices  24.5 us (7%)
  other arithmetic  16.7 us (5%)
  between operations  14.5 us (4%)
    all_to_all x1, blocking collectives, shards(): arrived = lax.all_to_all(outgoing, 'chip', 0, 0, tiled=True)  98.3 us
    all_to_all x1, waiting for transfers between devices, shards(): returned = lax.all_to_all(summed, 'chip', 0, 0, tiled=True)  89.2 us
    all_gather x1, waiting for transfers between devices, shards(): piece = lax.all_gather(prefix_cache[0], TENSOR, axis=0, tiled=True)  21.8 us
    gather x1, local copies, waits for them, and re-layouts, shards(): returned.reshape(chips * CAP, model)[target].reshape(rows, TOPK, model)  10 us
    all_to_all x1, waiting for transfers between devices, shards(): lax.all_to_all(qkv_part.reshape(groups, rows, -1), 'dp', 0, 0, tiled=True)  8.36 us
  transfers between devices with their start and end apart: 9, of which 7 were waited for; matrix products, arithmetic and copies ran while one was open for 14% of the time, Pallas kernels for 0%

profile of v3, /device:TPU:32, one launch (start us, length us, event | category | flops | bytes accessed | tf_op | source)
XLA Modules:
  0.0 363.1 jit_solution(17586337651452222322)
XLA Ops:
  10.9 4.5 %all-to-all-start = ((bf16[4,128,1536]{2,1,0:T(8,128)(2,1)}), bf16[4,128,1536]{2,1,0:T(8,128)(2,1)}, u32[]{:S(2)}, u32[]{:S(2)}) async-start(bf16[4,128,1536]{2,1,0:T(8,128)(2,1)} %broadcast_in_dim.61), calls=%async_computation | async-start | bytes 3145728 | tf_op jit(solution)/shard_map/all_to_all | solution.py:94
  17.5 7.0 %gather_fusion.2 = f32[1024]{0:T(1024)S(1)} fusion(f32[128,32]{0,1:T(8,128)S(1)} %fusion.65, s32[1024]{0:T(1024)S(1)} %reshape.433), kind=kCustom, calls=%fused_computation.2 | custom fusion | bytes 16384 | tf_op jit(solution)/shard_map/jit(take_along_axis)/gather | solution.py:162
  24.6 4.3 %scatter_custom_fusion = s32[1280]{0:T(1024)S(1)} fusion(s32[1024]{0:T(1024)S(1)} %bitcast.190, s32[1024]{0:T(1024)S(1)} %reshape.443, s32[]{:T(128)} %constant.26.clone.1), kind=kCustom, calls=%fused_computation.105 | custom fusion | bytes 5124 | tf_op jit(solution)/shard_map/scatter | solution.py:165
  29.4 7.0 %all-to-all-done = bf16[4,128,1536]{2,1,0:T(8,128)(2,1)} async-done(((bf16[4,128,1536]{2,1,0:T(8,128)(2,1)}), bf16[4,128,1536]{2,1,0:T(8,128)(2,1)}, u32[]{:S(2)}, u32[]{:S(2)}) %all-to-all-start) | async-done | bytes 1572896 | tf_op jit(solution)/shard_map/all_to_all | solution.py:94
  36.4 3.7 %convolution_convert_fusion.2 = bf16[512,640]{1,0:T(8,128)(2,1)} fusion(bf16[512,1536]{1,0:T(8,128)(2,1)} %bitcast.5, bf16[1536,640]{1,0:T(8,128)(2,1)S(1)} %copy-done), kind=kOutput, calls=%fused_computation.31 | convolution fusion | flops 1006960640 | bytes 4194304 | tf_op jit(solution)/shard_map/dot_general | solution.py:95
  40.1 2.2 copy.46
  42.2 3.5 all-to-all-start.1
  47.5 8.4 %all-to-all-done.1 = bf16[4,128,640]{1,2,0:T(8,128)(2,1)S(1)} async-done(((bf16[4,128,640]{1,2,0:T(8,128)(2,1)}), bf16[4,128,640]{1,2,0:T(8,128)(2,1)S(1)}, u32[]{:S(2)}, u32[]{:S(2)}) %all-to-all-start.1) | async-done | bytes 655392 | tf_op jit(solution)/shard_map/all_to_all | solution.py:96
  55.8 2.6 broadcast_in_dim.118
  58.4 5.0 %all-to-all-start.2 = ((bf16[4,384,1536]{2,1,0:T(8,128)(2,1)}), bf16[4,384,1536]{2,1,0:T(8,128)(2,1)}, u32[]{:S(2)}, u32[]{:S(2)}) async-start(bf16[4,384,1536]{2,1,0:T(8,128)(2,1)} %broadcast_in_dim.118), calls=%async_computation.2 | async-start | bytes 9437184 | tf_op jit(solution)/shard_map/all_to_all | solution.py:92
  63.6 1.9 collective-permute-start
  65.8 5.5 %collective-permute-done = bf16[1,128,2,512]{1,3,2,0:T(8,128)(2,1)S(1)} collective-permute-done((bf16[1,128,2,512]{1,3,2,0:T(8,128)(2,1)S(1)}, bf16[1,128,2,512]{1,3,2,0:T(8,128)(2,1)S(1)}, u32[]{:S(2)}, u32[]{:S(2)}) %collective-permute-start) | collective-permute-done | bytes 262176 | tf_op jit(solution)/shard_map/ppermute | solution.py:23
  72.1 4.1 %collective-permute-start.1 = (bf16[2,128,2,512]{1,3,2,0:T(8,128)(2,1)}, bf16[2,128,2,512]{1,3,2,0:T(8,128)(2,1)}, u32[]{:S(2)}, u32[]{:S(2)}) collective-permute-start(bf16[2,128,2,512]{1,3,2,0:T(8,128)(2,1)} %pad_maximum_fusion.1), channel_id=1, source_target_pairs={{0,2},{1,3},{2,4},{3,5},{4,6},{5,7},{6,8},{7,9},{8,10},{9,11},{10,... | collective-permute-start | bytes 1572872 | tf_op jit(solution)/shard_map/ppermute | solution.py:23
  76.2 21.8 %all-gather.3.cloned.1.call-done = bf16[1,512,2,512]{3,2,0,1:T(2,128)(2,1)} async-done(((bf16[1,8,2,512]{3,2,0,1:T(2,128)(2,1)}), bf16[1,512,2,512]{3,2,0,1:T(2,128)(2,1)}) %all-gather.3.cloned.1.call-update) | async-done | bytes 1048592 | tf_op jit(solution)/shard_map/all_gather | solution.py:140
  98.0 3.1 fusion.79
  102.5 3.7 %bitcast_reduce_fusion = (f32[128,8,3]{0,2,1:T(4,128)S(1)}, f32[8,128,3,512]{3,1,2,0:T(8,128)}) fusion(bf16[128,8,3,64]{0,3,2,1:T(8,128)(2,1)S(1)} %fusion.53, bf16[512,8,64,1]{0,2,3,1:T(8,128)(2,1)S(1)} %bitcast.178), kind=kOutput, calls=%fused_computation.9 | convolution fusion | flops 204469248 | bytes 7221248 | tf_op jit(solution)/shard_map/tgrd,ngd->tgrn/dot_general | solution.py:145
  106.2 2.3 copy.53
  111.8 3.6 fusion.3
  117.0 1.7 fusion.35
  118.8 1.7 fusion.42
  120.5 3.2 fusion.48
  124.0 5.4 %gather_fusion = bf16[1280,1536]{1,0:T(8,128)(2,1)} fusion(bf16[129,1536]{1,0:T(8,128)(2,1)S(1)} %concatenate.37, s32[2048]{0:T(1024)S(1)} %copy-done.8), kind=kCustom, calls=%fused_computation | custom fusion | bytes 7869440 | tf_op jit(solution)/shard_map/gather | solution.py:167
  129.4 98.3 %all_to_all.25 = bf16[32,40,1536]{2,1,0:T(8,128)(2,1)S(1)} all-to-all(bf16[32,40,1536]{2,1,0:T(8,128)(2,1)} %bitcast.167), channel_id=1, replica_groups=mesh['dp'=4,'chip'=32,'core'=2] {'chip'}, dimensions={0} | all-to-all | bytes 7864320 | tf_op jit(solution)/shard_map/all_to_all | solution.py:168
  227.7 6.8 %collective-permute-done.2 = bf16[32,40,1536]{2,1,0:T(8,128)(2,1)S(1)} collective-permute-done((bf16[32,40,1536]{2,1,0:T(8,128)(2,1)S(1)}, bf16[32,40,1536]{2,1,0:T(8,128)(2,1)S(1)}, u32[]{:S(2)}, u32[]{:S(2)}) %collective-permute-start.2) | collective-permute-done | bytes 3932192 | tf_op jit(solution)/shard_map/ppermute | solution.py:169
  234.5 2.2 fusion.17
  238.2 2.2 fusion.19
  241.6 3.2 collective-permute-done.3
  244.8 2.9 fusion
  247.8 5.3 %all-to-all-start.4 = ((bf16[32,40,1536]{2,1,0:T(8,128)(2,1)}), bf16[32,40,1536]{2,1,0:T(8,128)(2,1)}, u32[]{:S(2)}, u32[]{:S(2)}) async-start(bf16[32,40,1536]{2,1,0:T(8,128)(2,1)} %fusion), calls=%async_computation.4 | async-start | bytes 7864320 | tf_op jit(solution)/shard_map/all_to_all | solution.py:180
  253.3 89.2 %all-to-all-done.4 = bf16[32,40,1536]{2,1,0:T(8,128)(2,1)} async-done(((bf16[32,40,1536]{2,1,0:T(8,128)(2,1)}), bf16[32,40,1536]{2,1,0:T(8,128)(2,1)}, u32[]{:S(2)}, u32[]{:S(2)}) %all-to-all-start.4) | async-done | bytes 3932192 | tf_op jit(solution)/shard_map/all_to_all | solution.py:180
  342.5 10.0 %gather_fusion.1 = bf16[1024,1536]{1,0:T(8,128)(2,1)} fusion(bf16[1280,1536]{1,0:T(8,128)(2,1)} %bitcast.54, s32[1024]{0:T(1024)S(1)} %broadcast_clamp_fusion), kind=kCustom, calls=%fused_computation.1 | custom fusion | bytes 6295552 | tf_op jit(solution)/shard_map/gather | solution.py:181
  352.5 2.8 fusion.9
  (102 shorter events, 19.3 us)
Async XLA Ops:
  7.2 29.2 %copy-start = (bf16[1536,640]{1,0:T(8,128)(2,1)S(1)}, bf16[1536,640]{1,0:T(8,128)(2,1)}, u32[]{:S(2)}) copy-start(bf16[1536,640]{1,0:T(8,128)(2,1)} %param.13) | copy-start | bytes 5898244
  7.2 9.0 %copy-start.7 = (s32[1,128,8]{1,2,0:T(8,128)S(1)}, s32[1,128,8]{1,2,0:T(8,128)}, u32[]{:S(2)}) copy-start(s32[1,128,8]{1,2,0:T(8,128)} %param.18) | copy-start | bytes 12292
  7.2 9.1 %copy-start.13 = (s32[1,256]{1,0:T(1,128)S(1)}, s32[1,256]{1,0:T(1,128)}, u32[]{:S(2)}) copy-start(s32[1,256]{1,0:T(1,128)} %param.16) | copy-start | bytes 3076
  10.9 25.4 %all-to-all-start = ((bf16[4,128,1536]{2,1,0:T(8,128)(2,1)}), bf16[4,128,1536]{2,1,0:T(8,128)(2,1)}, u32[]{:S(2)}, u32[]{:S(2)}) async-start(bf16[4,128,1536]{2,1,0:T(8,128)(2,1)} %broadcast_in_dim.61), calls=%async_computation | async-start | bytes 3145728 | tf_op jit(solution)/shard_map/all_to_all | solution.py:94
  15.4 82.6 %all-gather.3.cloned.1.call-start = ((), (), s32[]{:S(2)}) async-start(), calls=%async_computation.5 | async-start | bytes 1064960 | tf_op jit(solution)/shard_map/all_gather | solution.py:140
  24.5 11.8 %copy-start.9 = (s32[1024,1]{0,1:T(1,128)}, s32[1024,1]{0,1:T(1,128)S(1)}, u32[]{:S(2)}) copy-start(s32[1024,1]{0,1:T(1,128)S(1)} %compare_select_fusion.1) | copy-start | bytes 12292
  36.4 19.5 %copy-start.4 = (bf16[384,1536]{1,0:T(8,128)(2,1)S(1)}, bf16[384,1536]{1,0:T(8,128)(2,1)}, u32[]{:S(2)}) copy-start(bf16[384,1536]{1,0:T(8,128)(2,1)} %param.14) | copy-start | bytes 3538948
  42.2 13.6 %all-to-all-start.1 = ((bf16[4,128,640]{1,2,0:T(8,128)(2,1)}), bf16[4,128,640]{1,2,0:T(8,128)(2,1)S(1)}, u32[]{:S(2)}, u32[]{:S(2)}) async-start(bf16[4,128,640]{1,2,0:T(8,128)(2,1)} %copy.46), calls=%async_computation.1 | async-start | bytes 1310720 | tf_op jit(solution)/shard_map/all_to_all | solution.py:96
  58.4 62.0 %all-to-all-start.2 = ((bf16[4,384,1536]{2,1,0:T(8,128)(2,1)}), bf16[4,384,1536]{2,1,0:T(8,128)(2,1)}, u32[]{:S(2)}, u32[]{:S(2)}) async-start(bf16[4,384,1536]{2,1,0:T(8,128)(2,1)} %broadcast_in_dim.118), calls=%async_computation.2 | async-start | bytes 9437184 | tf_op jit(solution)/shard_map/all_to_all | solution.py:92
  63.6 7.7 %collective-permute-start = (bf16[1,128,2,512]{1,3,2,0:T(8,128)(2,1)S(1)}, bf16[1,128,2,512]{1,3,2,0:T(8,128)(2,1)S(1)}, u32[]{:S(2)}, u32[]{:S(2)}) collective-permute-start(bf16[1,128,2,512]{1,3,2,0:T(8,128)(2,1)S(1)} %maximum_bitcast_fusion), channel_id=1, source_target_pairs={{0,1},{1,2},{2,3},{3,4},{4,5},{5,6},{6,7},{7,8},{8,9},{9,10},{10,1... | collective-permute-start | bytes 786440 | tf_op jit(solution)/shard_map/ppermute | solution.py:23
  72.1 36.3 %collective-permute-start.1 = (bf16[2,128,2,512]{1,3,2,0:T(8,128)(2,1)}, bf16[2,128,2,512]{1,3,2,0:T(8,128)(2,1)}, u32[]{:S(2)}, u32[]{:S(2)}) collective-permute-start(bf16[2,128,2,512]{1,3,2,0:T(8,128)(2,1)} %pad_maximum_fusion.1), channel_id=1, source_target_pairs={{0,2},{1,3},{2,4},{3,5},{4,6},{5,7},{6,8},{7,9},{8,10},{9,11},{10,... | collective-permute-start | bytes 1572872 | tf_op jit(solution)/shard_map/ppermute | solution.py:23
  108.4 2.2 copy-start.5
  115.4 3.3 slice-start
  116.9 1.8 slice-start.1
  117.0 1.8 copy-start.6
  118.8 1.7 copy-start.2
  120.4 3.3 copy-start.11
  120.5 3.5 copy-start.8
  123.7 231.6 %copy-start.3 = (bf16[128,1536]{1,0:T(8,128)(2,1)}, bf16[128,1536]{1,0:T(8,128)(2,1)S(1)}, u32[]{:S(2)}) copy-start(bf16[128,1536]{1,0:T(8,128)(2,1)S(1)} %get-tuple-element.26) | copy-start | bytes 1179652
  129.4 105.1 %copy-start.14 = (bf16[1,1536,512]{2,1,0:T(8,128)(2,1)S(1)}, bf16[1,1536,512]{2,1,0:T(8,128)(2,1)}, u32[]{:S(2)}) copy-start(bf16[1,1536,512]{2,1,0:T(8,128)(2,1)} %param.20) | copy-start | bytes 4718596
  227.7 6.8 %collective-permute-start.2 = (bf16[32,40,1536]{2,1,0:T(8,128)(2,1)S(1)}, bf16[32,40,1536]{2,1,0:T(8,128)(2,1)S(1)}, u32[]{:S(2)}, u32[]{:S(2)}) collective-permute-start(bf16[32,40,1536]{2,1,0:T(8,128)(2,1)S(1)} %all_to_all.25), channel_id=1, source_target_pairs={{0,1},{1,0},{2,3},{3,2},{4,5},{5,4},{6,7},{7,6},{8,9},{9,8},{10,11... | collective-permute-start | bytes 11796488 | tf_op jit(solution)/shard_map/ppermute | solution.py:169
  234.5 2.2 copy-start.15
  237.9 6.9 %collective-permute-start.3 = (bf16[32,40,1536]{2,1,0:T(8,128)(2,1)S(1)}, bf16[32,40,1536]{2,1,0:T(8,128)(2,1)S(1)}, u32[]{:S(2)}, u32[]{:S(2)}) collective-permute-start(bf16[32,40,1536]{2,1,0:T(8,128)(2,1)S(1)} %bitcast.196), channel_id=1, source_target_pairs={{0,1},{1,0},{2,3},{3,2},{4,5},{5,4},{6,7},{7,6},{8,9},{9,8},{10,11... | collective-permute-start | bytes 11796488 | tf_op jit(solution)/shard_map/ppermute | solution.py:178
  247.8 5.4 %copy-start.12 = (f32[1,128,8]{1,2,0:T(8,128)S(1)}, f32[1,128,8]{1,2,0:T(8,128)}, u32[]{:S(2)}) copy-start(f32[1,128,8]{1,2,0:T(8,128)} %param.19) | copy-start | bytes 12292
  247.8 5.5 %copy-start.10 = (s32[1024,1]{0,1:T(1,128)S(1)}, s32[1024,1]{0,1:T(1,128)}, u32[]{:S(2)}) copy-start(s32[1024,1]{0,1:T(1,128)} %copy-done.9) | copy-start | bytes 12292
  247.8 94.7 %all-to-all-start.4 = ((bf16[32,40,1536]{2,1,0:T(8,128)(2,1)}), bf16[32,40,1536]{2,1,0:T(8,128)(2,1)}, u32[]{:S(2)}, u32[]{:S(2)}) async-start(bf16[32,40,1536]{2,1,0:T(8,128)(2,1)} %fusion), calls=%async_computation.4 | async-start | bytes 7864320 | tf_op jit(solution)/shard_map/all_to_all | solution.py:180
  342.5 13.7 %copy-start.1 = (bf16[1536,640]{1,0:T(8,128)(2,1)S(1)}, bf16[1536,640]{1,0:T(8,128)(2,1)}, u32[]{:S(2)}) copy-start(bf16[1536,640]{1,0:T(8,128)(2,1)} %param.13) | copy-start | bytes 5898244
Sparse Core Ops, SparseCore 0:
  19.0 78.9 all-gather.2

commit v4 on v3

--- a/solution.py
+++ b/solution.py
@@ -115,10 +115,7 @@
         jnp.zeros((rows, KV_HEADS, ratio), jnp.float32),
         jnp.zeros((rows, KV_HEADS, ratio, HEAD_DIM), jnp.float32),
     )
-    window = local_pairs[None]
-    for bit in range(SHIFTS):
-        earlier = from_behind(window, TENSOR, 2**bit)
-        window = jnp.concatenate([window, earlier], axis=0)
+    window = jnp.stack([local_pairs] + [from_behind(local_pairs, TENSOR, step) for step in range(1, 2**SHIFTS)])
     depth = window.shape[0]
     k_index = (
         (lane - jnp.arange(depth, dtype=jnp.int32))[:, None] * rows
@@ -137,7 +134,8 @@
         jnp.einsum("tgrd,ngd->tgrn", query, suffix_keys, preferred_element_type=jnp.float32) * scale
     )
     carry = merge_block(start_carry, scores, suffix_values, visible[:, None, None, :])
-    piece = lax.all_gather(prefix_cache[0], TENSOR, axis=0, tiled=True)
+    cache_spread = jnp.broadcast_to(prefix_cache[0][None], (lanes,) + prefix_cache.shape[1:])
+    piece = lax.all_to_all(cache_spread, TENSOR, 0, 0, tiled=True).reshape((prefix_len,) + prefix_cache.shape[2:])
     count = piece.shape[0]
     cached_keys = piece[:, 0].reshape(count, KV_HEADS, HEAD_DIM)
     cached_values = piece[:, 1].reshape(count, KV_HEADS, HEAD_DIM)

time: 366 us -> 406 us (1.11)
  waiting for transfers between devices: 143 us -> 188 us
  starting transfers between devices: 24.5 us -> 40.6 us
  between operations: 14.5 us -> 1.17 us
  other arithmetic: 16.7 us -> 11.6 us
    all_to_all x1, waiting for transfers between devices: 0.01 us -> 41.7 us  [shards(): lax.all_to_all(out_spread, 'dp', 0, 0, tiled=True)]
    ppermute x2 -> x3, waiting for transfers between devices: 5.49 us -> 29.4 us  [from_behind(): lax.ppermute(value, axis, [(source, source + steps) for source in range(f...]
    all_gather x1 -> x0, waiting for transfers between devices: 21.8 us -> none  [shards(): piece = lax.all_gather(prefix_cache[0], TENSOR, axis=0, tiled=True)]
    all_to_all x0 -> x1, starting transfers between devices: none -> 11.6 us  [shards(): lax.all_to_all(cache_spread, TENSOR, 0, 0, tiled=True)]
    slice x2, local copies, waits for them, and re-layouts: 5.39 us -> 0.28 us  [shards(): cached_values = piece[:, 1].reshape(count, KV_HEADS, HEAD_DIM)]
    ppermute x2 -> x3, starting transfers between devices: 5.98 us -> 10.6 us  [from_behind(): lax.ppermute(value, axis, [(source, source + steps) for source in range(f...]
  transfers between devices with their start and end apart: 9 -> 10, of which waited for: 7 -> 9; matrix products, arithmetic and copies ran while one was open for 14% -> 8% of each run, Pallas kernels for 0% -> 0%
where the time goes in v4:
time: 406 us; the launch traced here: 404 us
  waiting for transfers between devices  188 us (46%)
  blocking collectives  99.3 us (24%)
  starting transfers between devices  40.6 us (10%)
  local copies, waits for them, and re-layouts  39.5 us (10%)
  matrix products  24.1 us (6%)
  other arithmetic  11.6 us (3%)
    all_to_all x1, blocking collectives, shards(): arrived = lax.all_to_all(outgoing, 'chip', 0, 0, tiled=True)  99.3 us
    all_to_all x1, waiting for transfers between devices, shards(): returned = lax.all_to_all(summed, 'chip', 0, 0, tiled=True)  89.2 us
    all_to_all x1, waiting for transfers between devices, shards(): lax.all_to_all(out_spread, 'dp', 0, 0, tiled=True)  41.7 us
    ppermute x3, waiting for transfers between devices, from_behind(): lax.ppermute(value, axis, [(source, source + steps) for source in range(f...  29.4 us
    all_to_all x1, starting transfers between devices, shards(): lax.all_to_all(cache_spread, TENSOR, 0, 0, tiled=True)  11.6 us
    ppermute x3, starting transfers between devices, from_behind(): lax.ppermute(value, axis, [(source, source + steps) for source in range(f...  10.6 us
    gather x1, local copies, waits for them, and re-layouts, shards(): returned.reshape(chips * CAP, model)[target].reshape(rows, TOPK, model)  10 us
    all_to_all x1, waiting for transfers between devices, shards(): lax.all_to_all(qkv_part.reshape(groups, rows, -1), 'dp', 0, 0, tiled=True)  9.72 us
  transfers between devices with their start and end apart: 10, of which 9 were waited for; matrix products, arithmetic and copies ran while one was open for 8% of the time, Pallas kernels for 0%

profile of v4, /device:TPU:32, one launch (start us, length us, event | category | flops | bytes accessed | tf_op | source)
XLA Modules:
  0.0 403.8 jit_solution(1844425499034408386)
XLA Ops:
  4.4 4.5 %all-to-all-start = ((bf16[4,128,1536]{2,1,0:T(8,128)(2,1)}), bf16[4,128,1536]{2,1,0:T(8,128)(2,1)}, u32[]{:S(2)}, u32[]{:S(2)}) async-start(bf16[4,128,1536]{2,1,0:T(8,128)(2,1)} %broadcast_in_dim.63), calls=%async_computation | async-start | bytes 3145728 | tf_op jit(solution)/shard_map/all_to_all | solution.py:94
  10.1 7.0 %gather_fusion.2 = f32[1024]{0:T(1024)S(1)} fusion(f32[128,32]{0,1:T(8,128)S(1)} %fusion.65, s32[1024]{0:T(1024)S(1)} %reshape.437), kind=kCustom, calls=%fused_computation.2 | custom fusion | bytes 16384 | tf_op jit(solution)/shard_map/jit(take_along_axis)/gather | solution.py:160
  17.5 4.3 %scatter_custom_fusion = s32[1280]{0:T(1024)S(1)} fusion(s32[1024]{0:T(1024)S(1)} %bitcast.198, s32[1024]{0:T(1024)S(1)} %reshape.447, s32[]{:T(128)} %constant.26.clone.1), kind=kCustom, calls=%fused_computation.105 | custom fusion | bytes 5124 | tf_op jit(solution)/shard_map/scatter | solution.py:163
  22.3 7.5 %all-to-all-done = bf16[4,128,1536]{2,1,0:T(8,128)(2,1)} async-done(((bf16[4,128,1536]{2,1,0:T(8,128)(2,1)}), bf16[4,128,1536]{2,1,0:T(8,128)(2,1)}, u32[]{:S(2)}, u32[]{:S(2)}) %all-to-all-start) | async-done | bytes 1572896 | tf_op jit(solution)/shard_map/all_to_all | solution.py:94
  29.8 2.8 convolution_convert_fusion.2
  33.7 3.5 all-to-all-start.1
  37.6 9.7 %all-to-all-done.1 = bf16[4,128,640]{1,2,0:T(8,128)(2,1)S(1)} async-done(((bf16[4,128,640]{1,2,0:T(8,128)(2,1)}), bf16[4,128,640]{1,2,0:T(8,128)(2,1)S(1)}, u32[]{:S(2)}, u32[]{:S(2)}) %all-to-all-start.1) | async-done | bytes 655392 | tf_op jit(solution)/shard_map/all_to_all | solution.py:96
  48.4 11.6 %all-to-all-start.2 = ((bf16[64,8,2,512]{3,1,2,0:T(8,128)(2,1)}), bf16[64,8,2,512]{3,1,2,0:T(8,128)(2,1)S(1)}, u32[]{:S(2)}, u32[]{:S(2)}) async-start(bf16[64,8,2,512]{3,1,2,0:T(8,128)(2,1)} %broadcast_in_dim.122), calls=%async_computation.2 | async-start | bytes 2097152 | tf_op jit(solution)/shard_map/all_to_all | solution.py:138
  60.2 3.1 collective-permute-start.2
  63.3 3.4 collective-permute-start.1
  66.7 4.1 %collective-permute-start = (bf16[128,2,512]{0,2,1:T(8,128)(2,1)S(1)}, bf16[128,2,512]{0,2,1:T(8,128)(2,1)S(1)}, u32[]{:S(2)}, u32[]{:S(2)}) collective-permute-start(bf16[128,2,512]{0,2,1:T(8,128)(2,1)S(1)} %get-tuple-element.15), channel_id=1, source_target_pairs={{0,1},{1,2},{2,3},{3,4},{4,5},{5,6},{6,7},{7,8},{8,9},{9,10},{10,1... | collective-permute-start | bytes 786440 | tf_op jit(solution)/shard_map/ppermute | solution.py:23
  71.1 20.2 %collective-permute-done.2 = bf16[128,2,512]{0,2,1:T(8,128)(2,1)S(1)} collective-permute-done((bf16[128,2,512]{0,2,1:T(8,128)(2,1)S(1)}, bf16[128,2,512]{0,2,1:T(8,128)(2,1)S(1)}, u32[]{:S(2)}, u32[]{:S(2)}) %collective-permute-start.2) | collective-permute-done | bytes 262176 | tf_op jit(solution)/shard_map/ppermute | solution.py:23
  91.3 7.0 %collective-permute-done.1 = bf16[128,2,512]{0,2,1:T(8,128)(2,1)S(1)} collective-permute-done((bf16[128,2,512]{0,2,1:T(8,128)(2,1)S(1)}, bf16[128,2,512]{0,2,1:T(8,128)(2,1)S(1)}, u32[]{:S(2)}, u32[]{:S(2)}) %collective-permute-start.1) | collective-permute-done | bytes 262176 | tf_op jit(solution)/shard_map/ppermute | solution.py:23
  98.2 2.3 collective-permute-done
  104.5 3.8 broadcast_in_dim.123
  108.3 5.1 %all-to-all-start.3 = ((bf16[4,384,1536]{2,1,0:T(8,128)(2,1)}), bf16[4,384,1536]{2,1,0:T(8,128)(2,1)}, u32[]{:S(2)}, u32[]{:S(2)}) async-start(bf16[4,384,1536]{2,1,0:T(8,128)(2,1)} %broadcast_in_dim.123), calls=%async_computation.3 | async-start | bytes 9437184 | tf_op jit(solution)/shard_map/all_to_all | solution.py:92
  113.5 3.7 fusion.2
  122.2 1.7 fusion.35
  123.9 1.7 fusion.42
  125.6 41.7 %all-to-all-done.3 = bf16[4,384,1536]{2,1,0:T(8,128)(2,1)} async-done(((bf16[4,384,1536]{2,1,0:T(8,128)(2,1)}), bf16[4,384,1536]{2,1,0:T(8,128)(2,1)}, u32[]{:S(2)}, u32[]{:S(2)}) %all-to-all-start.3) | async-done | bytes 4718624 | tf_op jit(solution)/shard_map/all_to_all | solution.py:92
  167.3 3.2 fusion.48
  170.8 5.4 %gather_fusion = bf16[1280,1536]{1,0:T(8,128)(2,1)} fusion(bf16[129,1536]{1,0:T(8,128)(2,1)S(1)} %concatenate.28, s32[2048]{0:T(1024)S(1)} %pad_clamp_fusion), kind=kCustom, calls=%fused_computation | custom fusion | bytes 7869440 | tf_op jit(solution)/shard_map/gather | solution.py:165
  176.2 99.3 %all_to_all.30 = bf16[32,40,1536]{2,1,0:T(8,128)(2,1)S(1)} all-to-all(bf16[32,40,1536]{2,1,0:T(8,128)(2,1)} %bitcast.172), channel_id=1, replica_groups=mesh['dp'=4,'chip'=32,'core'=2] {'chip'}, dimensions={0} | all-to-all | bytes 7864320 | tf_op jit(solution)/shard_map/all_to_all | solution.py:166
  275.5 6.8 %collective-permute-done.3 = bf16[32,40,1536]{2,1,0:T(8,128)(2,1)S(1)} collective-permute-done((bf16[32,40,1536]{2,1,0:T(8,128)(2,1)S(1)}, bf16[32,40,1536]{2,1,0:T(8,128)(2,1)S(1)}, u32[]{:S(2)}, u32[]{:S(2)}) %collective-permute-start.3) | collective-permute-done | bytes 3932192 | tf_op jit(solution)/shard_map/ppermute | solution.py:167
  282.3 2.2 fusion.17
  286.0 2.2 fusion.19
  289.4 3.2 collective-permute-done.4
  292.6 3.0 fusion
  295.6 5.1 %all-to-all-start.5 = ((bf16[32,40,1536]{2,1,0:T(8,128)(2,1)}), bf16[32,40,1536]{2,1,0:T(8,128)(2,1)}, u32[]{:S(2)}, u32[]{:S(2)}) async-start(bf16[32,40,1536]{2,1,0:T(8,128)(2,1)} %fusion), calls=%async_computation.5 | async-start | bytes 7864320 | tf_op jit(solution)/shard_map/all_to_all | solution.py:178
  300.9 89.2 %all-to-all-done.5 = bf16[32,40,1536]{2,1,0:T(8,128)(2,1)} async-done(((bf16[32,40,1536]{2,1,0:T(8,128)(2,1)}), bf16[32,40,1536]{2,1,0:T(8,128)(2,1)}, u32[]{:S(2)}, u32[]{:S(2)}) %all-to-all-start.5) | async-done | bytes 3932192 | tf_op jit(solution)/shard_map/all_to_all | solution.py:178
  390.1 10.0 %gather_fusion.1 = bf16[1024,1536]{1,0:T(8,128)(2,1)} fusion(bf16[1280,1536]{1,0:T(8,128)(2,1)} %bitcast.57, s32[1024]{0:T(1024)S(1)} %broadcast_clamp_fusion), kind=kCustom, calls=%fused_computation.1 | custom fusion | bytes 6295552 | tf_op jit(solution)/shard_map/gather | solution.py:179
  400.1 2.8 fusion.9
  (97 shorter events, 21.4 us)
Async XLA Ops:
  0.6 29.2 %copy-start = (bf16[1536,640]{1,0:T(8,128)(2,1)S(1)}, bf16[1536,640]{1,0:T(8,128)(2,1)}, u32[]{:S(2)}) copy-start(bf16[1536,640]{1,0:T(8,128)(2,1)} %param.13) | copy-start | bytes 5898244
  0.6 8.2 %copy-start.5 = (s32[1,128,8]{1,2,0:T(8,128)S(1)}, s32[1,128,8]{1,2,0:T(8,128)}, u32[]{:S(2)}) copy-start(s32[1,128,8]{1,2,0:T(8,128)} %param.18) | copy-start | bytes 12292
  0.7 8.4 %copy-start.9 = (s32[1,256]{1,0:T(1,128)S(1)}, s32[1,256]{1,0:T(1,128)}, u32[]{:S(2)}) copy-start(s32[1,256]{1,0:T(1,128)} %param.16) | copy-start | bytes 3076
  4.4 25.4 %all-to-all-start = ((bf16[4,128,1536]{2,1,0:T(8,128)(2,1)}), bf16[4,128,1536]{2,1,0:T(8,128)(2,1)}, u32[]{:S(2)}, u32[]{:S(2)}) async-start(bf16[4,128,1536]{2,1,0:T(8,128)(2,1)} %broadcast_in_dim.63), calls=%async_computation | async-start | bytes 3145728 | tf_op jit(solution)/shard_map/all_to_all | solution.py:94
  29.8 7.4 %copy-start.6 = (bf16[1,8,2,512]{3,2,1,0:T(2,128)(2,1)S(1)}, bf16[1,8,2,512]{3,2,1,0:T(2,128)(2,1)}, u32[]{:S(2)}) copy-start(bf16[1,8,2,512]{3,2,1,0:T(2,128)(2,1)} %param.15) | copy-start | bytes 49156
  33.7 13.6 %all-to-all-start.1 = ((bf16[4,128,640]{1,2,0:T(8,128)(2,1)}), bf16[4,128,640]{1,2,0:T(8,128)(2,1)S(1)}, u32[]{:S(2)}, u32[]{:S(2)}) async-start(bf16[4,128,640]{1,2,0:T(8,128)(2,1)} %copy.48), calls=%async_computation.1 | async-start | bytes 1310720 | tf_op jit(solution)/shard_map/all_to_all | solution.py:96
  48.4 56.1 %all-to-all-start.2 = ((bf16[64,8,2,512]{3,1,2,0:T(8,128)(2,1)}), bf16[64,8,2,512]{3,1,2,0:T(8,128)(2,1)S(1)}, u32[]{:S(2)}, u32[]{:S(2)}) async-start(bf16[64,8,2,512]{3,1,2,0:T(8,128)(2,1)} %broadcast_in_dim.122), calls=%async_computation.2 | async-start | bytes 2097152 | tf_op jit(solution)/shard_map/all_to_all | solution.py:138
  60.2 31.1 %collective-permute-start.2 = (bf16[128,2,512]{0,2,1:T(8,128)(2,1)S(1)}, bf16[128,2,512]{0,2,1:T(8,128)(2,1)S(1)}, u32[]{:S(2)}, u32[]{:S(2)}) collective-permute-start(bf16[128,2,512]{0,2,1:T(8,128)(2,1)S(1)} %get-tuple-element.15), channel_id=1, source_target_pairs={{0,3},{1,4},{2,5},{3,6},{4,7},{5,8},{6,9},{7,10},{8,11},{9,12},{10... | collective-permute-start | bytes 786440 | tf_op jit(solution)/shard_map/ppermute | solution.py:23
  63.3 34.9 %collective-permute-start.1 = (bf16[128,2,512]{0,2,1:T(8,128)(2,1)S(1)}, bf16[128,2,512]{0,2,1:T(8,128)(2,1)S(1)}, u32[]{:S(2)}, u32[]{:S(2)}) collective-permute-start(bf16[128,2,512]{0,2,1:T(8,128)(2,1)S(1)} %get-tuple-element.15), channel_id=1, source_target_pairs={{0,2},{1,3},{2,4},{3,5},{4,6},{5,7},{6,8},{7,9},{8,10},{9,11},{10,... | collective-permute-start | bytes 786440 | tf_op jit(solution)/shard_map/ppermute | solution.py:23
  66.7 33.9 %collective-permute-start = (bf16[128,2,512]{0,2,1:T(8,128)(2,1)S(1)}, bf16[128,2,512]{0,2,1:T(8,128)(2,1)S(1)}, u32[]{:S(2)}, u32[]{:S(2)}) collective-permute-start(bf16[128,2,512]{0,2,1:T(8,128)(2,1)S(1)} %get-tuple-element.15), channel_id=1, source_target_pairs={{0,1},{1,2},{2,3},{3,4},{4,5},{5,6},{6,7},{7,8},{8,9},{9,10},{10,1... | collective-permute-start | bytes 786440 | tf_op jit(solution)/shard_map/ppermute | solution.py:23
  108.3 59.0 %all-to-all-start.3 = ((bf16[4,384,1536]{2,1,0:T(8,128)(2,1)}), bf16[4,384,1536]{2,1,0:T(8,128)(2,1)}, u32[]{:S(2)}, u32[]{:S(2)}) async-start(bf16[4,384,1536]{2,1,0:T(8,128)(2,1)} %broadcast_in_dim.123), calls=%async_computation.3 | async-start | bytes 9437184 | tf_op jit(solution)/shard_map/all_to_all | solution.py:92
  117.7 2.8 slice-start
  117.8 2.9 slice-start.1
  120.5 1.6 copy-start.4
  123.9 43.4 %copy-start.2 = (bf16[1,128,1536]{2,1,0:T(8,128)(2,1)S(1)}, bf16[1,128,1536]{2,1,0:T(8,128)(2,1)}, u32[]{:S(2)}) copy-start(bf16[1,128,1536]{2,1,0:T(8,128)(2,1)} %param.11) | copy-start | bytes 1179652
  125.6 45.0 %copy-start.7 = (f32[1536]{0:T(1024)S(1)}, f32[1536]{0:T(1024)}, u32[]{:S(2)}) copy-start(f32[1536]{0:T(1024)} %param.17) | copy-start | bytes 18436
  170.5 232.4 %copy-start.3 = (bf16[128,1536]{1,0:T(8,128)(2,1)}, bf16[128,1536]{1,0:T(8,128)(2,1)S(1)}, u32[]{:S(2)}) copy-start(bf16[128,1536]{1,0:T(8,128)(2,1)S(1)} %get-tuple-element.28) | copy-start | bytes 1179652
  176.2 106.0 %copy-start.10 = (bf16[1,1536,512]{2,1,0:T(8,128)(2,1)S(1)}, bf16[1,1536,512]{2,1,0:T(8,128)(2,1)}, u32[]{:S(2)}) copy-start(bf16[1,1536,512]{2,1,0:T(8,128)(2,1)} %param.20) | copy-start | bytes 4718596
  275.5 6.8 %collective-permute-start.3 = (bf16[32,40,1536]{2,1,0:T(8,128)(2,1)S(1)}, bf16[32,40,1536]{2,1,0:T(8,128)(2,1)S(1)}, u32[]{:S(2)}, u32[]{:S(2)}) collective-permute-start(bf16[32,40,1536]{2,1,0:T(8,128)(2,1)S(1)} %all_to_all.30), channel_id=1, source_target_pairs={{0,1},{1,0},{2,3},{3,2},{4,5},{5,4},{6,7},{7,6},{8,9},{9,8},{10,11... | collective-permute-start | bytes 11796488 | tf_op jit(solution)/shard_map/ppermute | solution.py:167
  282.3 2.2 copy-start.11
  285.8 6.9 %collective-permute-start.4 = (bf16[32,40,1536]{2,1,0:T(8,128)(2,1)S(1)}, bf16[32,40,1536]{2,1,0:T(8,128)(2,1)S(1)}, u32[]{:S(2)}, u32[]{:S(2)}) collective-permute-start(bf16[32,40,1536]{2,1,0:T(8,128)(2,1)S(1)} %bitcast.204), channel_id=1, source_target_pairs={{0,1},{1,0},{2,3},{3,2},{4,5},{5,4},{6,7},{7,6},{8,9},{9,8},{10,11... | collective-permute-start | bytes 11796488 | tf_op jit(solution)/shard_map/ppermute | solution.py:176
  295.6 5.1 %copy-start.8 = (f32[1,128,8]{1,2,0:T(8,128)S(1)}, f32[1,128,8]{1,2,0:T(8,128)}, u32[]{:S(2)}) copy-start(f32[1,128,8]{1,2,0:T(8,128)} %param.19) | copy-start | bytes 12292
  295.6 94.5 %all-to-all-start.5 = ((bf16[32,40,1536]{2,1,0:T(8,128)(2,1)}), bf16[32,40,1536]{2,1,0:T(8,128)(2,1)}, u32[]{:S(2)}, u32[]{:S(2)}) async-start(bf16[32,40,1536]{2,1,0:T(8,128)(2,1)} %fusion), calls=%async_computation.5 | async-start | bytes 7864320 | tf_op jit(solution)/shard_map/all_to_all | solution.py:178
  390.1 13.7 %copy-start.1 = (bf16[1536,640]{1,0:T(8,128)(2,1)S(1)}, bf16[1536,640]{1,0:T(8,128)(2,1)}, u32[]{:S(2)}) copy-start(bf16[1536,640]{1,0:T(8,128)(2,1)} %param.13) | copy-start | bytes 5898244

commit v5 on v3

--- a/solution.py
+++ b/solution.py
@@ -138,6 +138,7 @@
     )
     carry = merge_block(start_carry, scores, suffix_values, visible[:, None, None, :])
     piece = lax.all_gather(prefix_cache[0], TENSOR, axis=0, tiled=True)
+    piece, carry = lax.optimization_barrier((piece, carry))
     count = piece.shape[0]
     cached_keys = piece[:, 0].reshape(count, KV_HEADS, HEAD_DIM)
     cached_values = piece[:, 1].reshape(count, KV_HEADS, HEAD_DIM)

time: 366 us -> 361 us (0.986)
  other arithmetic: 16.7 us -> 11.1 us
  waiting for transfers between devices: 143 us -> 147 us
    all_gather x1, waiting for transfers between devices: 21.8 us -> 3.8 us  [shards(): piece = lax.all_gather(prefix_cache[0], TENSOR, axis=0, tiled=True)]
    ppermute x2, waiting for transfers between devices: 5.49 us -> 17.8 us  [from_behind(): lax.ppermute(value, axis, [(source, source + steps) for source in range(f...]
    all_to_all x1, waiting for transfers between devices: 0.01 us -> 8.44 us  [shards(): lax.all_to_all(out_spread, 'dp', 0, 0, tiled=True)]
    all_to_all x1, waiting for transfers between devices: 6.97 us -> 11.2 us  [shards(): lax.all_to_all(spread, 'dp', 0, 0, tiled=True).reshape(groups * rows, model)]
    slice x2 -> x1, local copies, waits for them, and re-layouts: 5.39 us -> 1.32 us  [shards(): cached_values = piece[:, 1].reshape(count, KV_HEADS, HEAD_DIM)]
  transfers between devices with their start and end apart: 9 -> 9, of which waited for: 7 -> 9; matrix products, arithmetic and copies ran while one was open for 14% -> 12% of each run, Pallas kernels for 0% -> 0%
where the time goes in v5:
time: 361 us; the launch traced here: 359 us
  waiting for transfers between devices  147 us (41%)
  blocking collectives  99.1 us (27%)
  local copies, waits for them, and re-layouts  40.6 us (11%)
  starting transfers between devices  24.1 us (7%)
  matrix products  22.9 us (6%)
  between operations  14.5 us (4%)
  other arithmetic  11.1 us (3%)
    all_to_all x1, blocking collectives, shards(): arrived = lax.all_to_all(outgoing, 'chip', 0, 0, tiled=True)  99.1 us
    all_to_all x1, waiting for transfers between devices, shards(): returned = lax.all_to_all(summed, 'chip', 0, 0, tiled=True)  89.2 us
    ppermute x2, waiting for transfers between devices, from_behind(): lax.ppermute(value, axis, [(source, source + steps) for source in range(f...  17.8 us
    all_to_all x1, waiting for transfers between devices, shards(): lax.all_to_all(spread, 'dp', 0, 0, tiled=True).reshape(groups * rows, model)  11.2 us
    gather x1, local copies, waits for them, and re-layouts, shards(): returned.reshape(chips * CAP, model)[target].reshape(rows, TOPK, model)  10 us
    all_to_all x1, waiting for transfers between devices, shards(): lax.all_to_all(out_spread, 'dp', 0, 0, tiled=True)  8.44 us
  transfers between devices with their start and end apart: 9, of which 9 were waited for; matrix products, arithmetic and copies ran while one was open for 12% of the time, Pallas kernels for 0%

profile of v5, /device:TPU:32, one launch (start us, length us, event | category | flops | bytes accessed | tf_op | source)
XLA Modules:
  0.0 359.1 jit_solution(16788456425131368589)
XLA Ops:
  10.9 4.5 %all-to-all-start = ((bf16[4,128,1536]{2,1,0:T(8,128)(2,1)}), bf16[4,128,1536]{2,1,0:T(8,128)(2,1)}, u32[]{:S(2)}, u32[]{:S(2)}) async-start(bf16[4,128,1536]{2,1,0:T(8,128)(2,1)} %broadcast_in_dim.59), calls=%async_computation | async-start | bytes 3145728 | tf_op jit(solution)/shard_map/all_to_all | solution.py:94
  17.4 7.0 %gather_fusion.2 = f32[1024]{0:T(1024)S(1)} fusion(f32[128,32]{0,1:T(8,128)S(1)} %fusion.62, s32[1024]{0:T(1024)S(1)} %reshape.413), kind=kCustom, calls=%fused_computation.2 | custom fusion | bytes 16384 | tf_op jit(solution)/shard_map/jit(take_along_axis)/gather | solution.py:163
  25.1 11.2 %all-to-all-done = bf16[4,128,1536]{2,1,0:T(8,128)(2,1)} async-done(((bf16[4,128,1536]{2,1,0:T(8,128)(2,1)}), bf16[4,128,1536]{2,1,0:T(8,128)(2,1)}, u32[]{:S(2)}, u32[]{:S(2)}) %all-to-all-start) | async-done | bytes 1572896 | tf_op jit(solution)/shard_map/all_to_all | solution.py:94
  36.3 3.7 %convolution_convert_fusion.2 = bf16[512,640]{1,0:T(8,128)(2,1)} fusion(bf16[512,1536]{1,0:T(8,128)(2,1)} %bitcast.7, bf16[1536,640]{1,0:T(8,128)(2,1)S(1)} %copy-done), kind=kOutput, calls=%fused_computation.31 | convolution fusion | flops 1006960640 | bytes 4194304 | tf_op jit(solution)/shard_map/dot_general | solution.py:95
  40.1 2.2 copy.51
  42.2 3.5 all-to-all-start.1
  45.8 4.3 %scatter_custom_fusion = s32[1280]{0:T(1024)S(1)} fusion(s32[1024]{0:T(1024)S(1)} %bitcast.184, s32[1024]{0:T(1024)S(1)} %reshape.423, s32[]{:T(128)} %constant.25.clone.1), kind=kCustom, calls=%fused_computation.104 | custom fusion | bytes 5124 | tf_op jit(solution)/shard_map/scatter | solution.py:166
  50.2 5.6 %all-to-all-done.1 = bf16[4,128,640]{1,2,0:T(8,128)(2,1)S(1)} async-done(((bf16[4,128,640]{1,2,0:T(8,128)(2,1)}), bf16[4,128,640]{1,2,0:T(8,128)(2,1)S(1)}, u32[]{:S(2)}, u32[]{:S(2)}) %all-to-all-start.1) | async-done | bytes 655392 | tf_op jit(solution)/shard_map/all_to_all | solution.py:96
  55.8 2.5 broadcast_in_dim.118
  58.4 4.9 %all-to-all-start.2 = ((bf16[4,384,1536]{2,1,0:T(8,128)(2,1)}), bf16[4,384,1536]{2,1,0:T(8,128)(2,1)}, u32[]{:S(2)}, u32[]{:S(2)}) async-start(bf16[4,384,1536]{2,1,0:T(8,128)(2,1)} %broadcast_in_dim.118), calls=%async_computation.2 | async-start | bytes 9437184 | tf_op jit(solution)/shard_map/all_to_all | solution.py:92
  63.5 1.9 collective-permute-start
  65.7 5.5 %collective-permute-done = bf16[1,128,2,512]{1,3,2,0:T(8,128)(2,1)S(1)} collective-permute-done((bf16[1,128,2,512]{1,3,2,0:T(8,128)(2,1)S(1)}, bf16[1,128,2,512]{1,3,2,0:T(8,128)(2,1)S(1)}, u32[]{:S(2)}, u32[]{:S(2)}) %collective-permute-start) | collective-permute-done | bytes 262176 | tf_op jit(solution)/shard_map/ppermute | solution.py:23
  71.2 4.0 %collective-permute-start.1 = (bf16[2,128,2,512]{1,3,2,0:T(8,128)(2,1)S(1)}, bf16[2,128,2,512]{1,3,2,0:T(8,128)(2,1)S(1)}, u32[]{:S(2)}, u32[]{:S(2)}) collective-permute-start(bf16[2,128,2,512]{1,3,2,0:T(8,128)(2,1)S(1)} %pad_maximum_fusion.1), channel_id=1, source_target_pairs={{0,2},{1,3},{2,4},{3,5},{4,6},{5,7},{6,8},{7,9},{8,10},{9,11},{10,... | collective-permute-start | bytes 1572872 | tf_op jit(solution)/shard_map/ppermute | solution.py:23
  75.5 12.3 %collective-permute-done.1 = bf16[2,128,2,512]{1,3,2,0:T(8,128)(2,1)S(1)} collective-permute-done((bf16[2,128,2,512]{1,3,2,0:T(8,128)(2,1)S(1)}, bf16[2,128,2,512]{1,3,2,0:T(8,128)(2,1)S(1)}, u32[]{:S(2)}, u32[]{:S(2)}) %collective-permute-start.1) | collective-permute-done | bytes 524320 | tf_op jit(solution)/shard_map/ppermute | solution.py:23
  90.1 1.5 fusion.6
  91.6 2.6 fusion.32
  94.2 3.8 %all-gather.3.cloned.1.call-done = bf16[1,512,2,512]{3,2,0,1:T(2,128)(2,1)} async-done(((bf16[1,8,2,512]{3,2,0,1:T(2,128)(2,1)}), bf16[1,512,2,512]{3,2,0,1:T(2,128)(2,1)}) %all-gather.3.cloned.1.call-update) | async-done | bytes 1048592 | tf_op jit(solution)/shard_map/all_gather | solution.py:140
  98.0 3.2 fusion.76
  106.1 1.3 fusion.39
  107.4 8.4 %all-to-all-done.2 = bf16[4,384,1536]{2,1,0:T(8,128)(2,1)} async-done(((bf16[4,384,1536]{2,1,0:T(8,128)(2,1)}), bf16[4,384,1536]{2,1,0:T(8,128)(2,1)}, u32[]{:S(2)}, u32[]{:S(2)}) %all-to-all-start.2) | async-done | bytes 4718624 | tf_op jit(solution)/shard_map/all_to_all | solution.py:92
  115.9 3.2 fusion.45
  119.4 5.4 %gather_fusion = bf16[1280,1536]{1,0:T(8,128)(2,1)} fusion(bf16[129,1536]{1,0:T(8,128)(2,1)S(1)} %concatenate.37, s32[2048]{0:T(1024)S(1)} %pad_clamp_fusion), kind=kCustom, calls=%fused_computation | custom fusion | bytes 7869440 | tf_op jit(solution)/shard_map/gather | solution.py:168
  124.8 99.1 %all_to_all.25 = bf16[32,40,1536]{2,1,0:T(8,128)(2,1)S(1)} all-to-all(bf16[32,40,1536]{2,1,0:T(8,128)(2,1)} %bitcast.161), channel_id=1, replica_groups=mesh['dp'=4,'chip'=32,'core'=2] {'chip'}, dimensions={0} | all-to-all | bytes 7864320 | tf_op jit(solution)/shard_map/all_to_all | solution.py:169
  223.9 6.8 %collective-permute-done.2 = bf16[32,40,1536]{2,1,0:T(8,128)(2,1)S(1)} collective-permute-done((bf16[32,40,1536]{2,1,0:T(8,128)(2,1)S(1)}, bf16[32,40,1536]{2,1,0:T(8,128)(2,1)S(1)}, u32[]{:S(2)}, u32[]{:S(2)}) %collective-permute-start.2) | collective-permute-done | bytes 3932192 | tf_op jit(solution)/shard_map/ppermute | solution.py:170
  230.7 2.2 fusion.17
  234.4 2.2 fusion.19
  237.8 3.2 collective-permute-done.3
  241.1 3.0 fusion
  244.0 5.1 %all-to-all-start.4 = ((bf16[32,40,1536]{2,1,0:T(8,128)(2,1)}), bf16[32,40,1536]{2,1,0:T(8,128)(2,1)}, u32[]{:S(2)}, u32[]{:S(2)}) async-start(bf16[32,40,1536]{2,1,0:T(8,128)(2,1)} %fusion), calls=%async_computation.4 | async-start | bytes 7864320 | tf_op jit(solution)/shard_map/all_to_all | solution.py:181
  249.3 89.2 %all-to-all-done.4 = bf16[32,40,1536]{2,1,0:T(8,128)(2,1)} async-done(((bf16[32,40,1536]{2,1,0:T(8,128)(2,1)}), bf16[32,40,1536]{2,1,0:T(8,128)(2,1)}, u32[]{:S(2)}, u32[]{:S(2)}) %all-to-all-start.4) | async-done | bytes 3932192 | tf_op jit(solution)/shard_map/all_to_all | solution.py:181
  338.5 10.0 %gather_fusion.1 = bf16[1024,1536]{1,0:T(8,128)(2,1)} fusion(bf16[1280,1536]{1,0:T(8,128)(2,1)} %bitcast.54, s32[1024]{0:T(1024)S(1)} %broadcast_clamp_fusion), kind=kCustom, calls=%fused_computation.1 | custom fusion | bytes 6295552 | tf_op jit(solution)/shard_map/gather | solution.py:182
  348.5 2.8 fusion.9
  (91 shorter events, 18.1 us)
Async XLA Ops:
  7.2 29.2 %copy-start = (bf16[1536,640]{1,0:T(8,128)(2,1)S(1)}, bf16[1536,640]{1,0:T(8,128)(2,1)}, u32[]{:S(2)}) copy-start(bf16[1536,640]{1,0:T(8,128)(2,1)} %param.13) | copy-start | bytes 5898244
  7.2 9.0 %copy-start.8 = (s32[1,256]{1,0:T(1,128)S(1)}, s32[1,256]{1,0:T(1,128)}, u32[]{:S(2)}) copy-start(s32[1,256]{1,0:T(1,128)} %param.16) | copy-start | bytes 3076
  7.2 9.6 %copy-start.5 = (s32[1,128,8]{1,2,0:T(8,128)S(1)}, s32[1,128,8]{1,2,0:T(8,128)}, u32[]{:S(2)}) copy-start(s32[1,128,8]{1,2,0:T(8,128)} %param.18) | copy-start | bytes 12292
  10.9 25.4 %all-to-all-start = ((bf16[4,128,1536]{2,1,0:T(8,128)(2,1)}), bf16[4,128,1536]{2,1,0:T(8,128)(2,1)}, u32[]{:S(2)}, u32[]{:S(2)}) async-start(bf16[4,128,1536]{2,1,0:T(8,128)(2,1)} %broadcast_in_dim.59), calls=%async_computation | async-start | bytes 3145728 | tf_op jit(solution)/shard_map/all_to_all | solution.py:94
  15.4 82.6 %all-gather.3.cloned.1.call-start = ((), (), s32[]{:S(2)}) async-start(), calls=%async_computation.5 | async-start | bytes 1064960 | tf_op jit(solution)/shard_map/all_gather | solution.py:140
  36.3 19.5 %copy-start.4 = (bf16[384,1536]{1,0:T(8,128)(2,1)S(1)}, bf16[384,1536]{1,0:T(8,128)(2,1)}, u32[]{:S(2)}) copy-start(bf16[384,1536]{1,0:T(8,128)(2,1)} %param.14) | copy-start | bytes 3538948
  42.2 13.6 %all-to-all-start.1 = ((bf16[4,128,640]{1,2,0:T(8,128)(2,1)}), bf16[4,128,640]{1,2,0:T(8,128)(2,1)S(1)}, u32[]{:S(2)}, u32[]{:S(2)}) async-start(bf16[4,128,640]{1,2,0:T(8,128)(2,1)} %copy.51), calls=%async_computation.1 | async-start | bytes 1310720 | tf_op jit(solution)/shard_map/all_to_all | solution.py:96
  58.4 57.5 %all-to-all-start.2 = ((bf16[4,384,1536]{2,1,0:T(8,128)(2,1)}), bf16[4,384,1536]{2,1,0:T(8,128)(2,1)}, u32[]{:S(2)}, u32[]{:S(2)}) async-start(bf16[4,384,1536]{2,1,0:T(8,128)(2,1)} %broadcast_in_dim.118), calls=%async_computation.2 | async-start | bytes 9437184 | tf_op jit(solution)/shard_map/all_to_all | solution.py:92
  63.5 7.7 %collective-permute-start = (bf16[1,128,2,512]{1,3,2,0:T(8,128)(2,1)S(1)}, bf16[1,128,2,512]{1,3,2,0:T(8,128)(2,1)S(1)}, u32[]{:S(2)}, u32[]{:S(2)}) collective-permute-start(bf16[1,128,2,512]{1,3,2,0:T(8,128)(2,1)S(1)} %maximum_bitcast_fusion), channel_id=1, source_target_pairs={{0,1},{1,2},{2,3},{3,4},{4,5},{5,6},{6,7},{7,8},{8,9},{9,10},{10,1... | collective-permute-start | bytes 786440 | tf_op jit(solution)/shard_map/ppermute | solution.py:23
  71.2 16.6 %collective-permute-start.1 = (bf16[2,128,2,512]{1,3,2,0:T(8,128)(2,1)S(1)}, bf16[2,128,2,512]{1,3,2,0:T(8,128)(2,1)S(1)}, u32[]{:S(2)}, u32[]{:S(2)}) collective-permute-start(bf16[2,128,2,512]{1,3,2,0:T(8,128)(2,1)S(1)} %pad_maximum_fusion.1), channel_id=1, source_target_pairs={{0,2},{1,3},{2,4},{3,5},{4,6},{5,7},{6,8},{7,9},{8,10},{9,11},{10,... | collective-permute-start | bytes 1572872 | tf_op jit(solution)/shard_map/ppermute | solution.py:23
  104.9 1.1 copy-start.11
  106.1 9.8 %copy-start.2 = (bf16[1,128,1536]{2,1,0:T(8,128)(2,1)S(1)}, bf16[1,128,1536]{2,1,0:T(8,128)(2,1)}, u32[]{:S(2)}) copy-start(bf16[1,128,1536]{2,1,0:T(8,128)(2,1)} %param.11) | copy-start | bytes 1179652
  107.4 11.7 %copy-start.6 = (f32[1536]{0:T(1024)S(1)}, f32[1536]{0:T(1024)}, u32[]{:S(2)}) copy-start(f32[1536]{0:T(1024)} %param.17) | copy-start | bytes 18436
  119.1 232.2 %copy-start.3 = (bf16[128,1536]{1,0:T(8,128)(2,1)}, bf16[128,1536]{1,0:T(8,128)(2,1)S(1)}, u32[]{:S(2)}) copy-start(bf16[128,1536]{1,0:T(8,128)(2,1)S(1)} %get-tuple-element.33) | copy-start | bytes 1179652
  124.8 105.9 %copy-start.9 = (bf16[1,1536,512]{2,1,0:T(8,128)(2,1)S(1)}, bf16[1,1536,512]{2,1,0:T(8,128)(2,1)}, u32[]{:S(2)}) copy-start(bf16[1,1536,512]{2,1,0:T(8,128)(2,1)} %param.20) | copy-start | bytes 4718596
  223.9 6.8 %collective-permute-start.2 = (bf16[32,40,1536]{2,1,0:T(8,128)(2,1)S(1)}, bf16[32,40,1536]{2,1,0:T(8,128)(2,1)S(1)}, u32[]{:S(2)}, u32[]{:S(2)}) collective-permute-start(bf16[32,40,1536]{2,1,0:T(8,128)(2,1)S(1)} %all_to_all.25), channel_id=1, source_target_pairs={{0,1},{1,0},{2,3},{3,2},{4,5},{5,4},{6,7},{7,6},{8,9},{9,8},{10,11... | collective-permute-start | bytes 11796488 | tf_op jit(solution)/shard_map/ppermute | solution.py:170
  230.7 2.3 copy-start.10
  234.2 6.9 %collective-permute-start.3 = (bf16[32,40,1536]{2,1,0:T(8,128)(2,1)S(1)}, bf16[32,40,1536]{2,1,0:T(8,128)(2,1)S(1)}, u32[]{:S(2)}, u32[]{:S(2)}) collective-permute-start(bf16[32,40,1536]{2,1,0:T(8,128)(2,1)S(1)} %bitcast.190), channel_id=1, source_target_pairs={{0,1},{1,0},{2,3},{3,2},{4,5},{5,4},{6,7},{7,6},{8,9},{9,8},{10,11... | collective-permute-start | bytes 11796488 | tf_op jit(solution)/shard_map/ppermute | solution.py:179
  244.0 5.1 %copy-start.7 = (f32[1,128,8]{1,2,0:T(8,128)S(1)}, f32[1,128,8]{1,2,0:T(8,128)}, u32[]{:S(2)}) copy-start(f32[1,128,8]{1,2,0:T(8,128)} %param.19) | copy-start | bytes 12292
  244.0 94.5 %all-to-all-start.4 = ((bf16[32,40,1536]{2,1,0:T(8,128)(2,1)}), bf16[32,40,1536]{2,1,0:T(8,128)(2,1)}, u32[]{:S(2)}, u32[]{:S(2)}) async-start(bf16[32,40,1536]{2,1,0:T(8,128)(2,1)} %fusion), calls=%async_computation.4 | async-start | bytes 7864320 | tf_op jit(solution)/shard_map/all_to_all | solution.py:181
  338.5 13.7 %copy-start.1 = (bf16[1536,640]{1,0:T(8,128)(2,1)S(1)}, bf16[1536,640]{1,0:T(8,128)(2,1)}, u32[]{:S(2)}) copy-start(bf16[1536,640]{1,0:T(8,128)(2,1)} %param.13) | copy-start | bytes 5898244
Sparse Core Ops, SparseCore 0:
  19.0 78.9 all-gather.2

commit v6 on v5

--- a/solution.py
+++ b/solution.py
@@ -10,6 +10,7 @@
 TOPK = 8
 SHIFTS = 2
 CAP = 40
+CHUNKS = 2
 TENSOR = ("chip", "core")
 
 
@@ -161,24 +162,28 @@
     below = (order[None, :] < order[:, None]).astype(jnp.bfloat16)
     earlier = jnp.dot(below, named.astype(jnp.bfloat16), preferred_element_type=jnp.float32)
     slots = jnp.take_along_axis(earlier, own_ids, axis=1).astype(jnp.int32).reshape(-1)
-    target = flat_ids * CAP + slots
+    part = CAP // CHUNKS
+    target = (slots // part) * (chips * part) + flat_ids * part + slots % part
     row_of = jnp.repeat(jnp.arange(rows, dtype=jnp.int32), TOPK)
     source = jnp.full((chips * CAP,), rows, jnp.int32).at[target].set(row_of)
     padded_input = jnp.concatenate([moe_input, jnp.zeros((1, model), jnp.bfloat16)], axis=0)
-    outgoing = padded_input[source].reshape(chips, CAP, model)
-    arrived = lax.all_to_all(outgoing, "chip", 0, 0, tiled=True)
-    sibling = lax.ppermute(arrived, "core", [(0, 1), (1, 0)])
+    outgoing = padded_input[source].reshape(CHUNKS, chips, part, model)
 
     def unit(block):
-        inner = jnp.dot(block.reshape(chips * CAP, model), expert_in[0], preferred_element_type=jnp.float32)
+        inner = jnp.dot(block.reshape(chips * part, model), expert_in[0], preferred_element_type=jnp.float32)
         activated = (jax.nn.silu(inner[:, :unit_ff]) * inner[:, unit_ff:]).astype(jnp.bfloat16)
         produced = jnp.dot(activated, expert_out[0], preferred_element_type=jnp.float32).astype(jnp.bfloat16)
-        return produced.reshape(chips, CAP, model)
-
-    own_part = unit(arrived)
-    partner = lax.ppermute(unit(sibling), "core", [(0, 1), (1, 0)])
-    summed = (own_part.astype(jnp.float32) + partner.astype(jnp.float32)).astype(jnp.bfloat16)
-    returned = lax.all_to_all(summed, "chip", 0, 0, tiled=True)
+        return produced.reshape(chips, part, model)
+
+    pieces = []
+    for chunk in range(CHUNKS):
+        arrived = lax.all_to_all(outgoing[chunk], "chip", 0, 0, tiled=True)
+        sibling = lax.ppermute(arrived, "core", [(0, 1), (1, 0)])
+        own_part = unit(arrived)
+        partner = lax.ppermute(unit(sibling), "core", [(0, 1), (1, 0)])
+        summed = (own_part.astype(jnp.float32) + partner.astype(jnp.float32)).astype(jnp.bfloat16)
+        pieces.append(lax.all_to_all(summed, "chip", 0, 0, tiled=True))
+    returned = jnp.stack(pieces)
     picked = returned.reshape(chips * CAP, model)[target].reshape(rows, TOPK, model)
     combined = jnp.einsum("tk,tkd->td", gate_weights[0], picked.astype(jnp.float32))
     mixed = (hidden_state.astype(jnp.float32) + combined).astype(jnp.bfloat16)

time: 361 us -> 452 us (1.25); the launches traced: 359 us -> 444 us
  blocking collectives: 99.1 us -> 0 us
  local copies, waits for them, and re-layouts: 40.6 us -> 112 us
  waiting for transfers between devices: 147 us -> 204 us
  starting transfers between devices: 24.1 us -> 50.8 us
  matrix products: 22.9 us -> 38 us
  other arithmetic: 11.1 us -> 24.5 us
    all_to_all x1 -> x0, blocking collectives: 99.1 us -> none  [shards(): arrived = lax.all_to_all(outgoing, 'chip', 0, 0, tiled=True)]
    all_to_all x1 -> x4, waiting for transfers between devices: 89.2 us -> 156 us  [the longest x2 87.6 us: shards(): arrived = lax.all_to_all(outgoing[chunk], 'chip', 0, 0, tiled=True)]
    reshape x0 -> x9, local copies, waits for them, and re-layouts: none -> 37.8 us  [the longest x4 15.8 us: unit(): block.reshape(chips * part, model)]
    all_to_all x1 -> x4, starting transfers between devices: 5.08 us -> 32 us  [the longest x2 17.1 us: shards(): arrived = lax.all_to_all(outgoing[chunk], 'chip', 0, 0, tiled=True)]
    convert_element_type x0 -> x2, local copies, waits for them, and re-layouts: none -> 9.7 us  [shards(): own_part.astype(jnp.float32) + partner.astype(jnp.float32)]
    dot_general x2 -> x4, matrix products: 4.43 us -> 12.8 us  [unit(): jnp.dot(block.reshape(chips * part, model), expert_in[0], preferred_eleme...]
    convert_element_type x1 -> x2, other arithmetic: 2.96 us -> 11.3 us  [shards(): (own_part.astype(jnp.float32) + partner.astype(jnp.float32)).astype(jnp.b...]
    all_to_all x0 -> x2, local copies, waits for them, and re-layouts: none -> 7.16 us  [shards(): arrived = lax.all_to_all(outgoing[chunk], 'chip', 0, 0, tiled=True)]
  transfers between devices with their start and end apart: 9 -> 14, of which waited for: 9 -> 10; matrix products, arithmetic and copies ran while one was open for 12% -> 28% of each run, Pallas kernels for 0% -> 0%
where the time goes in v6:
time: 452 us; the launch traced here: 444 us
  waiting for transfers between devices  204 us (45%)
  local copies, waits for them, and re-layouts  112 us (25%)
  starting transfers between devices  50.8 us (11%)
  matrix products  38 us (8%)
  other arithmetic  24.5 us (5%)
  between operations  15 us (3%)
    all_to_all x2, waiting for transfers between devices, shards(): arrived = lax.all_to_all(outgoing[chunk], 'chip', 0, 0, tiled=True)  87.6 us
    all_to_all x2, waiting for transfers between devices, shards(): pieces.append(lax.all_to_all(summed, 'chip', 0, 0, tiled=True))  68.8 us
    ppermute x2, waiting for transfers between devices, from_behind(): lax.ppermute(value, axis, [(source, source + steps) for source in range(f...  17.8 us
    all_to_all x2, starting transfers between devices, shards(): arrived = lax.all_to_all(outgoing[chunk], 'chip', 0, 0, tiled=True)  17.1 us
    reshape x4, local copies, waits for them, and re-layouts, unit(): block.reshape(chips * part, model)  15.8 us
    reshape x4, local copies, waits for them, and re-layouts, unit(): return produced.reshape(chips, part, model)  15.1 us
    all_to_all x2, starting transfers between devices, shards(): pieces.append(lax.all_to_all(summed, 'chip', 0, 0, tiled=True))  14.9 us
    dot_general x4, matrix products, unit(): jnp.dot(block.reshape(chips * part, model), expert_in[0], preferred_eleme...  12.8 us
  transfers between devices with their start and end apart: 14, of which 10 were waited for; matrix products, arithmetic and copies ran while one was open for 28% of the time, Pallas kernels for 0%

profile of v6, /device:TPU:32, one launch (start us, length us, event | category | flops | bytes accessed | tf_op | source)
XLA Modules:
  0.0 444.2 jit_solution(11322354291174426987)
XLA Ops:
  10.9 4.5 %all-to-all-start = ((bf16[4,128,1536]{2,1,0:T(8,128)(2,1)}), bf16[4,128,1536]{2,1,0:T(8,128)(2,1)}, u32[]{:S(2)}, u32[]{:S(2)}) async-start(bf16[4,128,1536]{2,1,0:T(8,128)(2,1)} %broadcast_in_dim.59), calls=%async_computation | async-start | bytes 3145728 | tf_op jit(solution)/shard_map/all_to_all | solution.py:95
  17.4 7.0 %gather_fusion.2 = f32[1024]{0:T(1024)S(1)} fusion(f32[128,32]{0,1:T(8,128)S(1)} %fusion.75, s32[1024]{0:T(1024)S(1)} %reshape.472), kind=kCustom, calls=%fused_computation.2 | custom fusion | bytes 16384 | tf_op jit(solution)/shard_map/jit(take_along_axis)/gather | solution.py:164
  25.1 11.2 %all-to-all-done = bf16[4,128,1536]{2,1,0:T(8,128)(2,1)} async-done(((bf16[4,128,1536]{2,1,0:T(8,128)(2,1)}), bf16[4,128,1536]{2,1,0:T(8,128)(2,1)}, u32[]{:S(2)}, u32[]{:S(2)}) %all-to-all-start) | async-done | bytes 1572896 | tf_op jit(solution)/shard_map/all_to_all | solution.py:95
  45.9 4.3 scatter_custom_fusion
  50.3 5.6 %all-to-all-done.1 = bf16[4,128,640]{1,2,0:T(8,128)(2,1)S(1)} async-done(((bf16[4,128,640]{1,2,0:T(8,128)(2,1)}), bf16[4,128,640]{1,2,0:T(8,128)(2,1)S(1)}, u32[]{:S(2)}, u32[]{:S(2)}) %all-to-all-start.1) | async-done | bytes 655392 | tf_op jit(solution)/shard_map/all_to_all | solution.py:97
  58.5 5.0 %all-to-all-start.2 = ((bf16[4,384,1536]{2,1,0:T(8,128)(2,1)}), bf16[4,384,1536]{2,1,0:T(8,128)(2,1)}, u32[]{:S(2)}, u32[]{:S(2)}) async-start(bf16[4,384,1536]{2,1,0:T(8,128)(2,1)} %broadcast_in_dim.118), calls=%async_computation.2 | async-start | bytes 9437184 | tf_op jit(solution)/shard_map/all_to_all | solution.py:93
  65.9 5.5 %collective-permute-done = bf16[1,128,2,512]{1,3,2,0:T(8,128)(2,1)S(1)} collective-permute-done((bf16[1,128,2,512]{1,3,2,0:T(8,128)(2,1)S(1)}, bf16[1,128,2,512]{1,3,2,0:T(8,128)(2,1)S(1)}, u32[]{:S(2)}, u32[]{:S(2)}) %collective-permute-start) | collective-permute-done | bytes 262176 | tf_op jit(solution)/shard_map/ppermute | solution.py:24
  71.4 4.0 collective-permute-start.1
  75.7 12.3 %collective-permute-done.1 = bf16[2,128,2,512]{1,3,2,0:T(8,128)(2,1)S(1)} collective-permute-done((bf16[2,128,2,512]{1,3,2,0:T(8,128)(2,1)S(1)}, bf16[2,128,2,512]{1,3,2,0:T(8,128)(2,1)S(1)}, u32[]{:S(2)}, u32[]{:S(2)}) %collective-permute-start.1) | collective-permute-done | bytes 524320 | tf_op jit(solution)/shard_map/ppermute | solution.py:24
  107.5 8.6 %all-to-all-done.2 = bf16[4,384,1536]{2,1,0:T(8,128)(2,1)} async-done(((bf16[4,384,1536]{2,1,0:T(8,128)(2,1)}), bf16[4,384,1536]{2,1,0:T(8,128)(2,1)}, u32[]{:S(2)}, u32[]{:S(2)}) %all-to-all-start.2) | async-done | bytes 4718624 | tf_op jit(solution)/shard_map/all_to_all | solution.py:93
  119.6 5.5 %gather_fusion = bf16[1280,1536]{1,0:T(8,128)(2,1)} fusion(bf16[129,1536]{1,0:T(8,128)(2,1)S(1)} %concatenate.37, s32[2048]{0:T(1024)S(1)} %pad_clamp_fusion), kind=kCustom, calls=%fused_computation | custom fusion | bytes 7869440 | tf_op jit(solution)/shard_map/gather | solution.py:170
  132.7 11.4 %all-to-all-start.3 = ((bf16[32,20,1536]{2,1,0:T(8,128)(2,1)}), bf16[32,20,1536]{2,1,0:T(8,128)(2,1)}, u32[]{:S(2)}, u32[]{:S(2)}) async-start(bf16[32,20,1536]{2,1,0:T(8,128)(2,1)} %squeeze.34), calls=%async_computation.3 | async-start | bytes 4718592 | tf_op jit(solution)/shard_map/all_to_all | solution.py:180
  146.2 51.1 %all-to-all-done.3 = bf16[32,20,1536]{2,1,0:T(8,128)(2,1)} async-done(((bf16[32,20,1536]{2,1,0:T(8,128)(2,1)}), bf16[32,20,1536]{2,1,0:T(8,128)(2,1)}, u32[]{:S(2)}, u32[]{:S(2)}) %all-to-all-start.3) | async-done | bytes 1966112 | tf_op jit(solution)/shard_map/all_to_all | solution.py:180
  201.0 5.6 %all-to-all-start.5 = ((bf16[32,20,1536]{2,1,0:T(8,128)(2,1)}), bf16[32,20,1536]{2,1,0:T(8,128)(2,1)}, u32[]{:S(2)}, u32[]{:S(2)}) async-start(bf16[32,20,1536]{2,1,0:T(8,128)(2,1)} %squeeze.37), calls=%async_computation.5 | async-start | bytes 4718592 | tf_op jit(solution)/shard_map/all_to_all | solution.py:180
  218.4 4.0 reshape.447
  225.9 36.5 %all-to-all-done.5 = bf16[32,20,1536]{2,1,0:T(8,128)(2,1)} async-done(((bf16[32,20,1536]{2,1,0:T(8,128)(2,1)}), bf16[32,20,1536]{2,1,0:T(8,128)(2,1)}, u32[]{:S(2)}, u32[]{:S(2)}) %all-to-all-start.5) | async-done | bytes 1966112 | tf_op jit(solution)/shard_map/all_to_all | solution.py:180
  266.0 4.0 reshape.445
  275.8 4.8 %reshape.454 = f32[32,20,1536]{2,1,0:T(8,128)} reshape(f32[640,1536]{1,0:T(8,128)} %fusion.7) | data formatting | bytes 7864320 | tf_op jit(solution)/shard_map/convert_element_type | solution.py:184
  280.6 5.7 %add_convert_fusion.1 = bf16[32,20,1536]{2,1,0:T(8,128)(2,1)} fusion(f32[32,20,1536]{2,1,0:T(8,128)} %reshape.454, bf16[32,20,1536]{2,0,1:T(8,128)(2,1)} %collective-permute-done.3), kind=kLoop, calls=%fused_computation.14 | loop fusion | flops 2949120 | bytes 7864320 | tf_op jit(solution)/shard_map/convert_element_type | solution.py:184
  286.2 7.7 %all-to-all-start.4 = ((bf16[32,20,1536]{2,1,0:T(8,128)(2,1)}), bf16[32,20,1536]{2,1,0:T(8,128)(2,1)}, u32[]{:S(2)}, u32[]{:S(2)}) async-start(bf16[32,20,1536]{2,1,0:T(8,128)(2,1)} %add_convert_fusion.1), calls=%async_computation.4 | async-start | bytes 4718592 | tf_op jit(solution)/shard_map/all_to_all | solution.py:185
  294.0 4.1 copy.74
  298.1 4.0 reshape.449
  307.3 4.0 reshape.450
  314.9 4.0 reshape.448
  324.6 4.9 %reshape.455 = f32[32,20,1536]{2,1,0:T(8,128)} reshape(f32[640,1536]{1,0:T(8,128)} %fusion.6) | data formatting | bytes 7864320 | tf_op jit(solution)/shard_map/convert_element_type | solution.py:184
  329.4 5.6 %add_convert_fusion = bf16[32,20,1536]{2,1,0:T(8,128)(2,1)} fusion(f32[32,20,1536]{2,1,0:T(8,128)} %reshape.455, bf16[32,20,1536]{2,0,1:T(8,128)(2,1)} %collective-permute-done.5), kind=kLoop, calls=%fused_computation.13 | loop fusion | flops 2949120 | bytes 7864320 | tf_op jit(solution)/shard_map/convert_element_type | solution.py:184
  335.1 14.5 %all-to-all-done.4 = bf16[32,20,1536]{2,1,0:T(8,128)(2,1)} async-done(((bf16[32,20,1536]{2,1,0:T(8,128)(2,1)}), bf16[32,20,1536]{2,1,0:T(8,128)(2,1)}, u32[]{:S(2)}, u32[]{:S(2)}) %all-to-all-start.4) | async-done | bytes 1966112 | tf_op jit(solution)/shard_map/all_to_all | solution.py:185
  349.5 7.2 %all-to-all-start.6 = ((bf16[32,20,1536]{2,1,0:T(8,128)(2,1)}), bf16[32,20,1536]{2,1,0:T(8,128)(2,1)}, u32[]{:S(2)}, u32[]{:S(2)}) async-start(bf16[32,20,1536]{2,1,0:T(8,128)(2,1)} %add_convert_fusion), calls=%async_computation.6 | async-start | bytes 4718592 | tf_op jit(solution)/shard_map/all_to_all | solution.py:185
  356.9 54.3 %all-to-all-done.6 = bf16[32,20,1536]{2,1,0:T(8,128)(2,1)} async-done(((bf16[32,20,1536]{2,1,0:T(8,128)(2,1)}), bf16[32,20,1536]{2,1,0:T(8,128)(2,1)}, u32[]{:S(2)}, u32[]{:S(2)}) %all-to-all-start.6) | async-done | bytes 1966112 | tf_op jit(solution)/shard_map/all_to_all | solution.py:185
  411.3 5.1 %pad_maximum_fusion = bf16[2,32,20,1536]{3,2,1,0:T(8,128)(2,1)} fusion(bf16[1,32,20,1536]{3,2,1,0:T(8,128)(2,1)} %bitcast.50, bf16[1,32,20,1536]{3,2,1,0:T(8,128)(2,1)} %bitcast.49), kind=kLoop, calls=%fused_computation.12 | loop fusion | flops 1966080 | bytes 7864320 | tf_op jit(solution)/shard_map/stack | solution.py:186
  416.3 6.9 %reshape.451 = bf16[1280,1536]{1,0:T(8,128)(2,1)} reshape(bf16[2,32,20,1536]{3,2,1,0:T(8,128)(2,1)} %pad_maximum_fusion) | data formatting | bytes 7864320 | tf_op jit(solution)/shard_map/reshape | solution.py:187
  423.2 10.0 %gather_fusion.1 = bf16[1024,1536]{1,0:T(8,128)(2,1)} fusion(bf16[1280,1536]{1,0:T(8,128)(2,1)} %reshape.451, s32[1024]{0:T(1024)S(1)} %broadcast_clamp_fusion), kind=kCustom, calls=%fused_computation.1 | custom fusion | bytes 6295552 | tf_op jit(solution)/shard_map/gather | solution.py:187
  (122 shorter events, 100.5 us)
Async XLA Ops:
  7.2 29.2 %copy-start = (bf16[1536,640]{1,0:T(8,128)(2,1)S(1)}, bf16[1536,640]{1,0:T(8,128)(2,1)}, u32[]{:S(2)}) copy-start(bf16[1536,640]{1,0:T(8,128)(2,1)} %param.13) | copy-start | bytes 5898244
  9.7 6.5 %copy-start.9 = (s32[1,256]{1,0:T(1,128)S(1)}, s32[1,256]{1,0:T(1,128)}, u32[]{:S(2)}) copy-start(s32[1,256]{1,0:T(1,128)} %param.16) | copy-start | bytes 3076
  9.7 7.1 %copy-start.6 = (s32[1,128,8]{1,2,0:T(8,128)S(1)}, s32[1,128,8]{1,2,0:T(8,128)}, u32[]{:S(2)}) copy-start(s32[1,128,8]{1,2,0:T(8,128)} %param.18) | copy-start | bytes 12292
  10.9 25.4 %all-to-all-start = ((bf16[4,128,1536]{2,1,0:T(8,128)(2,1)}), bf16[4,128,1536]{2,1,0:T(8,128)(2,1)}, u32[]{:S(2)}, u32[]{:S(2)}) async-start(bf16[4,128,1536]{2,1,0:T(8,128)(2,1)} %broadcast_in_dim.59), calls=%async_computation | async-start | bytes 3145728 | tf_op jit(solution)/shard_map/all_to_all | solution.py:95
  15.4 82.5 %all-gather.3.cloned.1.call-start = ((), (), s32[]{:S(2)}) async-start(), calls=%async_computation.7 | async-start | bytes 1064960 | tf_op jit(solution)/shard_map/all_gather | solution.py:141
  40.0 15.9 %copy-start.5 = (bf16[384,1536]{1,0:T(8,128)(2,1)S(1)}, bf16[384,1536]{1,0:T(8,128)(2,1)}, u32[]{:S(2)}) copy-start(bf16[384,1536]{1,0:T(8,128)(2,1)} %param.14) | copy-start | bytes 3538948
  42.3 13.6 %all-to-all-start.1 = ((bf16[4,128,640]{1,2,0:T(8,128)(2,1)}), bf16[4,128,640]{1,2,0:T(8,128)(2,1)S(1)}, u32[]{:S(2)}, u32[]{:S(2)}) async-start(bf16[4,128,640]{1,2,0:T(8,128)(2,1)} %copy.59), calls=%async_computation.1 | async-start | bytes 1310720 | tf_op jit(solution)/shard_map/all_to_all | solution.py:97
  58.5 57.6 %all-to-all-start.2 = ((bf16[4,384,1536]{2,1,0:T(8,128)(2,1)}), bf16[4,384,1536]{2,1,0:T(8,128)(2,1)}, u32[]{:S(2)}, u32[]{:S(2)}) async-start(bf16[4,384,1536]{2,1,0:T(8,128)(2,1)} %broadcast_in_dim.118), calls=%async_computation.2 | async-start | bytes 9437184 | tf_op jit(solution)/shard_map/all_to_all | solution.py:93
  63.7 7.7 %collective-permute-start = (bf16[1,128,2,512]{1,3,2,0:T(8,128)(2,1)S(1)}, bf16[1,128,2,512]{1,3,2,0:T(8,128)(2,1)S(1)}, u32[]{:S(2)}, u32[]{:S(2)}) collective-permute-start(bf16[1,128,2,512]{1,3,2,0:T(8,128)(2,1)S(1)} %maximum_bitcast_fusion), channel_id=1, source_target_pairs={{0,1},{1,2},{2,3},{3,4},{4,5},{5,6},{6,7},{7,8},{8,9},{9,10},{10,1... | collective-permute-start | bytes 786440 | tf_op jit(solution)/shard_map/ppermute | solution.py:24
  71.4 16.6 %collective-permute-start.1 = (bf16[2,128,2,512]{1,3,2,0:T(8,128)(2,1)S(1)}, bf16[2,128,2,512]{1,3,2,0:T(8,128)(2,1)S(1)}, u32[]{:S(2)}, u32[]{:S(2)}) collective-permute-start(bf16[2,128,2,512]{1,3,2,0:T(8,128)(2,1)S(1)} %pad_maximum_fusion.2), channel_id=1, source_target_pairs={{0,2},{1,3},{2,4},{3,5},{4,6},{5,7},{6,8},{7,9},{8,10},{9,11},{10,... | collective-permute-start | bytes 1572872 | tf_op jit(solution)/shard_map/ppermute | solution.py:24
  105.0 1.1 copy-start.10
  106.2 9.9 %copy-start.2 = (bf16[1,128,1536]{2,1,0:T(8,128)(2,1)S(1)}, bf16[1,128,1536]{2,1,0:T(8,128)(2,1)}, u32[]{:S(2)}) copy-start(bf16[1,128,1536]{2,1,0:T(8,128)(2,1)} %param.11) | copy-start | bytes 1179652
  116.1 3.3 copy-start.7
  119.4 316.7 %copy-start.3 = (bf16[128,1536]{1,0:T(8,128)(2,1)}, bf16[128,1536]{1,0:T(8,128)(2,1)S(1)}, u32[]{:S(2)}) copy-start(bf16[128,1536]{1,0:T(8,128)(2,1)S(1)} %get-tuple-element.35) | copy-start | bytes 1179652
  132.7 64.7 %all-to-all-start.3 = ((bf16[32,20,1536]{2,1,0:T(8,128)(2,1)}), bf16[32,20,1536]{2,1,0:T(8,128)(2,1)}, u32[]{:S(2)}, u32[]{:S(2)}) async-start(bf16[32,20,1536]{2,1,0:T(8,128)(2,1)} %squeeze.34), calls=%async_computation.3 | async-start | bytes 4718592 | tf_op jit(solution)/shard_map/all_to_all | solution.py:180
  201.0 5.6 %collective-permute-start.2 = (bf16[32,20,1536]{2,0,1:T(8,128)(2,1)}, bf16[32,20,1536]{2,0,1:T(8,128)(2,1)S(1)}, u32[]{:S(2)}, u32[]{:S(2)}) collective-permute-start(bf16[32,20,1536]{2,0,1:T(8,128)(2,1)} %copy.69), channel_id=1, source_target_pairs={{0,1},{1,0},{2,3},{3,2},{4,5},{5,4},{6,7},{7,6},{8,9},{9,8},{10,11... | collective-permute-start | bytes 5898248 | tf_op jit(solution)/shard_map/ppermute | solution.py:181
  201.0 61.4 %all-to-all-start.5 = ((bf16[32,20,1536]{2,1,0:T(8,128)(2,1)}), bf16[32,20,1536]{2,1,0:T(8,128)(2,1)}, u32[]{:S(2)}, u32[]{:S(2)}) async-start(bf16[32,20,1536]{2,1,0:T(8,128)(2,1)} %squeeze.37), calls=%async_computation.5 | async-start | bytes 4718592 | tf_op jit(solution)/shard_map/all_to_all | solution.py:180
  213.1 3.3 copy-start.4
  225.9 54.7 %collective-permute-start.3 = (bf16[32,20,1536]{2,0,1:T(8,128)(2,1)}, bf16[32,20,1536]{2,0,1:T(8,128)(2,1)}, u32[]{:S(2)}, u32[]{:S(2)}) collective-permute-start(bf16[32,20,1536]{2,0,1:T(8,128)(2,1)} %copy.71), channel_id=1, source_target_pairs={{0,1},{1,0},{2,3},{3,2},{4,5},{5,4},{6,7},{7,6},{8,9},{9,8},{10,11... | collective-permute-start | bytes 5898248 | tf_op jit(solution)/shard_map/ppermute | solution.py:183
  266.0 28.0 %collective-permute-start.4 = (bf16[32,20,1536]{2,0,1:T(8,128)(2,1)}, bf16[32,20,1536]{2,0,1:T(8,128)(2,1)}, u32[]{:S(2)}, u32[]{:S(2)}) collective-permute-start(bf16[32,20,1536]{2,0,1:T(8,128)(2,1)} %copy.73), channel_id=1, source_target_pairs={{0,1},{1,0},{2,3},{3,2},{4,5},{5,4},{6,7},{7,6},{8,9},{9,8},{10,11... | collective-permute-start | bytes 5898248 | tf_op jit(solution)/shard_map/ppermute | solution.py:181
  286.2 63.3 %all-to-all-start.4 = ((bf16[32,20,1536]{2,1,0:T(8,128)(2,1)}), bf16[32,20,1536]{2,1,0:T(8,128)(2,1)}, u32[]{:S(2)}, u32[]{:S(2)}) async-start(bf16[32,20,1536]{2,1,0:T(8,128)(2,1)} %add_convert_fusion.1), calls=%async_computation.4 | async-start | bytes 4718592 | tf_op jit(solution)/shard_map/all_to_all | solution.py:185
  314.9 14.6 %collective-permute-start.5 = (bf16[32,20,1536]{2,0,1:T(8,128)(2,1)}, bf16[32,20,1536]{2,0,1:T(8,128)(2,1)}, u32[]{:S(2)}, u32[]{:S(2)}) collective-permute-start(bf16[32,20,1536]{2,0,1:T(8,128)(2,1)} %copy.75), channel_id=1, source_target_pairs={{0,1},{1,0},{2,3},{3,2},{4,5},{5,4},{6,7},{7,6},{8,9},{9,8},{10,11... | collective-permute-start | bytes 5898248 | tf_op jit(solution)/shard_map/ppermute | solution.py:183
  335.1 21.7 %copy-start.8 = (f32[1,128,8]{1,2,0:T(8,128)S(1)}, f32[1,128,8]{1,2,0:T(8,128)}, u32[]{:S(2)}) copy-start(f32[1,128,8]{1,2,0:T(8,128)} %param.19) | copy-start | bytes 12292
  349.5 61.7 %all-to-all-start.6 = ((bf16[32,20,1536]{2,1,0:T(8,128)(2,1)}), bf16[32,20,1536]{2,1,0:T(8,128)(2,1)}, u32[]{:S(2)}, u32[]{:S(2)}) async-start(bf16[32,20,1536]{2,1,0:T(8,128)(2,1)} %add_convert_fusion), calls=%async_computation.6 | async-start | bytes 4718592 | tf_op jit(solution)/shard_map/all_to_all | solution.py:185
  423.2 13.7 %copy-start.1 = (bf16[1536,640]{1,0:T(8,128)(2,1)S(1)}, bf16[1536,640]{1,0:T(8,128)(2,1)}, u32[]{:S(2)}) copy-start(bf16[1536,640]{1,0:T(8,128)(2,1)} %param.13) | copy-start | bytes 5898244
Sparse Core Ops, SparseCore 0:
  19.0 78.8 all-gather.2

commit v7 on v5

--- a/solution.py
+++ b/solution.py
@@ -153,19 +153,17 @@
     chips = lax.axis_size("chip")
     unit_ff = expert_in.shape[2] // 2
     own_ids = expert_ids[0]
-    flat_ids = own_ids.reshape(-1)
-    named = jnp.sum(
-        (own_ids[:, :, None] == jnp.arange(EXPERTS, dtype=jnp.int32)[None, None, :]).astype(jnp.float32), axis=1
-    )
+    picks = (own_ids[:, :, None] == jnp.arange(EXPERTS, dtype=jnp.int32)[None, None, :]).astype(jnp.float32)
+    named = jnp.sum(picks, axis=1)
+    gates = jnp.sum(picks * gate_weights[0][:, :, None], axis=1)
     order = jnp.arange(rows, dtype=jnp.int32)
     below = (order[None, :] < order[:, None]).astype(jnp.bfloat16)
     earlier = jnp.dot(below, named.astype(jnp.bfloat16), preferred_element_type=jnp.float32)
-    slots = jnp.take_along_axis(earlier, own_ids, axis=1).astype(jnp.int32).reshape(-1)
-    target = flat_ids * CAP + slots
-    row_of = jnp.repeat(jnp.arange(rows, dtype=jnp.int32), TOPK)
-    source = jnp.full((chips * CAP,), rows, jnp.int32).at[target].set(row_of)
-    padded_input = jnp.concatenate([moe_input, jnp.zeros((1, model), jnp.bfloat16)], axis=0)
-    outgoing = padded_input[source].reshape(chips, CAP, model)
+    at_slot = earlier[:, :, None] == jnp.arange(CAP, dtype=jnp.float32)[None, None, :]
+    routes = jnp.where(at_slot, named[:, :, None], 0.0).reshape(rows, chips * CAP)
+    weights = jnp.where(at_slot, gates[:, :, None], 0.0).reshape(rows, chips * CAP)
+    outgoing = jnp.dot(routes.astype(jnp.bfloat16).T, moe_input, preferred_element_type=jnp.float32)
+    outgoing = outgoing.astype(jnp.bfloat16).reshape(chips, CAP, model)
     arrived = lax.all_to_all(outgoing, "chip", 0, 0, tiled=True)
     sibling = lax.ppermute(arrived, "core", [(0, 1), (1, 0)])
 
@@ -179,8 +177,12 @@
     partner = lax.ppermute(unit(sibling), "core", [(0, 1), (1, 0)])
     summed = (own_part.astype(jnp.float32) + partner.astype(jnp.float32)).astype(jnp.bfloat16)
     returned = lax.all_to_all(summed, "chip", 0, 0, tiled=True)
-    picked = returned.reshape(chips * CAP, model)[target].reshape(rows, TOPK, model)
-    combined = jnp.einsum("tk,tkd->td", gate_weights[0], picked.astype(jnp.float32))
+    returned = returned.reshape(chips * CAP, model)
+    weights_hi = weights.astype(jnp.bfloat16)
+    weights_lo = (weights - weights_hi.astype(jnp.float32)).astype(jnp.bfloat16)
+    combined = jnp.dot(weights_hi, returned, preferred_element_type=jnp.float32) + jnp.dot(
+        weights_lo, returned, preferred_element_type=jnp.float32
+    )
     mixed = (hidden_state.astype(jnp.float32) + combined).astype(jnp.bfloat16)
     return (hidden_state[None], mixed[None])
 

time: 361 us -> 342 us (0.947)
  blocking collectives: 99.1 us -> 194 us
  waiting for transfers between devices: 147 us -> 59.6 us
  local copies, waits for them, and re-layouts: 40.6 us -> 15 us
  other arithmetic: 11.1 us -> 16.4 us
  starting transfers between devices: 24.1 us -> 18.9 us
    all_to_all x0 -> x1, blocking collectives: none -> 95.4 us  [shards(): returned = lax.all_to_all(summed, 'chip', 0, 0, tiled=True)]
    all_to_all x1 -> x0, waiting for transfers between devices: 89.2 us -> none  [shards(): returned = lax.all_to_all(summed, 'chip', 0, 0, tiled=True)]
    gather x5 -> x0, local copies, waits for them, and re-layouts: 22.7 us -> none  [the longest x1 10 us: shards(): returned.reshape(chips * CAP, model)[target].reshape(rows, TOPK, model)]
    all_to_all x1 -> x0, starting transfers between devices: 5.08 us -> none  [shards(): returned = lax.all_to_all(summed, 'chip', 0, 0, tiled=True)]
    scatter x1 -> x0, local copies, waits for them, and re-layouts: 4.32 us -> none  [shards(): source = jnp.full((chips * CAP,), rows, jnp.int32).at[target].set(row_of)]
  transfers between devices with their start and end apart: 9 -> 8, of which waited for: 9 -> 8; matrix products, arithmetic and copies ran while one was open for 12% -> 11% of each run, Pallas kernels for 0% -> 0%
where the time goes in v7:
time: 342 us; the launch traced here: 341 us
  blocking collectives  194 us (57%)
  waiting for transfers between devices  59.6 us (17%)
  matrix products  22.7 us (7%)
  starting transfers between devices  18.9 us (6%)
  other arithmetic  16.4 us (5%)
  local copies, waits for them, and re-layouts  15 us (4%)
  between operations  14.5 us (4%)
    all_to_all x1, blocking collectives, shards(): arrived = lax.all_to_all(outgoing, 'chip', 0, 0, tiled=True)  98.6 us
    all_to_all x1, blocking collectives, shards(): returned = lax.all_to_all(summed, 'chip', 0, 0, tiled=True)  95.4 us
    ppermute x2, waiting for transfers between devices, from_behind(): lax.ppermute(value, axis, [(source, source + steps) for source in range(f...  17.3 us
    all_to_all x1, waiting for transfers between devices, shards(): lax.all_to_all(spread, 'dp', 0, 0, tiled=True).reshape(groups * rows, model)  12 us
    all_to_all x1, waiting for transfers between devices, shards(): lax.all_to_all(out_spread, 'dp', 0, 0, tiled=True)  7.84 us
    all_to_all x1, waiting for transfers between devices, shards(): lax.all_to_all(qkv_part.reshape(groups, rows, -1), 'dp', 0, 0, tiled=True)  7.62 us
  transfers between devices with their start and end apart: 8, of which 8 were waited for; matrix products, arithmetic and copies ran while one was open for 11% of the time, Pallas kernels for 0%

profile of v7, /device:TPU:32, one launch (start us, length us, event | category | flops | bytes accessed | tf_op | source)
XLA Modules:
  0.0 341.1 jit_solution(8560843197441047119)
XLA Ops:
  7.2 1.3 fusion.44
  11.0 4.5 %all-to-all-start = ((bf16[4,128,1536]{2,1,0:T(8,128)(2,1)}), bf16[4,128,1536]{2,1,0:T(8,128)(2,1)S(1)}, u32[]{:S(2)}, u32[]{:S(2)}) async-start(bf16[4,128,1536]{2,1,0:T(8,128)(2,1)} %broadcast_in_dim.119), calls=%async_computation | async-start | bytes 3145728 | tf_op jit(solution)/shard_map/all_to_all | solution.py:94
  18.1 1.3 select_reduce_fusion
  20.2 1.4 fusion.72
  22.8 1.3 multiply_cosine_fusion
  24.1 12.0 %all-to-all-done = bf16[4,128,1536]{2,1,0:T(8,128)(2,1)S(1)} async-done(((bf16[4,128,1536]{2,1,0:T(8,128)(2,1)}), bf16[4,128,1536]{2,1,0:T(8,128)(2,1)S(1)}, u32[]{:S(2)}, u32[]{:S(2)}) %all-to-all-start) | async-done | bytes 1572896 | tf_op jit(solution)/shard_map/all_to_all | solution.py:94
  36.1 2.2 convolution_convert_fusion.3
  38.4 2.2 copy.49
  40.5 3.5 %all-to-all-start.1 = ((bf16[4,128,640]{1,2,0:T(8,128)(2,1)}), bf16[4,128,640]{1,2,0:T(8,128)(2,1)S(1)}, u32[]{:S(2)}, u32[]{:S(2)}) async-start(bf16[4,128,640]{1,2,0:T(8,128)(2,1)} %copy.49), calls=%async_computation.1 | async-start | bytes 1310720 | tf_op jit(solution)/shard_map/all_to_all | solution.py:96
  46.4 7.6 %all-to-all-done.1 = bf16[4,128,640]{1,2,0:T(8,128)(2,1)S(1)} async-done(((bf16[4,128,640]{1,2,0:T(8,128)(2,1)}), bf16[4,128,640]{1,2,0:T(8,128)(2,1)S(1)}, u32[]{:S(2)}, u32[]{:S(2)}) %all-to-all-start.1) | async-done | bytes 655392 | tf_op jit(solution)/shard_map/all_to_all | solution.py:96
  54.0 3.8 %broadcast_in_dim.128 = bf16[4,384,1536]{2,1,0:T(8,128)(2,1)} broadcast(bf16[384,1536]{1,0:T(8,128)(2,1)} %param.14), dimensions={1,2} | broadcast | bytes 5898240 | tf_op jit(solution)/shard_map/broadcast_in_dim | solution.py:91
  57.9 5.0 %all-to-all-start.2 = ((bf16[4,384,1536]{2,1,0:T(8,128)(2,1)}), bf16[4,384,1536]{2,1,0:T(8,128)(2,1)}, u32[]{:S(2)}, u32[]{:S(2)}) async-start(bf16[4,384,1536]{2,1,0:T(8,128)(2,1)} %broadcast_in_dim.128), calls=%async_computation.2 | async-start | bytes 9437184 | tf_op jit(solution)/shard_map/all_to_all | solution.py:92
  63.0 1.9 collective-permute-start
  65.8 4.9 %collective-permute-done = bf16[1,128,2,512]{1,3,2,0:T(8,128)(2,1)S(1)} collective-permute-done((bf16[1,128,2,512]{1,3,2,0:T(8,128)(2,1)S(1)}, bf16[1,128,2,512]{1,3,2,0:T(8,128)(2,1)S(1)}, u32[]{:S(2)}, u32[]{:S(2)}) %collective-permute-start) | collective-permute-done | bytes 262176 | tf_op jit(solution)/shard_map/ppermute | solution.py:23
  70.7 3.8 %collective-permute-start.1 = (bf16[2,128,2,512]{1,3,2,0:T(8,128)(2,1)S(1)}, bf16[2,128,2,512]{1,3,2,0:T(8,128)(2,1)S(1)}, u32[]{:S(2)}, u32[]{:S(2)}) collective-permute-start(bf16[2,128,2,512]{1,3,2,0:T(8,128)(2,1)S(1)} %pad_maximum_fusion.1), channel_id=1, source_target_pairs={{0,2},{1,3},{2,4},{3,5},{4,6},{5,7},{6,8},{7,9},{8,10},{9,11},{10,... | collective-permute-start | bytes 1572872 | tf_op jit(solution)/shard_map/ppermute | solution.py:23
  74.8 12.5 %collective-permute-done.1 = bf16[2,128,2,512]{1,3,2,0:T(8,128)(2,1)S(1)} collective-permute-done((bf16[2,128,2,512]{1,3,2,0:T(8,128)(2,1)S(1)}, bf16[2,128,2,512]{1,3,2,0:T(8,128)(2,1)S(1)}, u32[]{:S(2)}, u32[]{:S(2)}) %collective-permute-start.1) | collective-permute-done | bytes 524320 | tf_op jit(solution)/shard_map/ppermute | solution.py:23
  89.8 1.5 fusion.6
  91.3 2.6 fusion.34
  93.9 4.1 %all-gather.3.cloned.1.call-done = bf16[1,512,2,512]{3,2,0,1:T(2,128)(2,1)} async-done(((bf16[1,8,2,512]{3,2,0,1:T(2,128)(2,1)}), bf16[1,512,2,512]{3,2,0,1:T(2,128)(2,1)}) %all-gather.3.cloned.1.call-update) | async-done | bytes 1048592 | tf_op jit(solution)/shard_map/all_gather | solution.py:140
  98.0 3.2 fusion.85
  101.2 1.3 copy.54
  102.6 1.3 copy.55
  106.1 1.3 fusion.41
  107.4 7.8 %all-to-all-done.2 = bf16[4,384,1536]{2,1,0:T(8,128)(2,1)} async-done(((bf16[4,384,1536]{2,1,0:T(8,128)(2,1)}), bf16[4,384,1536]{2,1,0:T(8,128)(2,1)}, u32[]{:S(2)}, u32[]{:S(2)}) %all-to-all-start.2) | async-done | bytes 4718624 | tf_op jit(solution)/shard_map/all_to_all | solution.py:92
  115.3 3.2 fusion.47
  119.9 98.6 %all_to_all.25 = bf16[32,40,1536]{2,1,0:T(8,128)(2,1)S(1)} all-to-all(bf16[32,40,1536]{2,1,0:T(8,128)(2,1)S(1)} %bitcast.168), channel_id=1, replica_groups=mesh['dp'=4,'chip'=32,'core'=2] {'chip'}, dimensions={0} | all-to-all | bytes 7864320 | tf_op jit(solution)/shard_map/all_to_all | solution.py:167
  218.4 6.8 %collective-permute-done.2 = bf16[32,40,1536]{2,1,0:T(8,128)(2,1)S(1)} collective-permute-done((bf16[32,40,1536]{2,1,0:T(8,128)(2,1)S(1)}, bf16[32,40,1536]{2,1,0:T(8,128)(2,1)S(1)}, u32[]{:S(2)}, u32[]{:S(2)}) %collective-permute-start.2) | collective-permute-done | bytes 3932192 | tf_op jit(solution)/shard_map/ppermute | solution.py:168
  225.2 2.2 fusion.19
  228.9 2.2 fusion.21
  232.4 3.2 collective-permute-done.3
  236.6 95.4 %all_to_all.26 = bf16[32,40,1536]{2,1,0:T(8,128)(2,1)S(1)} all-to-all(bf16[32,40,1536]{2,1,0:T(8,128)(2,1)S(1)} %fusion), channel_id=1, replica_groups=mesh['dp'=4,'chip'=32,'core'=2] {'chip'}, dimensions={0} | all-to-all | bytes 7864320 | tf_op jit(solution)/shard_map/all_to_all | solution.py:179
  332.8 1.5 fusion.18
  (86 shorter events, 21.1 us)
Async XLA Ops:
  7.2 29.0 %copy-start = (bf16[1536,640]{1,0:T(8,128)(2,1)S(1)}, bf16[1536,640]{1,0:T(8,128)(2,1)}, u32[]{:S(2)}) copy-start(bf16[1536,640]{1,0:T(8,128)(2,1)} %param.13) | copy-start | bytes 5898244
  7.2 10.0 %copy-start.9 = (s32[1,256]{1,0:T(1,128)S(1)}, s32[1,256]{1,0:T(1,128)}, u32[]{:S(2)}) copy-start(s32[1,256]{1,0:T(1,128)} %param.16) | copy-start | bytes 3076
  11.0 25.2 %all-to-all-start = ((bf16[4,128,1536]{2,1,0:T(8,128)(2,1)}), bf16[4,128,1536]{2,1,0:T(8,128)(2,1)S(1)}, u32[]{:S(2)}, u32[]{:S(2)}) async-start(bf16[4,128,1536]{2,1,0:T(8,128)(2,1)} %broadcast_in_dim.119), calls=%async_computation | async-start | bytes 3145728 | tf_op jit(solution)/shard_map/all_to_all | solution.py:94
  15.4 82.6 %all-gather.3.cloned.1.call-start = ((), (), s32[]{:S(2)}) async-start(), calls=%async_computation.5 | async-start | bytes 1064960 | tf_op jit(solution)/shard_map/all_gather | solution.py:140
  17.5 0.6 copy-start.7
  17.8 5.0 %copy-start.10 = (s32[128]{0:T(128)}, s32[128]{0:T(128)S(1)}, u32[]{:S(2)}) copy-start(s32[128]{0:T(128)S(1)} %iota_add_fusion) | copy-start | bytes 1540
  20.2 2.6 copy-start.5
  40.5 13.5 %all-to-all-start.1 = ((bf16[4,128,640]{1,2,0:T(8,128)(2,1)}), bf16[4,128,640]{1,2,0:T(8,128)(2,1)S(1)}, u32[]{:S(2)}, u32[]{:S(2)}) async-start(bf16[4,128,640]{1,2,0:T(8,128)(2,1)} %copy.49), calls=%async_computation.1 | async-start | bytes 1310720 | tf_op jit(solution)/shard_map/all_to_all | solution.py:96
  57.8 7.1 %copy-start.6 = (s32[256]{0:T(256)S(1)}, s32[256]{0:T(256)}, u32[]{:S(2)}) copy-start(s32[256]{0:T(256)} %copy-done.5) | copy-start | bytes 3076
  57.8 7.4 %copy-start.4 = (bf16[128,32]{0,1:T(8,128)(2,1)S(1)}, bf16[128,32]{0,1:T(8,128)(2,1)}, u32[]{:S(2)}) copy-start(bf16[128,32]{0,1:T(8,128)(2,1)} %get-tuple-element.11) | copy-start | bytes 24580
  57.8 7.7 %copy-start.11 = (s32[128]{0:T(128)S(1)}, s32[128]{0:T(128)}, u32[]{:S(2)}) copy-start(s32[128]{0:T(128)} %copy-done.10) | copy-start | bytes 1540
  57.8 7.7 %copy-start.12 = (s32[128]{0:T(128)S(1)}, s32[128]{0:T(128)}, u32[]{:S(2)}) copy-start(s32[128]{0:T(128)} %get-tuple-element.12) | copy-start | bytes 1540
  57.8 7.7 %copy-start.13 = (pred[512]{0:T(512)(128)(4,1)S(1)}, pred[512]{0:T(512)(128)(4,1)}, u32[]{:S(2)}) copy-start(pred[512]{0:T(512)(128)(4,1)} %broadcast_compare_fusion) | copy-start | bytes 1540
  57.9 57.4 %all-to-all-start.2 = ((bf16[4,384,1536]{2,1,0:T(8,128)(2,1)}), bf16[4,384,1536]{2,1,0:T(8,128)(2,1)}, u32[]{:S(2)}, u32[]{:S(2)}) async-start(bf16[4,384,1536]{2,1,0:T(8,128)(2,1)} %broadcast_in_dim.128), calls=%async_computation.2 | async-start | bytes 9437184 | tf_op jit(solution)/shard_map/all_to_all | solution.py:92
  63.0 7.7 %collective-permute-start = (bf16[1,128,2,512]{1,3,2,0:T(8,128)(2,1)S(1)}, bf16[1,128,2,512]{1,3,2,0:T(8,128)(2,1)S(1)}, u32[]{:S(2)}, u32[]{:S(2)}) collective-permute-start(bf16[1,128,2,512]{1,3,2,0:T(8,128)(2,1)S(1)} %maximum_bitcast_fusion), channel_id=1, source_target_pairs={{0,1},{1,2},{2,3},{3,4},{4,5},{5,6},{6,7},{7,8},{8,9},{9,10},{10,1... | collective-permute-start | bytes 786440 | tf_op jit(solution)/shard_map/ppermute | solution.py:23
  70.7 16.6 %collective-permute-start.1 = (bf16[2,128,2,512]{1,3,2,0:T(8,128)(2,1)S(1)}, bf16[2,128,2,512]{1,3,2,0:T(8,128)(2,1)S(1)}, u32[]{:S(2)}, u32[]{:S(2)}) collective-permute-start(bf16[2,128,2,512]{1,3,2,0:T(8,128)(2,1)S(1)} %pad_maximum_fusion.1), channel_id=1, source_target_pairs={{0,2},{1,3},{2,4},{3,5},{4,6},{5,7},{6,8},{7,9},{8,10},{9,11},{10,... | collective-permute-start | bytes 1572872 | tf_op jit(solution)/shard_map/ppermute | solution.py:23
  105.0 1.1 copy-start.16
  106.1 9.2 %copy-start.2 = (bf16[1,128,1536]{2,1,0:T(8,128)(2,1)S(1)}, bf16[1,128,1536]{2,1,0:T(8,128)(2,1)}, u32[]{:S(2)}) copy-start(bf16[1,128,1536]{2,1,0:T(8,128)(2,1)} %param.11) | copy-start | bytes 1179652
  107.4 11.1 %copy-start.8 = (f32[1536]{0:T(1024)S(1)}, f32[1536]{0:T(1024)}, u32[]{:S(2)}) copy-start(f32[1536]{0:T(1024)} %param.17) | copy-start | bytes 18436
  118.5 214.2 %copy-start.3 = (bf16[128,1536]{1,0:T(8,128)(2,1)}, bf16[128,1536]{1,0:T(8,128)(2,1)S(1)}, u32[]{:S(2)}) copy-start(bf16[128,1536]{1,0:T(8,128)(2,1)S(1)} %get-tuple-element.35) | copy-start | bytes 1179652
  119.8 105.4 %copy-start.14 = (bf16[1,1536,512]{2,1,0:T(8,128)(2,1)S(1)}, bf16[1,1536,512]{2,1,0:T(8,128)(2,1)}, u32[]{:S(2)}) copy-start(bf16[1,1536,512]{2,1,0:T(8,128)(2,1)} %param.20) | copy-start | bytes 4718596
  218.4 6.8 %collective-permute-start.2 = (bf16[32,40,1536]{2,1,0:T(8,128)(2,1)S(1)}, bf16[32,40,1536]{2,1,0:T(8,128)(2,1)S(1)}, u32[]{:S(2)}, u32[]{:S(2)}) collective-permute-start(bf16[32,40,1536]{2,1,0:T(8,128)(2,1)S(1)} %all_to_all.25), channel_id=1, source_target_pairs={{0,1},{1,0},{2,3},{3,2},{4,5},{5,4},{6,7},{7,6},{8,9},{9,8},{10,11... | collective-permute-start | bytes 11796488 | tf_op jit(solution)/shard_map/ppermute | solution.py:168
  225.2 2.2 copy-start.15
  228.7 6.9 %collective-permute-start.3 = (bf16[32,40,1536]{2,1,0:T(8,128)(2,1)S(1)}, bf16[32,40,1536]{2,1,0:T(8,128)(2,1)S(1)}, u32[]{:S(2)}, u32[]{:S(2)}) collective-permute-start(bf16[32,40,1536]{2,1,0:T(8,128)(2,1)S(1)} %bitcast.195), channel_id=1, source_target_pairs={{0,1},{1,0},{2,3},{3,2},{4,5},{5,4},{6,7},{7,6},{8,9},{9,8},{10,11... | collective-permute-start | bytes 11796488 | tf_op jit(solution)/shard_map/ppermute | solution.py:177
  332.0 2.2 copy-start.1
Sparse Core Ops, SparseCore 0:
  19.0 78.9 all-gather.2

commit v8 on v7

--- a/solution.py
+++ b/solution.py
@@ -88,8 +88,11 @@
     inputs = tokens[0]
     normed = rms_norm(inputs, attn_gain)
     groups = lax.axis_size("dp")
-    out_spread = jnp.broadcast_to(out_weight[None], (groups,) + out_weight.shape)
-    full_out = lax.all_to_all(out_spread, "dp", 0, 0, tiled=True).reshape(groups * out_weight.shape[0], -1)
+    ring = lax.axis_index("dp")
+    out_pieces = [out_weight] + [
+        lax.ppermute(out_weight, "dp", [(source, (source + step) % groups) for source in range(groups)])
+        for step in range(1, groups)
+    ]
     spread = jnp.broadcast_to(normed[None], (groups, rows, model))
     group_rows = lax.all_to_all(spread, "dp", 0, 0, tiled=True).reshape(groups * rows, model)
     qkv_part = jnp.dot(group_rows, qkv_weight, preferred_element_type=jnp.float32).astype(jnp.bfloat16)
@@ -147,7 +150,13 @@
     )
     best, total, acc = merge_block(carry, scores, cached_values, None)
     attended = (acc / total[..., None]).astype(jnp.bfloat16).reshape(rows, head_cols)
-    projected = jnp.dot(attended, full_out, preferred_element_type=jnp.float32)
+    band = out_weight.shape[0]
+    projected = None
+    for step, piece_w in enumerate(out_pieces):
+        first = ((ring - step) % groups) * band
+        part_in = lax.dynamic_slice_in_dim(attended, first, band, axis=1)
+        term = jnp.dot(part_in, piece_w, preferred_element_type=jnp.float32)
+        projected = term if projected is None else projected + term
     hidden_state = (inputs.astype(jnp.float32) + projected).astype(jnp.bfloat16)
     moe_input = rms_norm(hidden_state, ffn_gain)
     chips = lax.axis_size("chip")

time: 342 us -> 374 us (1.094)
  waiting for transfers between devices: 59.6 us -> 85.7 us
  matrix products: 22.7 us -> 27.8 us
    all_to_all x1, waiting for transfers between devices: 12 us -> 51.3 us  [shards(): lax.all_to_all(spread, 'dp', 0, 0, tiled=True).reshape(groups * rows, model)]
    all_to_all x1 -> x0, waiting for transfers between devices: 7.84 us -> none  [shards(): lax.all_to_all(out_spread, 'dp', 0, 0, tiled=True)]
    ppermute x0 -> x3, starting transfers between devices: none -> 5.3 us  [shards(): lax.ppermute(out_weight, 'dp', [(source, (source + step) % groups) for so...]
    all_to_all x1 -> x0, starting transfers between devices: 4.95 us -> none  [shards(): lax.all_to_all(out_spread, 'dp', 0, 0, tiled=True)]
    all_gather x1, waiting for transfers between devices: 4.14 us -> 0.01 us  [shards(): piece = lax.all_gather(prefix_cache[0], TENSOR, axis=0, tiled=True)]
    broadcast_in_dim x1 -> x0, local copies, waits for them, and re-layouts: 3.8 us -> none  [shards(): jnp.broadcast_to(out_weight[None], (groups,) + out_weight.shape)]
  transfers between devices with their start and end apart: 8 -> 10, of which waited for: 8 -> 6; matrix products, arithmetic and copies ran while one was open for 11% -> 12% of each run, Pallas kernels for 0% -> 0%
where the time goes in v8:
time: 374 us; the launch traced here: 373 us
  blocking collectives  196 us (52%)
  waiting for transfers between devices  85.7 us (23%)
  matrix products  27.8 us (7%)
  starting transfers between devices  18.6 us (5%)
  other arithmetic  16.3 us (4%)
  between operations  14.6 us (4%)
  local copies, waits for them, and re-layouts  14 us (4%)
    all_to_all x1, blocking collectives, shards(): arrived = lax.all_to_all(outgoing, 'chip', 0, 0, tiled=True)  100 us
    all_to_all x1, blocking collectives, shards(): returned = lax.all_to_all(summed, 'chip', 0, 0, tiled=True)  95.4 us
    all_to_all x1, waiting for transfers between devices, shards(): lax.all_to_all(spread, 'dp', 0, 0, tiled=True).reshape(groups * rows, model)  51.3 us
    ppermute x2, waiting for transfers between devices, from_behind(): lax.ppermute(value, axis, [(source, source + steps) for source in range(f...  15.7 us
    all_to_all x1, waiting for transfers between devices, shards(): lax.all_to_all(qkv_part.reshape(groups, rows, -1), 'dp', 0, 0, tiled=True)  7.96 us
  transfers between devices with their start and end apart: 10, of which 6 were waited for; matrix products, arithmetic and copies ran while one was open for 12% of the time, Pallas kernels for 0%

profile of v8, /device:TPU:32, one launch (start us, length us, event | category | flops | bytes accessed | tf_op | source)
XLA Modules:
  0.0 372.8 jit_solution(3809371762198966995)
XLA Ops:
  7.2 1.7 collective-permute-start.2
  8.8 1.7 collective-permute-start.4
  10.5 2.0 collective-permute-start.3
  16.1 3.6 all-to-all-start
  22.4 1.3 select_reduce_fusion
  24.5 1.4 fusion.74
  27.1 1.4 multiply_cosine_fusion
  28.5 51.3 %all-to-all-done = bf16[4,128,1536]{2,1,0:T(8,128)(2,1)S(1)} async-done(((bf16[4,128,1536]{2,1,0:T(8,128)(2,1)}), bf16[4,128,1536]{2,1,0:T(8,128)(2,1)S(1)}, u32[]{:S(2)}, u32[]{:S(2)}) %all-to-all-start) | async-done | bytes 1572896 | tf_op jit(solution)/shard_map/all_to_all | solution.py:97
  79.8 2.2 convolution_convert_fusion.3
  82.1 2.2 copy.49
  84.2 3.5 all-to-all-start.1
  90.0 8.0 %all-to-all-done.1 = bf16[4,128,640]{1,2,0:T(8,128)(2,1)S(1)} async-done(((bf16[4,128,640]{1,2,0:T(8,128)(2,1)}), bf16[4,128,640]{1,2,0:T(8,128)(2,1)S(1)}, u32[]{:S(2)}, u32[]{:S(2)}) %all-to-all-start.1) | async-done | bytes 655392 | tf_op jit(solution)/shard_map/all_to_all | solution.py:99
  98.2 1.9 collective-permute-start
  101.1 4.8 %collective-permute-done = bf16[1,128,2,512]{1,3,2,0:T(8,128)(2,1)S(1)} collective-permute-done((bf16[1,128,2,512]{1,3,2,0:T(8,128)(2,1)S(1)}, bf16[1,128,2,512]{1,3,2,0:T(8,128)(2,1)S(1)}, u32[]{:S(2)}, u32[]{:S(2)}) %collective-permute-start) | collective-permute-done | bytes 262176 | tf_op jit(solution)/shard_map/ppermute | solution.py:23
  105.9 4.0 %collective-permute-start.1 = (bf16[2,128,2,512]{1,3,2,0:T(8,128)(2,1)S(1)}, bf16[2,128,2,512]{1,3,2,0:T(8,128)(2,1)S(1)}, u32[]{:S(2)}, u32[]{:S(2)}) collective-permute-start(bf16[2,128,2,512]{1,3,2,0:T(8,128)(2,1)S(1)} %pad_maximum_fusion.1), channel_id=1, source_target_pairs={{0,2},{1,3},{2,4},{3,5},{4,6},{5,7},{6,8},{7,9},{8,10},{9,11},{10,... | collective-permute-start | bytes 1572872 | tf_op jit(solution)/shard_map/ppermute | solution.py:23
  110.2 11.0 %collective-permute-done.1 = bf16[2,128,2,512]{1,3,2,0:T(8,128)(2,1)S(1)} collective-permute-done((bf16[2,128,2,512]{1,3,2,0:T(8,128)(2,1)S(1)}, bf16[2,128,2,512]{1,3,2,0:T(8,128)(2,1)S(1)}, u32[]{:S(2)}, u32[]{:S(2)}) %collective-permute-start.1) | collective-permute-done | bytes 524320 | tf_op jit(solution)/shard_map/ppermute | solution.py:23
  123.4 1.5 fusion.6
  125.0 2.6 fusion.36
  127.6 3.3 fusion.97
  133.3 2.6 copy-done.2
  137.0 1.5 copy.55
  138.6 4.2 %fusion.43 = bf16[128,8,3,64]{0,3,2,1:T(8,128)(2,1)S(1)} fusion(bf16[512,8,64,1]{0,2,3,1:T(8,128)(2,1)S(1)} %bitcast.187, f32[8,512,128,3]{2,1,3,0:T(8,128)} %copy-done.2, f32[128,8,3]{0,2,1:T(4,128)S(1)} %max.3, f32[128,8,3,64]{0,3,2,1:T(8,128)S(1)} %copy-done.18, f32[128,8,3]{0,2,1:T(4,128)S(1)} %get-tuple-element.14, f32[128,8,3]{0,2,1:T(4,128)S(1)} %get-tuple-element.15), kind=kOutput, calls=%fused_computation.51 | convolution fusion | flops 206831616 | bytes 8032256 | tf_op jit(solution)/shard_map/tgrn,ngd->tgrd/dot_general | solution.py:60
  143.2 1.7 fusion.76
  144.9 1.7 convolution_add_fusion.1
  146.6 1.8 fusion.49
  149.8 100.4 %all_to_all.20 = bf16[32,40,1536]{2,1,0:T(8,128)(2,1)S(1)} all-to-all(bf16[32,40,1536]{2,1,0:T(8,128)(2,1)S(1)} %bitcast.169), channel_id=1, replica_groups=mesh['dp'=4,'chip'=32,'core'=2] {'chip'}, dimensions={0} | all-to-all | bytes 7864320 | tf_op jit(solution)/shard_map/all_to_all | solution.py:176
  250.2 6.8 %collective-permute-done.5 = bf16[32,40,1536]{2,1,0:T(8,128)(2,1)S(1)} collective-permute-done((bf16[32,40,1536]{2,1,0:T(8,128)(2,1)S(1)}, bf16[32,40,1536]{2,1,0:T(8,128)(2,1)S(1)}, u32[]{:S(2)}, u32[]{:S(2)}) %collective-permute-start.5) | collective-permute-done | bytes 3932192 | tf_op jit(solution)/shard_map/ppermute | solution.py:177
  256.9 2.2 fusion.21
  260.6 2.2 fusion.23
  264.1 3.2 collective-permute-done.6
  268.4 95.4 %all_to_all.21 = bf16[32,40,1536]{2,1,0:T(8,128)(2,1)S(1)} all-to-all(bf16[32,40,1536]{2,1,0:T(8,128)(2,1)S(1)} %fusion), channel_id=1, replica_groups=mesh['dp'=4,'chip'=32,'core'=2] {'chip'}, dimensions={0} | all-to-all | bytes 7864320 | tf_op jit(solution)/shard_map/all_to_all | solution.py:188
  364.5 1.5 fusion.20
  (96 shorter events, 23.8 us)
Async XLA Ops:
  7.2 72.7 %copy-start = (bf16[1536,640]{1,0:T(8,128)(2,1)S(1)}, bf16[1536,640]{1,0:T(8,128)(2,1)}, u32[]{:S(2)}) copy-start(bf16[1536,640]{1,0:T(8,128)(2,1)} %param.13) | copy-start | bytes 5898244
  7.2 14.3 %copy-start.11 = (s32[1,256]{1,0:T(1,128)S(1)}, s32[1,256]{1,0:T(1,128)}, u32[]{:S(2)}) copy-start(s32[1,256]{1,0:T(1,128)} %param.16) | copy-start | bytes 3076
  7.2 137.7 %collective-permute-start.2 = (bf16[384,1536]{1,0:T(8,128)(2,1)}, bf16[384,1536]{1,0:T(8,128)(2,1)}, u32[]{:S(2)}, u32[]{:S(2)}) collective-permute-start(bf16[384,1536]{1,0:T(8,128)(2,1)} %param.14), channel_id=1, source_target_pairs={{0,64},{64,128},{128,192},{192,0},{1,65},{65,129},{129,193},{193,1... | collective-permute-start | bytes 3538952 | tf_op jit(solution)/shard_map/ppermute | solution.py:93
  8.8 134.4 %collective-permute-start.4 = (bf16[384,1536]{1,0:T(8,128)(2,1)}, bf16[384,1536]{1,0:T(8,128)(2,1)}, u32[]{:S(2)}, u32[]{:S(2)}) collective-permute-start(bf16[384,1536]{1,0:T(8,128)(2,1)} %param.14), channel_id=1, source_target_pairs={{0,192},{64,0},{128,64},{192,128},{1,193},{65,1},{129,65},{193,129... | collective-permute-start | bytes 3538952 | tf_op jit(solution)/shard_map/ppermute | solution.py:93
  10.5 136.1 %collective-permute-start.3 = (bf16[384,1536]{1,0:T(8,128)(2,1)}, bf16[384,1536]{1,0:T(8,128)(2,1)}, u32[]{:S(2)}, u32[]{:S(2)}) collective-permute-start(bf16[384,1536]{1,0:T(8,128)(2,1)} %param.14), channel_id=1, source_target_pairs={{0,128},{64,192},{128,0},{192,64},{1,129},{65,193},{129,1},{193,65... | collective-permute-start | bytes 3538952 | tf_op jit(solution)/shard_map/ppermute | solution.py:93
  16.1 63.7 %all-to-all-start = ((bf16[4,128,1536]{2,1,0:T(8,128)(2,1)}), bf16[4,128,1536]{2,1,0:T(8,128)(2,1)S(1)}, u32[]{:S(2)}, u32[]{:S(2)}) async-start(bf16[4,128,1536]{2,1,0:T(8,128)(2,1)} %broadcast_in_dim.113), calls=%async_computation | async-start | bytes 3145728 | tf_op jit(solution)/shard_map/all_to_all | solution.py:97
  19.7 107.9 %all-gather.3.cloned.1.call-start = ((), (), s32[]{:S(2)}) async-start(), calls=%async_computation.4 | async-start | bytes 1064960 | tf_op jit(solution)/shard_map/all_gather | solution.py:143
  21.8 0.6 copy-start.9
  22.0 5.1 %copy-start.12 = (s32[128]{0:T(128)}, s32[128]{0:T(128)S(1)}, u32[]{:S(2)}) copy-start(s32[128]{0:T(128)S(1)} %iota_add_fusion) | copy-start | bytes 1540
  24.5 2.7 copy-start.7
  82.0 18.1 %copy-start.8 = (s32[256]{0:T(256)S(1)}, s32[256]{0:T(256)}, u32[]{:S(2)}) copy-start(s32[256]{0:T(256)} %copy-done.7) | copy-start | bytes 3076
  82.0 18.5 %copy-start.6 = (bf16[128,32]{0,1:T(8,128)(2,1)S(1)}, bf16[128,32]{0,1:T(8,128)(2,1)}, u32[]{:S(2)}) copy-start(bf16[128,32]{0,1:T(8,128)(2,1)} %get-tuple-element.11) | copy-start | bytes 24580
  82.0 18.7 %copy-start.13 = (s32[128]{0:T(128)S(1)}, s32[128]{0:T(128)}, u32[]{:S(2)}) copy-start(s32[128]{0:T(128)} %copy-done.12) | copy-start | bytes 1540
  82.0 18.8 %copy-start.14 = (s32[128]{0:T(128)S(1)}, s32[128]{0:T(128)}, u32[]{:S(2)}) copy-start(s32[128]{0:T(128)} %get-tuple-element.12) | copy-start | bytes 1540
  82.0 18.8 %copy-start.15 = (pred[512]{0:T(512)(128)(4,1)S(1)}, pred[512]{0:T(512)(128)(4,1)}, u32[]{:S(2)}) copy-start(pred[512]{0:T(512)(128)(4,1)} %broadcast_compare_fusion) | copy-start | bytes 1540
  84.2 13.8 %all-to-all-start.1 = ((bf16[4,128,640]{1,2,0:T(8,128)(2,1)}), bf16[4,128,640]{1,2,0:T(8,128)(2,1)S(1)}, u32[]{:S(2)}, u32[]{:S(2)}) async-start(bf16[4,128,640]{1,2,0:T(8,128)(2,1)} %copy.49), calls=%async_computation.1 | async-start | bytes 1310720 | tf_op jit(solution)/shard_map/all_to_all | solution.py:99
  98.2 7.7 %collective-permute-start = (bf16[1,128,2,512]{1,3,2,0:T(8,128)(2,1)S(1)}, bf16[1,128,2,512]{1,3,2,0:T(8,128)(2,1)S(1)}, u32[]{:S(2)}, u32[]{:S(2)}) collective-permute-start(bf16[1,128,2,512]{1,3,2,0:T(8,128)(2,1)S(1)} %maximum_bitcast_fusion), channel_id=1, source_target_pairs={{0,1},{1,2},{2,3},{3,4},{4,5},{5,6},{6,7},{7,8},{8,9},{9,10},{10,1... | collective-permute-start | bytes 786440 | tf_op jit(solution)/shard_map/ppermute | solution.py:23
  105.9 15.3 %collective-permute-start.1 = (bf16[2,128,2,512]{1,3,2,0:T(8,128)(2,1)S(1)}, bf16[2,128,2,512]{1,3,2,0:T(8,128)(2,1)S(1)}, u32[]{:S(2)}, u32[]{:S(2)}) collective-permute-start(bf16[2,128,2,512]{1,3,2,0:T(8,128)(2,1)S(1)} %pad_maximum_fusion.1), channel_id=1, source_target_pairs={{0,2},{1,3},{2,4},{3,5},{4,6},{5,7},{6,8},{7,9},{8,10},{9,11},{10,... | collective-permute-start | bytes 1572872 | tf_op jit(solution)/shard_map/ppermute | solution.py:23
  133.3 2.7 copy-start.2
  135.9 2.6 copy-start.18
  138.6 4.2 %copy-start.5 = (bf16[384,1536]{1,0:T(8,128)(2,1)S(1)}, bf16[384,1536]{1,0:T(8,128)(2,1)}, u32[]{:S(2)}) copy-start(bf16[384,1536]{1,0:T(8,128)(2,1)} %param.14) | copy-start | bytes 3538948
  142.8 3.8 %copy-start.3 = (bf16[1,128,1536]{2,1,0:T(8,128)(2,1)S(1)}, bf16[1,128,1536]{2,1,0:T(8,128)(2,1)}, u32[]{:S(2)}) copy-start(bf16[1,128,1536]{2,1,0:T(8,128)(2,1)} %param.11) | copy-start | bytes 1179652
  143.2 5.3 %copy-start.10 = (f32[1536]{0:T(1024)S(1)}, f32[1536]{0:T(1024)}, u32[]{:S(2)}) copy-start(f32[1536]{0:T(1024)} %param.17) | copy-start | bytes 18436
  148.4 216.0 %copy-start.4 = (bf16[128,1536]{1,0:T(8,128)(2,1)}, bf16[128,1536]{1,0:T(8,128)(2,1)S(1)}, u32[]{:S(2)}) copy-start(bf16[128,1536]{1,0:T(8,128)(2,1)S(1)} %get-tuple-element.35) | copy-start | bytes 1179652
  149.7 107.2 %copy-start.16 = (bf16[1,1536,512]{2,1,0:T(8,128)(2,1)S(1)}, bf16[1,1536,512]{2,1,0:T(8,128)(2,1)}, u32[]{:S(2)}) copy-start(bf16[1,1536,512]{2,1,0:T(8,128)(2,1)} %param.20) | copy-start | bytes 4718596
  250.1 6.8 %collective-permute-start.5 = (bf16[32,40,1536]{2,1,0:T(8,128)(2,1)S(1)}, bf16[32,40,1536]{2,1,0:T(8,128)(2,1)S(1)}, u32[]{:S(2)}, u32[]{:S(2)}) collective-permute-start(bf16[32,40,1536]{2,1,0:T(8,128)(2,1)S(1)} %all_to_all.20), channel_id=1, source_target_pairs={{0,1},{1,0},{2,3},{3,2},{4,5},{5,4},{6,7},{7,6},{8,9},{9,8},{10,11... | collective-permute-start | bytes 11796488 | tf_op jit(solution)/shard_map/ppermute | solution.py:177
  256.9 2.2 copy-start.17
  260.4 6.9 %collective-permute-start.6 = (bf16[32,40,1536]{2,1,0:T(8,128)(2,1)S(1)}, bf16[32,40,1536]{2,1,0:T(8,128)(2,1)S(1)}, u32[]{:S(2)}, u32[]{:S(2)}) collective-permute-start(bf16[32,40,1536]{2,1,0:T(8,128)(2,1)S(1)} %bitcast.199), channel_id=1, source_target_pairs={{0,1},{1,0},{2,3},{3,2},{4,5},{5,4},{6,7},{7,6},{8,9},{9,8},{10,11... | collective-permute-start | bytes 11796488 | tf_op jit(solution)/shard_map/ppermute | solution.py:186
  363.8 2.2 copy-start.1
Sparse Core Ops, SparseCore 0:
  23.3 78.7 all-gather.2

commit v9 on v7

--- a/solution.py
+++ b/solution.py
@@ -88,8 +88,6 @@
     inputs = tokens[0]
     normed = rms_norm(inputs, attn_gain)
     groups = lax.axis_size("dp")
-    out_spread = jnp.broadcast_to(out_weight[None], (groups,) + out_weight.shape)
-    full_out = lax.all_to_all(out_spread, "dp", 0, 0, tiled=True).reshape(groups * out_weight.shape[0], -1)
     spread = jnp.broadcast_to(normed[None], (groups, rows, model))
     group_rows = lax.all_to_all(spread, "dp", 0, 0, tiled=True).reshape(groups * rows, model)
     qkv_part = jnp.dot(group_rows, qkv_weight, preferred_element_type=jnp.float32).astype(jnp.bfloat16)
@@ -119,6 +117,9 @@
     for bit in range(SHIFTS):
         earlier = from_behind(window, TENSOR, 2**bit)
         window = jnp.concatenate([window, earlier], axis=0)
+    out_spread = jnp.broadcast_to(out_weight[None], (groups,) + out_weight.shape)
+    out_spread, window = lax.optimization_barrier((out_spread, window))
+    full_out = lax.all_to_all(out_spread, "dp", 0, 0, tiled=True).reshape(groups * out_weight.shape[0], -1)
     depth = window.shape[0]
     k_index = (
         (lane - jnp.arange(depth, dtype=jnp.int32))[:, None] * rows

time: 342 us -> 369 us (1.079)
  waiting for transfers between devices: 59.6 us -> 85.2 us
    all_to_all x1, waiting for transfers between devices: 7.84 us -> 32.5 us  [shards(): lax.all_to_all(out_spread, 'dp', 0, 0, tiled=True)]
  transfers between devices with their start and end apart: 8 -> 8, of which waited for: 8 -> 8; matrix products, arithmetic and copies ran while one was open for 11% -> 10% of each run, Pallas kernels for 0% -> 0%
where the time goes in v9:
time: 369 us
  blocking collectives  197 us (53%)
  waiting for transfers between devices  85.2 us (23%)
  matrix products  22.7 us (6%)
  starting transfers between devices  19 us (5%)
  other arithmetic  16.7 us (5%)
  between operations  14.5 us (4%)
  local copies, waits for them, and re-layouts  13.6 us (4%)
    all_to_all x1, blocking collectives, shards(): arrived = lax.all_to_all(outgoing, 'chip', 0, 0, tiled=True)  102 us
    all_to_all x1, blocking collectives, shards(): returned = lax.all_to_all(summed, 'chip', 0, 0, tiled=True)  95.4 us
    all_to_all x1, waiting for transfers between devices, shards(): lax.all_to_all(out_spread, 'dp', 0, 0, tiled=True)  32.5 us
    ppermute x2, waiting for transfers between devices, from_behind(): lax.ppermute(value, axis, [(source, source + steps) for source in range(f...  16.7 us
    all_to_all x1, waiting for transfers between devices, shards(): lax.all_to_all(spread, 'dp', 0, 0, tiled=True).reshape(groups * rows, model)  11.7 us
    all_to_all x1, waiting for transfers between devices, shards(): lax.all_to_all(qkv_part.reshape(groups, rows, -1), 'dp', 0, 0, tiled=True)  7.62 us
  transfers between devices with their start and end apart: 8, of which 8 were waited for; matrix products, arithmetic and copies ran while one was open for 10% of the time, Pallas kernels for 0%

profile of v9, /device:TPU:32, one launch (start us, length us, event | category | flops | bytes accessed | tf_op | source)
XLA Modules:
  0.0 368.6 jit_solution(10265982316297059977)
XLA Ops:
  7.2 1.3 fusion.44
  11.0 4.5 %all-to-all-start = ((bf16[4,128,1536]{2,1,0:T(8,128)(2,1)}), bf16[4,128,1536]{2,1,0:T(8,128)(2,1)S(1)}, u32[]{:S(2)}, u32[]{:S(2)}) async-start(bf16[4,128,1536]{2,1,0:T(8,128)(2,1)} %broadcast_in_dim.120), calls=%async_computation | async-start | bytes 3145728 | tf_op jit(solution)/shard_map/all_to_all | solution.py:92
  18.2 1.3 select_reduce_fusion
  20.3 1.4 fusion.72
  23.0 1.4 multiply_cosine_fusion
  24.4 11.7 %all-to-all-done = bf16[4,128,1536]{2,1,0:T(8,128)(2,1)S(1)} async-done(((bf16[4,128,1536]{2,1,0:T(8,128)(2,1)}), bf16[4,128,1536]{2,1,0:T(8,128)(2,1)S(1)}, u32[]{:S(2)}, u32[]{:S(2)}) %all-to-all-start) | async-done | bytes 1572896 | tf_op jit(solution)/shard_map/all_to_all | solution.py:92
  36.1 2.2 convolution_convert_fusion.3
  38.4 2.2 copy.49
  40.6 3.5 all-to-all-start.1
  46.4 7.6 %all-to-all-done.1 = bf16[4,128,640]{1,2,0:T(8,128)(2,1)S(1)} async-done(((bf16[4,128,640]{1,2,0:T(8,128)(2,1)}), bf16[4,128,640]{1,2,0:T(8,128)(2,1)S(1)}, u32[]{:S(2)}, u32[]{:S(2)}) %all-to-all-start.1) | async-done | bytes 655392 | tf_op jit(solution)/shard_map/all_to_all | solution.py:94
  54.2 1.9 collective-permute-start
  57.0 4.9 %collective-permute-done = bf16[1,128,2,512]{1,3,2,0:T(8,128)(2,1)S(1)} collective-permute-done((bf16[1,128,2,512]{1,3,2,0:T(8,128)(2,1)S(1)}, bf16[1,128,2,512]{1,3,2,0:T(8,128)(2,1)S(1)}, u32[]{:S(2)}, u32[]{:S(2)}) %collective-permute-start) | collective-permute-done | bytes 262176 | tf_op jit(solution)/shard_map/ppermute | solution.py:23
  62.0 3.8 %collective-permute-start.1 = (bf16[2,128,2,512]{1,3,2,0:T(8,128)(2,1)S(1)}, bf16[2,128,2,512]{1,3,2,0:T(8,128)(2,1)S(1)}, u32[]{:S(2)}, u32[]{:S(2)}) collective-permute-start(bf16[2,128,2,512]{1,3,2,0:T(8,128)(2,1)S(1)} %pad_maximum_fusion.1), channel_id=1, source_target_pairs={{0,2},{1,3},{2,4},{3,5},{4,6},{5,7},{6,8},{7,9},{8,10},{9,11},{10,... | collective-permute-start | bytes 1572872 | tf_op jit(solution)/shard_map/ppermute | solution.py:23
  66.1 11.9 %collective-permute-done.1 = bf16[2,128,2,512]{1,3,2,0:T(8,128)(2,1)S(1)} collective-permute-done((bf16[2,128,2,512]{1,3,2,0:T(8,128)(2,1)S(1)}, bf16[2,128,2,512]{1,3,2,0:T(8,128)(2,1)S(1)}, u32[]{:S(2)}, u32[]{:S(2)}) %collective-permute-start.1) | collective-permute-done | bytes 524320 | tf_op jit(solution)/shard_map/ppermute | solution.py:23
  78.1 2.5 broadcast_in_dim.118
  81.6 5.1 %all-to-all-start.2 = ((bf16[4,384,1536]{2,1,0:T(8,128)(2,1)}), bf16[4,384,1536]{2,1,0:T(8,128)(2,1)}, u32[]{:S(2)}, u32[]{:S(2)}) async-start(bf16[4,384,1536]{2,1,0:T(8,128)(2,1)} %broadcast_in_dim.118), calls=%async_computation.2 | async-start | bytes 9437184 | tf_op jit(solution)/shard_map/all_to_all | solution.py:122
  87.9 1.5 fusion.6
  89.4 2.6 fusion.34
  92.0 5.9 %all-gather.3.cloned.1.call-done = bf16[1,512,2,512]{3,2,0,1:T(2,128)(2,1)} async-done(((bf16[1,8,2,512]{3,2,0,1:T(2,128)(2,1)}), bf16[1,512,2,512]{3,2,0,1:T(2,128)(2,1)}) %all-gather.3.cloned.1.call-update) | async-done | bytes 1048592 | tf_op jit(solution)/shard_map/all_gather | solution.py:141
  97.9 3.2 fusion.85
  101.1 1.3 copy.54
  102.5 1.3 copy.55
  106.0 1.3 fusion.41
  107.3 32.5 %all-to-all-done.2 = bf16[4,384,1536]{2,1,0:T(8,128)(2,1)} async-done(((bf16[4,384,1536]{2,1,0:T(8,128)(2,1)}), bf16[4,384,1536]{2,1,0:T(8,128)(2,1)}, u32[]{:S(2)}, u32[]{:S(2)}) %all-to-all-start.2) | async-done | bytes 4718624 | tf_op jit(solution)/shard_map/all_to_all | solution.py:122
  139.8 3.2 fusion.47
  144.4 101.5 %all_to_all.25 = bf16[32,40,1536]{2,1,0:T(8,128)(2,1)S(1)} all-to-all(bf16[32,40,1536]{2,1,0:T(8,128)(2,1)S(1)} %bitcast.168), channel_id=1, replica_groups=mesh['dp'=4,'chip'=32,'core'=2] {'chip'}, dimensions={0} | all-to-all | bytes 7864320 | tf_op jit(solution)/shard_map/all_to_all | solution.py:168
  245.9 6.8 %collective-permute-done.2 = bf16[32,40,1536]{2,1,0:T(8,128)(2,1)S(1)} collective-permute-done((bf16[32,40,1536]{2,1,0:T(8,128)(2,1)S(1)}, bf16[32,40,1536]{2,1,0:T(8,128)(2,1)S(1)}, u32[]{:S(2)}, u32[]{:S(2)}) %collective-permute-start.2) | collective-permute-done | bytes 3932192 | tf_op jit(solution)/shard_map/ppermute | solution.py:169
  252.7 2.2 fusion.19
  256.4 2.2 fusion.21
  259.9 3.2 collective-permute-done.3
  264.1 95.4 %all_to_all.26 = bf16[32,40,1536]{2,1,0:T(8,128)(2,1)S(1)} all-to-all(bf16[32,40,1536]{2,1,0:T(8,128)(2,1)S(1)} %fusion), channel_id=1, replica_groups=mesh['dp'=4,'chip'=32,'core'=2] {'chip'}, dimensions={0} | all-to-all | bytes 7864320 | tf_op jit(solution)/shard_map/all_to_all | solution.py:180
  360.2 1.5 fusion.18
  (88 shorter events, 21.0 us)
Async XLA Ops:
  7.2 29.0 %copy-start = (bf16[1536,640]{1,0:T(8,128)(2,1)S(1)}, bf16[1536,640]{1,0:T(8,128)(2,1)}, u32[]{:S(2)}) copy-start(bf16[1536,640]{1,0:T(8,128)(2,1)} %param.13) | copy-start | bytes 5898244
  7.2 10.1 %copy-start.10 = (s32[1,256]{1,0:T(1,128)S(1)}, s32[1,256]{1,0:T(1,128)}, u32[]{:S(2)}) copy-start(s32[1,256]{1,0:T(1,128)} %param.16) | copy-start | bytes 3076
  11.0 25.2 %all-to-all-start = ((bf16[4,128,1536]{2,1,0:T(8,128)(2,1)}), bf16[4,128,1536]{2,1,0:T(8,128)(2,1)S(1)}, u32[]{:S(2)}, u32[]{:S(2)}) async-start(bf16[4,128,1536]{2,1,0:T(8,128)(2,1)} %broadcast_in_dim.120), calls=%async_computation | async-start | bytes 3145728 | tf_op jit(solution)/shard_map/all_to_all | solution.py:92
  15.4 82.5 %all-gather.3.cloned.1.call-start = ((), (), s32[]{:S(2)}) async-start(), calls=%async_computation.5 | async-start | bytes 1064960 | tf_op jit(solution)/shard_map/all_gather | solution.py:141
  17.6 0.6 copy-start.8
  17.9 5.1 %copy-start.11 = (s32[128]{0:T(128)}, s32[128]{0:T(128)S(1)}, u32[]{:S(2)}) copy-start(s32[128]{0:T(128)S(1)} %iota_add_fusion) | copy-start | bytes 1540
  20.3 2.7 copy-start.6
  38.4 17.8 %copy-start.7 = (s32[256]{0:T(256)S(1)}, s32[256]{0:T(256)}, u32[]{:S(2)}) copy-start(s32[256]{0:T(256)} %copy-done.6) | copy-start | bytes 3076
  38.4 18.1 %copy-start.5 = (bf16[128,32]{0,1:T(8,128)(2,1)S(1)}, bf16[128,32]{0,1:T(8,128)(2,1)}, u32[]{:S(2)}) copy-start(bf16[128,32]{0,1:T(8,128)(2,1)} %get-tuple-element.15) | copy-start | bytes 24580
  38.4 18.4 %copy-start.12 = (s32[128]{0:T(128)S(1)}, s32[128]{0:T(128)}, u32[]{:S(2)}) copy-start(s32[128]{0:T(128)} %copy-done.11) | copy-start | bytes 1540
  38.4 18.4 %copy-start.13 = (s32[128]{0:T(128)S(1)}, s32[128]{0:T(128)}, u32[]{:S(2)}) copy-start(s32[128]{0:T(128)} %get-tuple-element.16) | copy-start | bytes 1540
  38.4 18.4 %copy-start.14 = (pred[512]{0:T(512)(128)(4,1)S(1)}, pred[512]{0:T(512)(128)(4,1)}, u32[]{:S(2)}) copy-start(pred[512]{0:T(512)(128)(4,1)} %broadcast_compare_fusion) | copy-start | bytes 1540
  40.6 13.5 %all-to-all-start.1 = ((bf16[4,128,640]{1,2,0:T(8,128)(2,1)}), bf16[4,128,640]{1,2,0:T(8,128)(2,1)S(1)}, u32[]{:S(2)}, u32[]{:S(2)}) async-start(bf16[4,128,640]{1,2,0:T(8,128)(2,1)} %copy.49), calls=%async_computation.1 | async-start | bytes 1310720 | tf_op jit(solution)/shard_map/all_to_all | solution.py:94
  54.2 7.7 %collective-permute-start = (bf16[1,128,2,512]{1,3,2,0:T(8,128)(2,1)S(1)}, bf16[1,128,2,512]{1,3,2,0:T(8,128)(2,1)S(1)}, u32[]{:S(2)}, u32[]{:S(2)}) collective-permute-start(bf16[1,128,2,512]{1,3,2,0:T(8,128)(2,1)S(1)} %maximum_bitcast_fusion), channel_id=1, source_target_pairs={{0,1},{1,2},{2,3},{3,4},{4,5},{5,6},{6,7},{7,8},{8,9},{9,10},{10,1... | collective-permute-start | bytes 786440 | tf_op jit(solution)/shard_map/ppermute | solution.py:23
  57.0 21.0 %copy-start.4 = (bf16[384,1536]{1,0:T(8,128)(2,1)S(1)}, bf16[384,1536]{1,0:T(8,128)(2,1)}, u32[]{:S(2)}) copy-start(bf16[384,1536]{1,0:T(8,128)(2,1)} %param.14) | copy-start | bytes 3538948
  62.0 16.0 %collective-permute-start.1 = (bf16[2,128,2,512]{1,3,2,0:T(8,128)(2,1)S(1)}, bf16[2,128,2,512]{1,3,2,0:T(8,128)(2,1)S(1)}, u32[]{:S(2)}, u32[]{:S(2)}) collective-permute-start(bf16[2,128,2,512]{1,3,2,0:T(8,128)(2,1)S(1)} %pad_maximum_fusion.1), channel_id=1, source_target_pairs={{0,2},{1,3},{2,4},{3,5},{4,6},{5,7},{6,8},{7,9},{8,10},{9,11},{10,... | collective-permute-start | bytes 1572872 | tf_op jit(solution)/shard_map/ppermute | solution.py:23
  81.6 58.2 %all-to-all-start.2 = ((bf16[4,384,1536]{2,1,0:T(8,128)(2,1)}), bf16[4,384,1536]{2,1,0:T(8,128)(2,1)}, u32[]{:S(2)}, u32[]{:S(2)}) async-start(bf16[4,384,1536]{2,1,0:T(8,128)(2,1)} %broadcast_in_dim.118), calls=%async_computation.2 | async-start | bytes 9437184 | tf_op jit(solution)/shard_map/all_to_all | solution.py:122
  104.8 1.1 copy-start.17
  106.0 33.9 %copy-start.2 = (bf16[1,128,1536]{2,1,0:T(8,128)(2,1)S(1)}, bf16[1,128,1536]{2,1,0:T(8,128)(2,1)}, u32[]{:S(2)}) copy-start(bf16[1,128,1536]{2,1,0:T(8,128)(2,1)} %param.11) | copy-start | bytes 1179652
  107.3 35.8 %copy-start.9 = (f32[1536]{0:T(1024)S(1)}, f32[1536]{0:T(1024)}, u32[]{:S(2)}) copy-start(f32[1536]{0:T(1024)} %param.17) | copy-start | bytes 18436
  143.1 217.2 %copy-start.3 = (bf16[128,1536]{1,0:T(8,128)(2,1)}, bf16[128,1536]{1,0:T(8,128)(2,1)S(1)}, u32[]{:S(2)}) copy-start(bf16[128,1536]{1,0:T(8,128)(2,1)S(1)} %get-tuple-element.39) | copy-start | bytes 1179652
  144.4 108.3 %copy-start.15 = (bf16[1,1536,512]{2,1,0:T(8,128)(2,1)S(1)}, bf16[1,1536,512]{2,1,0:T(8,128)(2,1)}, u32[]{:S(2)}) copy-start(bf16[1,1536,512]{2,1,0:T(8,128)(2,1)} %param.20) | copy-start | bytes 4718596
  245.9 6.8 %collective-permute-start.2 = (bf16[32,40,1536]{2,1,0:T(8,128)(2,1)S(1)}, bf16[32,40,1536]{2,1,0:T(8,128)(2,1)S(1)}, u32[]{:S(2)}, u32[]{:S(2)}) collective-permute-start(bf16[32,40,1536]{2,1,0:T(8,128)(2,1)S(1)} %all_to_all.25), channel_id=1, source_target_pairs={{0,1},{1,0},{2,3},{3,2},{4,5},{5,4},{6,7},{7,6},{8,9},{9,8},{10,11... | collective-permute-start | bytes 11796488 | tf_op jit(solution)/shard_map/ppermute | solution.py:169
  252.7 2.2 copy-start.16
  256.2 6.9 %collective-permute-start.3 = (bf16[32,40,1536]{2,1,0:T(8,128)(2,1)S(1)}, bf16[32,40,1536]{2,1,0:T(8,128)(2,1)S(1)}, u32[]{:S(2)}, u32[]{:S(2)}) collective-permute-start(bf16[32,40,1536]{2,1,0:T(8,128)(2,1)S(1)} %bitcast.195), channel_id=1, source_target_pairs={{0,1},{1,0},{2,3},{3,2},{4,5},{5,4},{6,7},{7,6},{8,9},{9,8},{10,11... | collective-permute-start | bytes 11796488 | tf_op jit(solution)/shard_map/ppermute | solution.py:178
  359.5 2.2 copy-start.1
Sparse Core Ops, SparseCore 0:
  19.0 78.8 all-gather.2

commit v10 on v7

--- a/solution.py
+++ b/solution.py
@@ -1,6 +1,7 @@
 import jax
 import jax.numpy as jnp
 from jax import lax
+from jax.experimental import pallas as pl
 from jax.sharding import PartitionSpec as P
 
 HEADS = 24
@@ -21,6 +22,30 @@
     count = lax.axis_size(axis)
     first, last = (max(0, -steps), min(count, count - steps))
     return lax.ppermute(value, axis, [(source, source + steps) for source in range(first, last)])
+
+
+def unit_kernel(x_ref, win_ref, wout_ref, o_ref):
+    inner = jnp.dot(x_ref[...], win_ref[...], preferred_element_type=jnp.float32)
+    half = inner.shape[1] // 2
+    gate = inner[:, :half]
+    act = (gate / (1.0 + jnp.exp(-gate)) * inner[:, half:]).astype(jnp.bfloat16)
+    o_ref[...] = jnp.dot(act, wout_ref[...], preferred_element_type=jnp.float32).astype(o_ref.dtype)
+
+
+def unit_call(x, w_in, w_out, tile=320):
+    n, d = x.shape
+    f = w_in.shape[1]
+    return pl.pallas_call(
+        unit_kernel,
+        grid=(n // tile,),
+        in_specs=[
+            pl.BlockSpec((tile, d), lambda i: (i, 0)),
+            pl.BlockSpec((d, f), lambda i: (0, 0)),
+            pl.BlockSpec((f // 2, d), lambda i: (0, 0)),
+        ],
+        out_specs=pl.BlockSpec((tile, d), lambda i: (i, 0)),
+        out_shape=jax.ShapeDtypeStruct((n, d), jnp.bfloat16),
+    )(x, w_in, w_out)
 
 
 def rms_norm(x, gain):
@@ -168,9 +193,7 @@
     sibling = lax.ppermute(arrived, "core", [(0, 1), (1, 0)])
 
     def unit(block):
-        inner = jnp.dot(block.reshape(chips * CAP, model), expert_in[0], preferred_element_type=jnp.float32)
-        activated = (jax.nn.silu(inner[:, :unit_ff]) * inner[:, unit_ff:]).astype(jnp.bfloat16)
-        produced = jnp.dot(activated, expert_out[0], preferred_element_type=jnp.float32).astype(jnp.bfloat16)
+        produced = unit_call(block.reshape(chips * CAP, model), expert_in[0], expert_out[0])
         return produced.reshape(chips, CAP, model)
 
     own_part = unit(arrived)

time: 342 us -> 354 us (1.035)
  Pallas kernels: 0 us -> 15.1 us
  matrix products: 22.7 us -> 15.8 us
  local copies, waits for them, and re-layouts: 15 us -> 18.8 us
    pallas_call x0 -> x2, Pallas kernels: none -> 15.1 us  [unit_call(): pl.pallas_call(unit_kernel, grid=(n // tile,), in_specs=[pl.BlockSpec((ti...]
    dot_general x4 -> x0, matrix products: 6.92 us -> none  [the longest x2 4.47 us: unit(): jnp.dot(block.reshape(chips * CAP, model), expert_in[0], preferred_elemen...]
    unnamed x34, local copies, waits for them, and re-layouts: 0.4 us -> 4.24 us
  transfers between devices with their start and end apart: 8 -> 8, of which waited for: 8 -> 7; matrix products, arithmetic and copies ran while one was open for 11% -> 10% of each run, Pallas kernels for 0% -> 2%
where the time goes in v10:
time: 354 us; the launch traced here: 353 us
  blocking collectives  194 us (55%)
  waiting for transfers between devices  56.4 us (16%)
  other arithmetic  19.8 us (6%)
  local copies, waits for them, and re-layouts  18.8 us (5%)
  starting transfers between devices  18.8 us (5%)
  matrix products  15.8 us (4%)
  Pallas kernels  15.1 us (4%)
  between operations  14.4 us (4%)
    all_to_all x1, blocking collectives, shards(): arrived = lax.all_to_all(outgoing, 'chip', 0, 0, tiled=True)  98.4 us
    all_to_all x1, blocking collectives, shards(): returned = lax.all_to_all(summed, 'chip', 0, 0, tiled=True)  95.4 us
    ppermute x2, waiting for transfers between devices, from_behind(): lax.ppermute(value, axis, [(source, source + steps) for source in range(f...  17.3 us
    pallas_call x2, Pallas kernels, unit_call(): pl.pallas_call(unit_kernel, grid=(n // tile,), in_specs=[pl.BlockSpec((ti...  15.1 us
    all_to_all x1, waiting for transfers between devices, shards(): lax.all_to_all(spread, 'dp', 0, 0, tiled=True).reshape(groups * rows, model)  12 us
    all_to_all x1, waiting for transfers between devices, shards(): lax.all_to_all(out_spread, 'dp', 0, 0, tiled=True)  7.84 us
    all_to_all x1, waiting for transfers between devices, shards(): lax.all_to_all(qkv_part.reshape(groups, rows, -1), 'dp', 0, 0, tiled=True)  7.62 us
  transfers between devices with their start and end apart: 8, of which 7 were waited for; matrix products, arithmetic and copies ran while one was open for 10% of the time, Pallas kernels for 2%

profile of v10, /device:TPU:32, one launch (start us, length us, event | category | flops | bytes accessed | tf_op | source)
XLA Modules:
  0.0 353.0 jit_solution(2343952366245873265)
XLA Ops:
  11.0 4.5 %all-to-all-start = ((bf16[4,128,1536]{2,1,0:T(8,128)(2,1)}), bf16[4,128,1536]{2,1,0:T(8,128)(2,1)S(1)}, u32[]{:S(2)}, u32[]{:S(2)}) async-start(bf16[4,128,1536]{2,1,0:T(8,128)(2,1)} %broadcast_in_dim.119), calls=%async_computation | async-start | bytes 3145728 | tf_op jit(solution)/shard_map/all_to_all | solution.py:119
  18.1 1.3 select_reduce_fusion
  20.2 1.4 fusion.60
  22.8 1.3 multiply_cosine_fusion
  24.2 12.0 %all-to-all-done = bf16[4,128,1536]{2,1,0:T(8,128)(2,1)S(1)} async-done(((bf16[4,128,1536]{2,1,0:T(8,128)(2,1)}), bf16[4,128,1536]{2,1,0:T(8,128)(2,1)S(1)}, u32[]{:S(2)}, u32[]{:S(2)}) %all-to-all-start) | async-done | bytes 1572896 | tf_op jit(solution)/shard_map/all_to_all | solution.py:119
  36.1 2.2 convolution_convert_fusion.1
  38.4 2.2 copy.49
  40.5 3.5 all-to-all-start.1
  46.4 7.6 %all-to-all-done.1 = bf16[4,128,640]{1,2,0:T(8,128)(2,1)S(1)} async-done(((bf16[4,128,640]{1,2,0:T(8,128)(2,1)}), bf16[4,128,640]{1,2,0:T(8,128)(2,1)S(1)}, u32[]{:S(2)}, u32[]{:S(2)}) %all-to-all-start.1) | async-done | bytes 655392 | tf_op jit(solution)/shard_map/all_to_all | solution.py:121
  54.0 3.8 %broadcast_in_dim.128 = bf16[4,384,1536]{2,1,0:T(8,128)(2,1)} broadcast(bf16[384,1536]{1,0:T(8,128)(2,1)} %param.14), dimensions={1,2} | broadcast | bytes 5898240 | tf_op jit(solution)/shard_map/broadcast_in_dim | solution.py:116
  57.9 5.0 %all-to-all-start.2 = ((bf16[4,384,1536]{2,1,0:T(8,128)(2,1)}), bf16[4,384,1536]{2,1,0:T(8,128)(2,1)}, u32[]{:S(2)}, u32[]{:S(2)}) async-start(bf16[4,384,1536]{2,1,0:T(8,128)(2,1)} %broadcast_in_dim.128), calls=%async_computation.2 | async-start | bytes 9437184 | tf_op jit(solution)/shard_map/all_to_all | solution.py:117
  63.0 1.9 collective-permute-start
  65.8 4.9 %collective-permute-done = bf16[1,128,2,512]{1,3,2,0:T(8,128)(2,1)S(1)} collective-permute-done((bf16[1,128,2,512]{1,3,2,0:T(8,128)(2,1)S(1)}, bf16[1,128,2,512]{1,3,2,0:T(8,128)(2,1)S(1)}, u32[]{:S(2)}, u32[]{:S(2)}) %collective-permute-start) | collective-permute-done | bytes 262176 | tf_op jit(solution)/shard_map/ppermute | solution.py:24
  70.7 3.8 %collective-permute-start.1 = (bf16[2,128,2,512]{1,3,2,0:T(8,128)(2,1)S(1)}, bf16[2,128,2,512]{1,3,2,0:T(8,128)(2,1)S(1)}, u32[]{:S(2)}, u32[]{:S(2)}) collective-permute-start(bf16[2,128,2,512]{1,3,2,0:T(8,128)(2,1)S(1)} %pad_maximum_fusion.1), channel_id=1, source_target_pairs={{0,2},{1,3},{2,4},{3,5},{4,6},{5,7},{6,8},{7,9},{8,10},{9,11},{10,... | collective-permute-start | bytes 1572872 | tf_op jit(solution)/shard_map/ppermute | solution.py:24
  74.8 12.5 %collective-permute-done.1 = bf16[2,128,2,512]{1,3,2,0:T(8,128)(2,1)S(1)} collective-permute-done((bf16[2,128,2,512]{1,3,2,0:T(8,128)(2,1)S(1)}, bf16[2,128,2,512]{1,3,2,0:T(8,128)(2,1)S(1)}, u32[]{:S(2)}, u32[]{:S(2)}) %collective-permute-start.1) | collective-permute-done | bytes 524320 | tf_op jit(solution)/shard_map/ppermute | solution.py:24
  89.8 1.5 fusion.6
  91.3 2.6 fusion.28
  93.9 4.1 %all-gather.3.cloned.1.call-done = bf16[1,512,2,512]{3,2,0,1:T(2,128)(2,1)} async-done(((bf16[1,8,2,512]{3,2,0,1:T(2,128)(2,1)}), bf16[1,512,2,512]{3,2,0,1:T(2,128)(2,1)}) %all-gather.3.cloned.1.call-update) | async-done | bytes 1048592 | tf_op jit(solution)/shard_map/all_gather | solution.py:165
  98.0 3.2 fusion.71
  101.2 1.3 copy.54
  106.1 1.3 fusion.35
  107.4 7.8 %all-to-all-done.2 = bf16[4,384,1536]{2,1,0:T(8,128)(2,1)} async-done(((bf16[4,384,1536]{2,1,0:T(8,128)(2,1)}), bf16[4,384,1536]{2,1,0:T(8,128)(2,1)}, u32[]{:S(2)}, u32[]{:S(2)}) %all-to-all-start.2) | async-done | bytes 4718624 | tf_op jit(solution)/shard_map/all_to_all | solution.py:117
  115.3 3.2 fusion.41
  119.8 98.4 %all_to_all.25 = bf16[32,40,1536]{2,1,0:T(8,128)(2,1)S(1)} all-to-all(bf16[32,40,1536]{2,1,0:T(8,128)(2,1)S(1)} %bitcast.160), channel_id=1, replica_groups=mesh['dp'=4,'chip'=32,'core'=2] {'chip'}, dimensions={0} | all-to-all | bytes 7864320 | tf_op jit(solution)/shard_map/all_to_all | solution.py:192
  218.3 1.9 copy-done.2
  220.1 6.8 %collective-permute-done.2 = bf16[32,40,1536]{2,1,0:T(8,128)(2,1)S(1)} collective-permute-done((bf16[32,40,1536]{2,1,0:T(8,128)(2,1)S(1)}, bf16[32,40,1536]{2,1,0:T(8,128)(2,1)S(1)}, u32[]{:S(2)}, u32[]{:S(2)}) %collective-permute-start.2) | collective-permute-done | bytes 3932192 | tf_op jit(solution)/shard_map/ppermute | solution.py:193
  226.9 2.0 copy-done.3
  228.9 7.5 %shard_map.123 = bf16[1280,1536]{1,0:T(8,128)(2,1)} custom-call(bf16[1280,1536]{1,0:T(8,128)(2,1)} %bitcast.168, bf16[1536,512]{1,0:T(8,128)(2,1)} %bitcast.163, bf16[256,1536]{1,0:T(8,128)(2,1)} %bitcast.173), custom_call_target="tpu_custom_call" | custom-call | tf_op jit(solution)/shard_map/pallas_call | solution.py:38
  236.6 7.6 %shard_map.122 = bf16[1280,1536]{1,0:T(8,128)(2,1)} custom-call(bf16[1280,1536]{1,0:T(8,128)(2,1)} %bitcast.158, bf16[1536,512]{1,0:T(8,128)(2,1)} %bitcast.164, bf16[256,1536]{1,0:T(8,128)(2,1)} %bitcast.174), custom_call_target="tpu_custom_call" | custom-call | tf_op jit(solution)/shard_map/pallas_call | solution.py:38
  244.2 4.4 %fusion = bf16[32,40,1536]{2,1,0:T(8,128)(2,1)S(1)} fusion(bf16[32,40,1536]{2,1,0:T(8,128)(2,1)} %bitcast.159, bf16[32,40,1536]{2,1,0:T(8,128)(2,1)} %collective-permute-done.3), kind=kLoop, calls=%fused_computation.1 | loop fusion | flops 7864320 | bytes 11796480 | tf_op jit(solution)/shard_map/convert_element_type | solution.py:201
  248.6 95.4 %all_to_all.26 = bf16[32,40,1536]{2,1,0:T(8,128)(2,1)S(1)} all-to-all(bf16[32,40,1536]{2,1,0:T(8,128)(2,1)S(1)} %fusion), channel_id=1, replica_groups=mesh['dp'=4,'chip'=32,'core'=2] {'chip'}, dimensions={0} | all-to-all | bytes 7864320 | tf_op jit(solution)/shard_map/all_to_all | solution.py:202
  344.7 1.5 fusion.18
  (84 shorter events, 20.1 us)
Async XLA Ops:
  7.2 29.0 %copy-start = (bf16[1536,640]{1,0:T(8,128)(2,1)S(1)}, bf16[1536,640]{1,0:T(8,128)(2,1)}, u32[]{:S(2)}) copy-start(bf16[1536,640]{1,0:T(8,128)(2,1)} %param.13) | copy-start | bytes 5898244
  7.2 10.0 %copy-start.11 = (s32[1,256]{1,0:T(1,128)S(1)}, s32[1,256]{1,0:T(1,128)}, u32[]{:S(2)}) copy-start(s32[1,256]{1,0:T(1,128)} %param.16) | copy-start | bytes 3076
  11.0 25.2 %all-to-all-start = ((bf16[4,128,1536]{2,1,0:T(8,128)(2,1)}), bf16[4,128,1536]{2,1,0:T(8,128)(2,1)S(1)}, u32[]{:S(2)}, u32[]{:S(2)}) async-start(bf16[4,128,1536]{2,1,0:T(8,128)(2,1)} %broadcast_in_dim.119), calls=%async_computation | async-start | bytes 3145728 | tf_op jit(solution)/shard_map/all_to_all | solution.py:119
  15.4 82.6 %all-gather.3.cloned.1.call-start = ((), (), s32[]{:S(2)}) async-start(), calls=%async_computation.5 | async-start | bytes 1064960 | tf_op jit(solution)/shard_map/all_gather | solution.py:165
  17.5 0.6 copy-start.9
  17.8 5.1 %copy-start.12 = (s32[128]{0:T(128)}, s32[128]{0:T(128)S(1)}, u32[]{:S(2)}) copy-start(s32[128]{0:T(128)S(1)} %iota_add_fusion) | copy-start | bytes 1540
  20.2 2.6 copy-start.7
  40.5 13.5 %all-to-all-start.1 = ((bf16[4,128,640]{1,2,0:T(8,128)(2,1)}), bf16[4,128,640]{1,2,0:T(8,128)(2,1)S(1)}, u32[]{:S(2)}, u32[]{:S(2)}) async-start(bf16[4,128,640]{1,2,0:T(8,128)(2,1)} %copy.49), calls=%async_computation.1 | async-start | bytes 1310720 | tf_op jit(solution)/shard_map/all_to_all | solution.py:121
  57.8 7.1 %copy-start.8 = (s32[256]{0:T(256)S(1)}, s32[256]{0:T(256)}, u32[]{:S(2)}) copy-start(s32[256]{0:T(256)} %copy-done.7) | copy-start | bytes 3076
  57.8 7.4 %copy-start.6 = (bf16[128,32]{0,1:T(8,128)(2,1)S(1)}, bf16[128,32]{0,1:T(8,128)(2,1)}, u32[]{:S(2)}) copy-start(bf16[128,32]{0,1:T(8,128)(2,1)} %get-tuple-element.11) | copy-start | bytes 24580
  57.8 7.7 %copy-start.13 = (s32[128]{0:T(128)S(1)}, s32[128]{0:T(128)}, u32[]{:S(2)}) copy-start(s32[128]{0:T(128)} %copy-done.12) | copy-start | bytes 1540
  57.8 7.7 %copy-start.14 = (s32[128]{0:T(128)S(1)}, s32[128]{0:T(128)}, u32[]{:S(2)}) copy-start(s32[128]{0:T(128)} %get-tuple-element.12) | copy-start | bytes 1540
  57.8 7.7 %copy-start.15 = (pred[512]{0:T(512)(128)(4,1)S(1)}, pred[512]{0:T(512)(128)(4,1)}, u32[]{:S(2)}) copy-start(pred[512]{0:T(512)(128)(4,1)} %broadcast_compare_fusion) | copy-start | bytes 1540
  57.9 57.4 %all-to-all-start.2 = ((bf16[4,384,1536]{2,1,0:T(8,128)(2,1)}), bf16[4,384,1536]{2,1,0:T(8,128)(2,1)}, u32[]{:S(2)}, u32[]{:S(2)}) async-start(bf16[4,384,1536]{2,1,0:T(8,128)(2,1)} %broadcast_in_dim.128), calls=%async_computation.2 | async-start | bytes 9437184 | tf_op jit(solution)/shard_map/all_to_all | solution.py:117
  63.0 7.7 %collective-permute-start = (bf16[1,128,2,512]{1,3,2,0:T(8,128)(2,1)S(1)}, bf16[1,128,2,512]{1,3,2,0:T(8,128)(2,1)S(1)}, u32[]{:S(2)}, u32[]{:S(2)}) collective-permute-start(bf16[1,128,2,512]{1,3,2,0:T(8,128)(2,1)S(1)} %maximum_bitcast_fusion), channel_id=1, source_target_pairs={{0,1},{1,2},{2,3},{3,4},{4,5},{5,6},{6,7},{7,8},{8,9},{9,10},{10,1... | collective-permute-start | bytes 786440 | tf_op jit(solution)/shard_map/ppermute | solution.py:24
  70.7 16.6 %collective-permute-start.1 = (bf16[2,128,2,512]{1,3,2,0:T(8,128)(2,1)S(1)}, bf16[2,128,2,512]{1,3,2,0:T(8,128)(2,1)S(1)}, u32[]{:S(2)}, u32[]{:S(2)}) collective-permute-start(bf16[2,128,2,512]{1,3,2,0:T(8,128)(2,1)S(1)} %pad_maximum_fusion.1), channel_id=1, source_target_pairs={{0,2},{1,3},{2,4},{3,5},{4,6},{5,7},{6,8},{7,9},{8,10},{9,11},{10,... | collective-permute-start | bytes 1572872 | tf_op jit(solution)/shard_map/ppermute | solution.py:24
  103.9 2.2 copy-start.16
  105.0 10.3 %copy-start.4 = (bf16[1,128,1536]{2,1,0:T(8,128)(2,1)S(1)}, bf16[1,128,1536]{2,1,0:T(8,128)(2,1)}, u32[]{:S(2)}) copy-start(bf16[1,128,1536]{2,1,0:T(8,128)(2,1)} %param.11) | copy-start | bytes 1179652
  106.1 12.5 %copy-start.10 = (f32[1536]{0:T(1024)S(1)}, f32[1536]{0:T(1024)}, u32[]{:S(2)}) copy-start(f32[1536]{0:T(1024)} %param.17) | copy-start | bytes 18436
  118.5 226.2 %copy-start.5 = (bf16[128,1536]{1,0:T(8,128)(2,1)}, bf16[128,1536]{1,0:T(8,128)(2,1)S(1)}, u32[]{:S(2)}) copy-start(bf16[128,1536]{1,0:T(8,128)(2,1)S(1)} %get-tuple-element.35) | copy-start | bytes 1179652
  218.3 1.9 copy-start.2
  220.1 6.8 %collective-permute-start.2 = (bf16[32,40,1536]{2,1,0:T(8,128)(2,1)S(1)}, bf16[32,40,1536]{2,1,0:T(8,128)(2,1)S(1)}, u32[]{:S(2)}, u32[]{:S(2)}) collective-permute-start(bf16[32,40,1536]{2,1,0:T(8,128)(2,1)S(1)} %all_to_all.25), channel_id=1, source_target_pairs={{0,1},{1,0},{2,3},{3,2},{4,5},{5,4},{6,7},{7,6},{8,9},{9,8},{10,11... | collective-permute-start | bytes 11796488 | tf_op jit(solution)/shard_map/ppermute | solution.py:193
  226.9 2.0 copy-start.3
  236.4 7.7 %collective-permute-start.3 = (bf16[32,40,1536]{2,1,0:T(8,128)(2,1)}, bf16[32,40,1536]{2,1,0:T(8,128)(2,1)}, u32[]{:S(2)}, u32[]{:S(2)}) collective-permute-start(bf16[32,40,1536]{2,1,0:T(8,128)(2,1)} %bitcast.167), channel_id=1, source_target_pairs={{0,1},{1,0},{2,3},{3,2},{4,5},{5,4},{6,7},{7,6},{8,9},{9,8},{10,11... | collective-permute-start | bytes 11796488 | tf_op jit(solution)/shard_map/ppermute | solution.py:200
  248.5 97.7 %copy-start.1 = (bf16[1536,640]{1,0:T(8,128)(2,1)S(1)}, bf16[1536,640]{1,0:T(8,128)(2,1)}, u32[]{:S(2)}) copy-start(bf16[1536,640]{1,0:T(8,128)(2,1)} %param.13) | copy-start | bytes 5898244
Sparse Core Ops, SparseCore 0:
  19.0 78.9 all-gather.2

commit v11 on v7

--- a/solution.py
+++ b/solution.py
@@ -151,6 +151,8 @@
     hidden_state = (inputs.astype(jnp.float32) + projected).astype(jnp.bfloat16)
     moe_input = rms_norm(hidden_state, ffn_gain)
     chips = lax.axis_size("chip")
+    weights_in, weights_out, moe_input = lax.optimization_barrier((expert_in[0], expert_out[0], moe_input))
+    other_in, other_out = lax.ppermute((weights_in, weights_out), "core", [(0, 1), (1, 0)])
     unit_ff = expert_in.shape[2] // 2
     own_ids = expert_ids[0]
     picks = (own_ids[:, :, None] == jnp.arange(EXPERTS, dtype=jnp.int32)[None, None, :]).astype(jnp.float32)
@@ -165,16 +167,15 @@
     outgoing = jnp.dot(routes.astype(jnp.bfloat16).T, moe_input, preferred_element_type=jnp.float32)
     outgoing = outgoing.astype(jnp.bfloat16).reshape(chips, CAP, model)
     arrived = lax.all_to_all(outgoing, "chip", 0, 0, tiled=True)
-    sibling = lax.ppermute(arrived, "core", [(0, 1), (1, 0)])
-
-    def unit(block):
-        inner = jnp.dot(block.reshape(chips * CAP, model), expert_in[0], preferred_element_type=jnp.float32)
+
+    def unit(block, w_in, w_out):
+        inner = jnp.dot(block.reshape(chips * CAP, model), w_in, preferred_element_type=jnp.float32)
         activated = (jax.nn.silu(inner[:, :unit_ff]) * inner[:, unit_ff:]).astype(jnp.bfloat16)
-        produced = jnp.dot(activated, expert_out[0], preferred_element_type=jnp.float32).astype(jnp.bfloat16)
+        produced = jnp.dot(activated, w_out, preferred_element_type=jnp.float32).astype(jnp.bfloat16)
         return produced.reshape(chips, CAP, model)
 
-    own_part = unit(arrived)
-    partner = lax.ppermute(unit(sibling), "core", [(0, 1), (1, 0)])
+    own_part = unit(arrived, expert_in[0], expert_out[0])
+    partner = unit(arrived, other_in, other_out)
     summed = (own_part.astype(jnp.float32) + partner.astype(jnp.float32)).astype(jnp.bfloat16)
     returned = lax.all_to_all(summed, "chip", 0, 0, tiled=True)
     returned = returned.reshape(chips * CAP, model)

time: 342 us -> 337 us (0.985)
  blocking collectives: 194 us -> 96 us
  waiting for transfers between devices: 59.6 us -> 134 us
  starting transfers between devices: 18.9 us -> 30.6 us
  matrix products: 22.7 us -> 30.5 us
    all_to_all x1 -> x0, blocking collectives: 98.6 us -> none  [shards(): arrived = lax.all_to_all(outgoing, 'chip', 0, 0, tiled=True)]
    all_to_all x0 -> x1, waiting for transfers between devices: none -> 84.5 us  [shards(): arrived = lax.all_to_all(outgoing, 'chip', 0, 0, tiled=True)]
    all_to_all x0 -> x1, starting transfers between devices: none -> 11.4 us  [shards(): arrived = lax.all_to_all(outgoing, 'chip', 0, 0, tiled=True)]
    ppermute x2, waiting for transfers between devices: 9.97 us -> 0.01 us  [shards(): lax.ppermute((weights_in, weights_out), 'core', [(0, 1), (1, 0)])]
    dot_general x4, matrix products: 6.92 us -> 12.9 us  [the longest x2 9.12 us: unit(): jnp.dot(block.reshape(chips * CAP, model), w_in, preferred_element_type=j...]
  transfers between devices with their start and end apart: 8 -> 9, of which waited for: 8 -> 7; matrix products, arithmetic and copies ran while one was open for 11% -> 14% of each run, Pallas kernels for 0% -> 0%
where the time goes in v11:
time: 337 us; the launch traced here: 336 us
  waiting for transfers between devices  134 us (40%)
  blocking collectives  96 us (28%)
  starting transfers between devices  30.6 us (9%)
  matrix products  30.5 us (9%)
  other arithmetic  15.8 us (5%)
  local copies, waits for them, and re-layouts  15.1 us (4%)
  between operations  14.5 us (4%)
    all_to_all x1, blocking collectives, shards(): returned = lax.all_to_all(summed, 'chip', 0, 0, tiled=True)  96 us
    all_to_all x1, waiting for transfers between devices, shards(): arrived = lax.all_to_all(outgoing, 'chip', 0, 0, tiled=True)  84.5 us
    ppermute x2, waiting for transfers between devices, from_behind(): lax.ppermute(value, axis, [(source, source + steps) for source in range(f...  17.3 us
    all_to_all x1, waiting for transfers between devices, shards(): lax.all_to_all(spread, 'dp', 0, 0, tiled=True).reshape(groups * rows, model)  11.8 us
    all_to_all x1, starting transfers between devices, shards(): arrived = lax.all_to_all(outgoing, 'chip', 0, 0, tiled=True)  11.4 us
    dot_general x2, matrix products, unit(): jnp.dot(block.reshape(chips * CAP, model), w_in, preferred_element_type=j...  9.12 us
    all_to_all x1, waiting for transfers between devices, shards(): lax.all_to_all(out_spread, 'dp', 0, 0, tiled=True)  7.68 us
    all_to_all x1, waiting for transfers between devices, shards(): lax.all_to_all(qkv_part.reshape(groups, rows, -1), 'dp', 0, 0, tiled=True)  7.61 us
  transfers between devices with their start and end apart: 9, of which 7 were waited for; matrix products, arithmetic and copies ran while one was open for 14% of the time, Pallas kernels for 0%

profile of v11, /device:TPU:32, one launch (start us, length us, event | category | flops | bytes accessed | tf_op | source)
XLA Modules:
  0.0 336.2 jit_solution(17490604929211994451)
XLA Ops:
  11.0 4.5 %all-to-all-start = ((bf16[4,128,1536]{2,1,0:T(8,128)(2,1)}), bf16[4,128,1536]{2,1,0:T(8,128)(2,1)S(1)}, u32[]{:S(2)}, u32[]{:S(2)}) async-start(bf16[4,128,1536]{2,1,0:T(8,128)(2,1)} %broadcast_in_dim.119), calls=%async_computation | async-start | bytes 3145728 | tf_op jit(solution)/shard_map/all_to_all | solution.py:94
  18.2 1.3 select_reduce_fusion
  20.2 1.5 fusion.62
  23.0 1.4 multiply_cosine_fusion
  24.3 11.8 %all-to-all-done = bf16[4,128,1536]{2,1,0:T(8,128)(2,1)S(1)} async-done(((bf16[4,128,1536]{2,1,0:T(8,128)(2,1)}), bf16[4,128,1536]{2,1,0:T(8,128)(2,1)S(1)}, u32[]{:S(2)}, u32[]{:S(2)}) %all-to-all-start) | async-done | bytes 1572896 | tf_op jit(solution)/shard_map/all_to_all | solution.py:94
  36.1 2.2 convolution_convert_fusion.3
  38.4 2.2 copy.49
  40.5 3.5 %all-to-all-start.1 = ((bf16[4,128,640]{1,2,0:T(8,128)(2,1)}), bf16[4,128,640]{1,2,0:T(8,128)(2,1)S(1)}, u32[]{:S(2)}, u32[]{:S(2)}) async-start(bf16[4,128,640]{1,2,0:T(8,128)(2,1)} %copy.49), calls=%async_computation.1 | async-start | bytes 1310720 | tf_op jit(solution)/shard_map/all_to_all | solution.py:96
  46.4 7.6 %all-to-all-done.1 = bf16[4,128,640]{1,2,0:T(8,128)(2,1)S(1)} async-done(((bf16[4,128,640]{1,2,0:T(8,128)(2,1)}), bf16[4,128,640]{1,2,0:T(8,128)(2,1)S(1)}, u32[]{:S(2)}, u32[]{:S(2)}) %all-to-all-start.1) | async-done | bytes 655392 | tf_op jit(solution)/shard_map/all_to_all | solution.py:96
  54.0 3.8 %broadcast_in_dim.128 = bf16[4,384,1536]{2,1,0:T(8,128)(2,1)} broadcast(bf16[384,1536]{1,0:T(8,128)(2,1)} %param.14), dimensions={1,2} | broadcast | bytes 5898240 | tf_op jit(solution)/shard_map/broadcast_in_dim | solution.py:91
  57.8 5.0 %all-to-all-start.2 = ((bf16[4,384,1536]{2,1,0:T(8,128)(2,1)}), bf16[4,384,1536]{2,1,0:T(8,128)(2,1)}, u32[]{:S(2)}, u32[]{:S(2)}) async-start(bf16[4,384,1536]{2,1,0:T(8,128)(2,1)} %broadcast_in_dim.128), calls=%async_computation.2 | async-start | bytes 9437184 | tf_op jit(solution)/shard_map/all_to_all | solution.py:92
  63.0 1.9 collective-permute-start
  65.8 4.9 %collective-permute-done = bf16[1,128,2,512]{1,3,2,0:T(8,128)(2,1)S(1)} collective-permute-done((bf16[1,128,2,512]{1,3,2,0:T(8,128)(2,1)S(1)}, bf16[1,128,2,512]{1,3,2,0:T(8,128)(2,1)S(1)}, u32[]{:S(2)}, u32[]{:S(2)}) %collective-permute-start) | collective-permute-done | bytes 262176 | tf_op jit(solution)/shard_map/ppermute | solution.py:23
  70.7 3.8 %collective-permute-start.1 = (bf16[2,128,2,512]{1,3,2,0:T(8,128)(2,1)S(1)}, bf16[2,128,2,512]{1,3,2,0:T(8,128)(2,1)S(1)}, u32[]{:S(2)}, u32[]{:S(2)}) collective-permute-start(bf16[2,128,2,512]{1,3,2,0:T(8,128)(2,1)S(1)} %pad_maximum_fusion.1), channel_id=1, source_target_pairs={{0,2},{1,3},{2,4},{3,5},{4,6},{5,7},{6,8},{7,9},{8,10},{9,11},{10,... | collective-permute-start | bytes 1572872 | tf_op jit(solution)/shard_map/ppermute | solution.py:23
  74.8 12.5 %collective-permute-done.1 = bf16[2,128,2,512]{1,3,2,0:T(8,128)(2,1)S(1)} collective-permute-done((bf16[2,128,2,512]{1,3,2,0:T(8,128)(2,1)S(1)}, bf16[2,128,2,512]{1,3,2,0:T(8,128)(2,1)S(1)}, u32[]{:S(2)}, u32[]{:S(2)}) %collective-permute-start.1) | collective-permute-done | bytes 524320 | tf_op jit(solution)/shard_map/ppermute | solution.py:23
  89.7 1.5 fusion.5
  91.3 2.6 fusion.29
  93.9 4.2 %all-gather.3.cloned.1.call-done = bf16[1,512,2,512]{3,2,0,1:T(2,128)(2,1)} async-done(((bf16[1,8,2,512]{3,2,0,1:T(2,128)(2,1)}), bf16[1,512,2,512]{3,2,0,1:T(2,128)(2,1)}) %all-gather.3.cloned.1.call-update) | async-done | bytes 1048592 | tf_op jit(solution)/shard_map/all_gather | solution.py:140
  98.0 3.4 fusion.78
  101.4 1.3 copy.54
  102.7 1.3 copy.55
  106.2 1.3 fusion.36
  107.6 7.7 %all-to-all-done.2 = bf16[4,384,1536]{2,1,0:T(8,128)(2,1)} async-done(((bf16[4,384,1536]{2,1,0:T(8,128)(2,1)}), bf16[4,384,1536]{2,1,0:T(8,128)(2,1)}, u32[]{:S(2)}, u32[]{:S(2)}) %all-to-all-start.2) | async-done | bytes 4718624 | tf_op jit(solution)/shard_map/all_to_all | solution.py:92
  115.3 3.2 fusion.42
  118.7 3.1 convolution_convert_fusion
  121.8 11.4 %all-to-all-start.3 = ((bf16[32,40,1536]{2,1,0:T(8,128)(2,1)}), bf16[32,40,1536]{2,1,0:T(8,128)(2,1)}, u32[]{:S(2)}, u32[]{:S(2)}) async-start(bf16[32,40,1536]{2,1,0:T(8,128)(2,1)} %bitcast.164), calls=%async_computation.3 | async-start | bytes 7864320 | tf_op jit(solution)/shard_map/all_to_all | solution.py:169
  133.8 84.5 %all-to-all-done.3 = bf16[32,40,1536]{2,1,0:T(8,128)(2,1)} async-done(((bf16[32,40,1536]{2,1,0:T(8,128)(2,1)}), bf16[32,40,1536]{2,1,0:T(8,128)(2,1)}, u32[]{:S(2)}, u32[]{:S(2)}) %all-to-all-start.3) | async-done | bytes 3932192 | tf_op jit(solution)/shard_map/all_to_all | solution.py:169
  218.3 4.3 %fusion.67 = f32[1280,512]{1,0:T(8,128)S(1)} fusion(bf16[1280,1536]{1,0:T(8,128)(2,1)} %bitcast.50, bf16[1,1536,512]{2,1,0:T(8,128)(2,1)S(1)} %copy-done.14), kind=kOutput, calls=%fused_computation.111 | convolution fusion | flops 2013265920 | bytes 8126464 | tf_op jit(solution)/shard_map/dot_general | solution.py:172
  223.8 4.8 %fusion.80 = f32[1280,512]{1,0:T(8,128)S(1)} fusion(bf16[1280,1536]{1,0:T(8,128)(2,1)} %bitcast.50, bf16[1536,512]{1,0:T(8,128)(2,1)} %collective-permute-done.2), kind=kOutput, calls=%fused_computation.124 | convolution fusion | flops 2013265920 | bytes 8126464 | tf_op jit(solution)/shard_map/dot_general | solution.py:172
  228.7 2.5 add_convert_fusion
  231.2 96.0 %all_to_all.25 = bf16[32,40,1536]{2,1,0:T(8,128)(2,1)S(1)} all-to-all(bf16[32,40,1536]{2,1,0:T(8,128)(2,1)S(1)} %bitcast.169), channel_id=1, replica_groups=mesh['dp'=4,'chip'=32,'core'=2] {'chip'}, dimensions={0} | all-to-all | bytes 7864320 | tf_op jit(solution)/shard_map/all_to_all | solution.py:180
  327.9 1.5 fusion.17
  (87 shorter events, 19.5 us)
Async XLA Ops:
  7.2 29.0 %copy-start = (bf16[1536,640]{1,0:T(8,128)(2,1)S(1)}, bf16[1536,640]{1,0:T(8,128)(2,1)}, u32[]{:S(2)}) copy-start(bf16[1536,640]{1,0:T(8,128)(2,1)} %param.13) | copy-start | bytes 5898244
  7.2 10.1 %copy-start.9 = (s32[1,256]{1,0:T(1,128)S(1)}, s32[1,256]{1,0:T(1,128)}, u32[]{:S(2)}) copy-start(s32[1,256]{1,0:T(1,128)} %param.16) | copy-start | bytes 3076
  11.0 25.2 %all-to-all-start = ((bf16[4,128,1536]{2,1,0:T(8,128)(2,1)}), bf16[4,128,1536]{2,1,0:T(8,128)(2,1)S(1)}, u32[]{:S(2)}, u32[]{:S(2)}) async-start(bf16[4,128,1536]{2,1,0:T(8,128)(2,1)} %broadcast_in_dim.119), calls=%async_computation | async-start | bytes 3145728 | tf_op jit(solution)/shard_map/all_to_all | solution.py:94
  15.4 82.6 %all-gather.3.cloned.1.call-start = ((), (), s32[]{:S(2)}) async-start(), calls=%async_computation.5 | async-start | bytes 1064960 | tf_op jit(solution)/shard_map/all_gather | solution.py:140
  17.6 0.6 copy-start.7
  17.8 5.1 %copy-start.10 = (s32[128]{0:T(128)}, s32[128]{0:T(128)S(1)}, u32[]{:S(2)}) copy-start(s32[128]{0:T(128)S(1)} %iota_add_fusion) | copy-start | bytes 1540
  20.2 2.7 copy-start.5
  40.5 13.5 %all-to-all-start.1 = ((bf16[4,128,640]{1,2,0:T(8,128)(2,1)}), bf16[4,128,640]{1,2,0:T(8,128)(2,1)S(1)}, u32[]{:S(2)}, u32[]{:S(2)}) async-start(bf16[4,128,640]{1,2,0:T(8,128)(2,1)} %copy.49), calls=%async_computation.1 | async-start | bytes 1310720 | tf_op jit(solution)/shard_map/all_to_all | solution.py:96
  57.8 7.1 %copy-start.6 = (s32[256]{0:T(256)S(1)}, s32[256]{0:T(256)}, u32[]{:S(2)}) copy-start(s32[256]{0:T(256)} %copy-done.5) | copy-start | bytes 3076
  57.8 7.4 %copy-start.4 = (bf16[128,32]{0,1:T(8,128)(2,1)S(1)}, bf16[128,32]{0,1:T(8,128)(2,1)}, u32[]{:S(2)}) copy-start(bf16[128,32]{0,1:T(8,128)(2,1)} %get-tuple-element.17) | copy-start | bytes 24580
  57.8 7.7 %copy-start.11 = (s32[128]{0:T(128)S(1)}, s32[128]{0:T(128)}, u32[]{:S(2)}) copy-start(s32[128]{0:T(128)} %copy-done.10) | copy-start | bytes 1540
  57.8 7.7 %copy-start.12 = (s32[128]{0:T(128)S(1)}, s32[128]{0:T(128)}, u32[]{:S(2)}) copy-start(s32[128]{0:T(128)} %get-tuple-element.18) | copy-start | bytes 1540
  57.8 7.7 %copy-start.13 = (pred[512]{0:T(512)(128)(4,1)S(1)}, pred[512]{0:T(512)(128)(4,1)}, u32[]{:S(2)}) copy-start(pred[512]{0:T(512)(128)(4,1)} %broadcast_compare_fusion) | copy-start | bytes 1540
  57.8 57.4 %all-to-all-start.2 = ((bf16[4,384,1536]{2,1,0:T(8,128)(2,1)}), bf16[4,384,1536]{2,1,0:T(8,128)(2,1)}, u32[]{:S(2)}, u32[]{:S(2)}) async-start(bf16[4,384,1536]{2,1,0:T(8,128)(2,1)} %broadcast_in_dim.128), calls=%async_computation.2 | async-start | bytes 9437184 | tf_op jit(solution)/shard_map/all_to_all | solution.py:92
  63.0 7.7 %collective-permute-start = (bf16[1,128,2,512]{1,3,2,0:T(8,128)(2,1)S(1)}, bf16[1,128,2,512]{1,3,2,0:T(8,128)(2,1)S(1)}, u32[]{:S(2)}, u32[]{:S(2)}) collective-permute-start(bf16[1,128,2,512]{1,3,2,0:T(8,128)(2,1)S(1)} %maximum_bitcast_fusion), channel_id=1, source_target_pairs={{0,1},{1,2},{2,3},{3,4},{4,5},{5,6},{6,7},{7,8},{8,9},{9,10},{10,1... | collective-permute-start | bytes 786440 | tf_op jit(solution)/shard_map/ppermute | solution.py:23
  70.7 16.6 %collective-permute-start.1 = (bf16[2,128,2,512]{1,3,2,0:T(8,128)(2,1)S(1)}, bf16[2,128,2,512]{1,3,2,0:T(8,128)(2,1)S(1)}, u32[]{:S(2)}, u32[]{:S(2)}) collective-permute-start(bf16[2,128,2,512]{1,3,2,0:T(8,128)(2,1)S(1)} %pad_maximum_fusion.1), channel_id=1, source_target_pairs={{0,2},{1,3},{2,4},{3,5},{4,6},{5,7},{6,8},{7,9},{8,10},{9,11},{10,... | collective-permute-start | bytes 1572872 | tf_op jit(solution)/shard_map/ppermute | solution.py:23
  105.1 1.1 copy-start.16
  106.2 9.0 %copy-start.2 = (bf16[1,128,1536]{2,1,0:T(8,128)(2,1)S(1)}, bf16[1,128,1536]{2,1,0:T(8,128)(2,1)}, u32[]{:S(2)}) copy-start(bf16[1,128,1536]{2,1,0:T(8,128)(2,1)} %param.11) | copy-start | bytes 1179652
  107.6 11.0 %copy-start.8 = (f32[1536]{0:T(1024)S(1)}, f32[1536]{0:T(1024)}, u32[]{:S(2)}) copy-start(f32[1536]{0:T(1024)} %param.17) | copy-start | bytes 18436
  118.5 209.4 %copy-start.3 = (bf16[128,1536]{1,0:T(8,128)(2,1)}, bf16[128,1536]{1,0:T(8,128)(2,1)S(1)}, u32[]{:S(2)}) copy-start(bf16[128,1536]{1,0:T(8,128)(2,1)S(1)} %get-tuple-element.41) | copy-start | bytes 1179652
  121.8 11.4 %copy-start.14 = (bf16[1,1536,512]{2,1,0:T(8,128)(2,1)S(1)}, bf16[1,1536,512]{2,1,0:T(8,128)(2,1)}, u32[]{:S(2)}) copy-start(bf16[1,1536,512]{2,1,0:T(8,128)(2,1)} %param.20) | copy-start | bytes 4718596
  121.8 11.5 %copy-start.15 = (bf16[1,256,1536]{2,1,0:T(8,128)(2,1)S(1)}, bf16[1,256,1536]{2,1,0:T(8,128)(2,1)}, u32[]{:S(2)}) copy-start(bf16[1,256,1536]{2,1,0:T(8,128)(2,1)} %param.21) | copy-start | bytes 2359300
  121.8 96.5 %all-to-all-start.3 = ((bf16[32,40,1536]{2,1,0:T(8,128)(2,1)}), bf16[32,40,1536]{2,1,0:T(8,128)(2,1)}, u32[]{:S(2)}, u32[]{:S(2)}) async-start(bf16[32,40,1536]{2,1,0:T(8,128)(2,1)} %bitcast.164), calls=%async_computation.3 | async-start | bytes 7864320 | tf_op jit(solution)/shard_map/all_to_all | solution.py:169
  133.2 90.7 %collective-permute-start.2 = (bf16[1536,512]{1,0:T(8,128)(2,1)S(1)}, bf16[1536,512]{1,0:T(8,128)(2,1)}, u32[]{:S(2)}, u32[]{:S(2)}) collective-permute-start(bf16[1536,512]{1,0:T(8,128)(2,1)S(1)} %bitcast.190), channel_id=1, source_target_pairs={{0,1},{1,0},{2,3},{3,2},{4,5},{5,4},{6,7},{7,6},{8,9},{9,8},{10,11... | collective-permute-start | bytes 4718600 | tf_op jit(solution)/shard_map/ppermute | solution.py:155
  133.3 95.4 %collective-permute-start.3 = (bf16[256,1536]{1,0:T(8,128)(2,1)S(1)}, bf16[256,1536]{1,0:T(8,128)(2,1)}, u32[]{:S(2)}, u32[]{:S(2)}) collective-permute-start(bf16[256,1536]{1,0:T(8,128)(2,1)S(1)} %bitcast.191), channel_id=1, source_target_pairs={{0,1},{1,0},{2,3},{3,2},{4,5},{5,4},{6,7},{7,6},{8,9},{9,8},{10,11... | collective-permute-start | bytes 2359304 | tf_op jit(solution)/shard_map/ppermute | solution.py:155
  327.2 2.2 copy-start.1
Sparse Core Ops, SparseCore 0:
  19.0 78.9 all-gather.2

commit v12 on v11

--- a/solution.py
+++ b/solution.py
@@ -119,6 +119,8 @@
     for bit in range(SHIFTS):
         earlier = from_behind(window, TENSOR, 2**bit)
         window = jnp.concatenate([window, earlier], axis=0)
+    weights_in, weights_out, window = lax.optimization_barrier((expert_in[0], expert_out[0], window))
+    other_in, other_out = lax.ppermute((weights_in, weights_out), "core", [(0, 1), (1, 0)])
     depth = window.shape[0]
     k_index = (
         (lane - jnp.arange(depth, dtype=jnp.int32))[:, None] * rows
@@ -151,8 +153,6 @@
     hidden_state = (inputs.astype(jnp.float32) + projected).astype(jnp.bfloat16)
     moe_input = rms_norm(hidden_state, ffn_gain)
     chips = lax.axis_size("chip")
-    weights_in, weights_out, moe_input = lax.optimization_barrier((expert_in[0], expert_out[0], moe_input))
-    other_in, other_out = lax.ppermute((weights_in, weights_out), "core", [(0, 1), (1, 0)])
     unit_ff = expert_in.shape[2] // 2
     own_ids = expert_ids[0]
     picks = (own_ids[:, :, None] == jnp.arange(EXPERTS, dtype=jnp.int32)[None, None, :]).astype(jnp.float32)

time: 337 us -> 337 us (level)
  no operation moved by 1% of the time
where the time goes in v12:
time: 337 us; the launch traced here: 336 us
  waiting for transfers between devices  134 us (40%)
  blocking collectives  96 us (28%)
  starting transfers between devices  30.6 us (9%)
  matrix products  30.6 us (9%)
  other arithmetic  15.6 us (5%)
  local copies, waits for them, and re-layouts  15.1 us (4%)
  between operations  14.5 us (4%)
    all_to_all x1, blocking collectives, shards(): returned = lax.all_to_all(summed, 'chip', 0, 0, tiled=True)  96 us
    all_to_all x1, waiting for transfers between devices, shards(): arrived = lax.all_to_all(outgoing, 'chip', 0, 0, tiled=True)  84.5 us
    ppermute x2, waiting for transfers between devices, from_behind(): lax.ppermute(value, axis, [(source, source + steps) for source in range(f...  17.3 us
    all_to_all x1, waiting for transfers between devices, shards(): lax.all_to_all(spread, 'dp', 0, 0, tiled=True).reshape(groups * rows, model)  11.8 us
    all_to_all x1, starting transfers between devices, shards(): arrived = lax.all_to_all(outgoing, 'chip', 0, 0, tiled=True)  11.4 us
    dot_general x2, matrix products, unit(): jnp.dot(block.reshape(chips * CAP, model), w_in, preferred_element_type=j...  9.12 us
    all_to_all x1, waiting for transfers between devices, shards(): lax.all_to_all(out_spread, 'dp', 0, 0, tiled=True)  7.68 us
    all_to_all x1, waiting for transfers between devices, shards(): lax.all_to_all(qkv_part.reshape(groups, rows, -1), 'dp', 0, 0, tiled=True)  7.61 us
  transfers between devices with their start and end apart: 9, of which 7 were waited for; matrix products, arithmetic and copies ran while one was open for 14% of the time, Pallas kernels for 0%

profile of v12, /device:TPU:32, one launch (start us, length us, event | category | flops | bytes accessed | tf_op | source)
XLA Modules:
  0.0 336.2 jit_solution(9364927619453359837)
XLA Ops:
  11.0 4.5 %all-to-all-start = ((bf16[4,128,1536]{2,1,0:T(8,128)(2,1)}), bf16[4,128,1536]{2,1,0:T(8,128)(2,1)S(1)}, u32[]{:S(2)}, u32[]{:S(2)}) async-start(bf16[4,128,1536]{2,1,0:T(8,128)(2,1)} %broadcast_in_dim.119), calls=%async_computation | async-start | bytes 3145728 | tf_op jit(solution)/shard_map/all_to_all | solution.py:94
  18.2 1.3 select_reduce_fusion
  20.2 1.5 fusion.65
  23.0 1.4 multiply_cosine_fusion
  24.3 11.8 %all-to-all-done = bf16[4,128,1536]{2,1,0:T(8,128)(2,1)S(1)} async-done(((bf16[4,128,1536]{2,1,0:T(8,128)(2,1)}), bf16[4,128,1536]{2,1,0:T(8,128)(2,1)S(1)}, u32[]{:S(2)}, u32[]{:S(2)}) %all-to-all-start) | async-done | bytes 1572896 | tf_op jit(solution)/shard_map/all_to_all | solution.py:94
  36.1 2.2 convolution_convert_fusion.3
  38.4 2.2 copy.49
  40.5 3.5 %all-to-all-start.1 = ((bf16[4,128,640]{1,2,0:T(8,128)(2,1)}), bf16[4,128,640]{1,2,0:T(8,128)(2,1)S(1)}, u32[]{:S(2)}, u32[]{:S(2)}) async-start(bf16[4,128,640]{1,2,0:T(8,128)(2,1)} %copy.49), calls=%async_computation.1 | async-start | bytes 1310720 | tf_op jit(solution)/shard_map/all_to_all | solution.py:96
  46.4 7.6 %all-to-all-done.1 = bf16[4,128,640]{1,2,0:T(8,128)(2,1)S(1)} async-done(((bf16[4,128,640]{1,2,0:T(8,128)(2,1)}), bf16[4,128,640]{1,2,0:T(8,128)(2,1)S(1)}, u32[]{:S(2)}, u32[]{:S(2)}) %all-to-all-start.1) | async-done | bytes 655392 | tf_op jit(solution)/shard_map/all_to_all | solution.py:96
  54.0 3.8 %broadcast_in_dim.128 = bf16[4,384,1536]{2,1,0:T(8,128)(2,1)} broadcast(bf16[384,1536]{1,0:T(8,128)(2,1)} %param.14), dimensions={1,2} | broadcast | bytes 5898240 | tf_op jit(solution)/shard_map/broadcast_in_dim | solution.py:91
  57.8 5.0 %all-to-all-start.2 = ((bf16[4,384,1536]{2,1,0:T(8,128)(2,1)}), bf16[4,384,1536]{2,1,0:T(8,128)(2,1)}, u32[]{:S(2)}, u32[]{:S(2)}) async-start(bf16[4,384,1536]{2,1,0:T(8,128)(2,1)} %broadcast_in_dim.128), calls=%async_computation.2 | async-start | bytes 9437184 | tf_op jit(solution)/shard_map/all_to_all | solution.py:92
  63.0 1.9 collective-permute-start
  65.8 4.9 %collective-permute-done = bf16[1,128,2,512]{1,3,2,0:T(8,128)(2,1)S(1)} collective-permute-done((bf16[1,128,2,512]{1,3,2,0:T(8,128)(2,1)S(1)}, bf16[1,128,2,512]{1,3,2,0:T(8,128)(2,1)S(1)}, u32[]{:S(2)}, u32[]{:S(2)}) %collective-permute-start) | collective-permute-done | bytes 262176 | tf_op jit(solution)/shard_map/ppermute | solution.py:23
  70.7 3.8 %collective-permute-start.1 = (bf16[2,128,2,512]{1,3,2,0:T(8,128)(2,1)S(1)}, bf16[2,128,2,512]{1,3,2,0:T(8,128)(2,1)S(1)}, u32[]{:S(2)}, u32[]{:S(2)}) collective-permute-start(bf16[2,128,2,512]{1,3,2,0:T(8,128)(2,1)S(1)} %pad_maximum_fusion.1), channel_id=1, source_target_pairs={{0,2},{1,3},{2,4},{3,5},{4,6},{5,7},{6,8},{7,9},{8,10},{9,11},{10,... | collective-permute-start | bytes 1572872 | tf_op jit(solution)/shard_map/ppermute | solution.py:23
  74.8 12.5 %collective-permute-done.1 = bf16[2,128,2,512]{1,3,2,0:T(8,128)(2,1)S(1)} collective-permute-done((bf16[2,128,2,512]{1,3,2,0:T(8,128)(2,1)S(1)}, bf16[2,128,2,512]{1,3,2,0:T(8,128)(2,1)S(1)}, u32[]{:S(2)}, u32[]{:S(2)}) %collective-permute-start.1) | collective-permute-done | bytes 524320 | tf_op jit(solution)/shard_map/ppermute | solution.py:23
  89.7 1.5 fusion.5
  91.3 2.6 fusion.29
  93.9 4.2 %all-gather.3.cloned.1.call-done = bf16[1,512,2,512]{3,2,0,1:T(2,128)(2,1)} async-done(((bf16[1,8,2,512]{3,2,0,1:T(2,128)(2,1)}), bf16[1,512,2,512]{3,2,0,1:T(2,128)(2,1)}) %all-gather.3.cloned.1.call-update) | async-done | bytes 1048592 | tf_op jit(solution)/shard_map/all_gather | solution.py:142
  98.0 3.4 fusion.81
  101.4 1.3 copy.54
  102.7 1.3 copy.55
  106.2 1.3 fusion.36
  107.6 7.7 %all-to-all-done.2 = bf16[4,384,1536]{2,1,0:T(8,128)(2,1)} async-done(((bf16[4,384,1536]{2,1,0:T(8,128)(2,1)}), bf16[4,384,1536]{2,1,0:T(8,128)(2,1)}, u32[]{:S(2)}, u32[]{:S(2)}) %all-to-all-start.2) | async-done | bytes 4718624 | tf_op jit(solution)/shard_map/all_to_all | solution.py:92
  115.3 3.2 fusion.42
  118.5 3.2 convolution_convert_fusion
  121.7 11.4 %all-to-all-start.3 = ((bf16[32,40,1536]{2,1,0:T(8,128)(2,1)}), bf16[32,40,1536]{2,1,0:T(8,128)(2,1)}, u32[]{:S(2)}, u32[]{:S(2)}) async-start(bf16[32,40,1536]{2,1,0:T(8,128)(2,1)} %bitcast.163), calls=%async_computation.3 | async-start | bytes 7864320 | tf_op jit(solution)/shard_map/all_to_all | solution.py:169
  133.7 84.5 %all-to-all-done.3 = bf16[32,40,1536]{2,1,0:T(8,128)(2,1)} async-done(((bf16[32,40,1536]{2,1,0:T(8,128)(2,1)}), bf16[32,40,1536]{2,1,0:T(8,128)(2,1)}, u32[]{:S(2)}, u32[]{:S(2)}) %all-to-all-start.3) | async-done | bytes 3932192 | tf_op jit(solution)/shard_map/all_to_all | solution.py:169
  218.2 4.3 %fusion.70 = f32[1280,512]{1,0:T(8,128)S(1)} fusion(bf16[1280,1536]{1,0:T(8,128)(2,1)} %bitcast.50, bf16[1,1536,512]{2,1,0:T(8,128)(2,1)S(1)} %copy-done.14), kind=kOutput, calls=%fused_computation.113 | convolution fusion | flops 2013265920 | bytes 8126464 | tf_op jit(solution)/shard_map/dot_general | solution.py:172
  223.8 4.8 %fusion.83 = f32[1280,512]{1,0:T(8,128)S(1)} fusion(bf16[1280,1536]{1,0:T(8,128)(2,1)} %bitcast.50, bf16[1536,512]{1,0:T(8,128)(2,1)} %collective-permute-done.2), kind=kOutput, calls=%fused_computation.126 | convolution fusion | flops 2013265920 | bytes 8126464 | tf_op jit(solution)/shard_map/dot_general | solution.py:172
  228.6 2.5 add_convert_fusion
  231.1 96.0 %all_to_all.25 = bf16[32,40,1536]{2,1,0:T(8,128)(2,1)S(1)} all-to-all(bf16[32,40,1536]{2,1,0:T(8,128)(2,1)S(1)} %bitcast.168), channel_id=1, replica_groups=mesh['dp'=4,'chip'=32,'core'=2] {'chip'}, dimensions={0} | all-to-all | bytes 7864320 | tf_op jit(solution)/shard_map/all_to_all | solution.py:180
  327.9 1.5 fusion.17
  (86 shorter events, 19.3 us)
Async XLA Ops:
  7.2 29.0 %copy-start = (bf16[1536,640]{1,0:T(8,128)(2,1)S(1)}, bf16[1536,640]{1,0:T(8,128)(2,1)}, u32[]{:S(2)}) copy-start(bf16[1536,640]{1,0:T(8,128)(2,1)} %param.13) | copy-start | bytes 5898244
  7.2 10.1 %copy-start.9 = (s32[1,256]{1,0:T(1,128)S(1)}, s32[1,256]{1,0:T(1,128)}, u32[]{:S(2)}) copy-start(s32[1,256]{1,0:T(1,128)} %param.16) | copy-start | bytes 3076
  11.0 25.2 %all-to-all-start = ((bf16[4,128,1536]{2,1,0:T(8,128)(2,1)}), bf16[4,128,1536]{2,1,0:T(8,128)(2,1)S(1)}, u32[]{:S(2)}, u32[]{:S(2)}) async-start(bf16[4,128,1536]{2,1,0:T(8,128)(2,1)} %broadcast_in_dim.119), calls=%async_computation | async-start | bytes 3145728 | tf_op jit(solution)/shard_map/all_to_all | solution.py:94
  15.4 82.6 %all-gather.3.cloned.1.call-start = ((), (), s32[]{:S(2)}) async-start(), calls=%async_computation.5 | async-start | bytes 1064960 | tf_op jit(solution)/shard_map/all_gather | solution.py:142
  17.6 0.6 copy-start.7
  17.8 5.1 %copy-start.10 = (s32[128]{0:T(128)}, s32[128]{0:T(128)S(1)}, u32[]{:S(2)}) copy-start(s32[128]{0:T(128)S(1)} %iota_add_fusion) | copy-start | bytes 1540
  20.2 2.7 copy-start.5
  40.5 13.5 %all-to-all-start.1 = ((bf16[4,128,640]{1,2,0:T(8,128)(2,1)}), bf16[4,128,640]{1,2,0:T(8,128)(2,1)S(1)}, u32[]{:S(2)}, u32[]{:S(2)}) async-start(bf16[4,128,640]{1,2,0:T(8,128)(2,1)} %copy.49), calls=%async_computation.1 | async-start | bytes 1310720 | tf_op jit(solution)/shard_map/all_to_all | solution.py:96
  57.8 7.1 %copy-start.6 = (s32[256]{0:T(256)S(1)}, s32[256]{0:T(256)}, u32[]{:S(2)}) copy-start(s32[256]{0:T(256)} %copy-done.5) | copy-start | bytes 3076
  57.8 7.4 %copy-start.4 = (bf16[128,32]{0,1:T(8,128)(2,1)S(1)}, bf16[128,32]{0,1:T(8,128)(2,1)}, u32[]{:S(2)}) copy-start(bf16[128,32]{0,1:T(8,128)(2,1)} %get-tuple-element.17) | copy-start | bytes 24580
  57.8 7.7 %copy-start.11 = (s32[128]{0:T(128)S(1)}, s32[128]{0:T(128)}, u32[]{:S(2)}) copy-start(s32[128]{0:T(128)} %copy-done.10) | copy-start | bytes 1540
  57.8 7.7 %copy-start.12 = (s32[128]{0:T(128)S(1)}, s32[128]{0:T(128)}, u32[]{:S(2)}) copy-start(s32[128]{0:T(128)} %get-tuple-element.18) | copy-start | bytes 1540
  57.8 7.7 %copy-start.13 = (pred[512]{0:T(512)(128)(4,1)S(1)}, pred[512]{0:T(512)(128)(4,1)}, u32[]{:S(2)}) copy-start(pred[512]{0:T(512)(128)(4,1)} %broadcast_compare_fusion) | copy-start | bytes 1540
  57.8 57.4 %all-to-all-start.2 = ((bf16[4,384,1536]{2,1,0:T(8,128)(2,1)}), bf16[4,384,1536]{2,1,0:T(8,128)(2,1)}, u32[]{:S(2)}, u32[]{:S(2)}) async-start(bf16[4,384,1536]{2,1,0:T(8,128)(2,1)} %broadcast_in_dim.128), calls=%async_computation.2 | async-start | bytes 9437184 | tf_op jit(solution)/shard_map/all_to_all | solution.py:92
  63.0 7.7 %collective-permute-start = (bf16[1,128,2,512]{1,3,2,0:T(8,128)(2,1)S(1)}, bf16[1,128,2,512]{1,3,2,0:T(8,128)(2,1)S(1)}, u32[]{:S(2)}, u32[]{:S(2)}) collective-permute-start(bf16[1,128,2,512]{1,3,2,0:T(8,128)(2,1)S(1)} %maximum_bitcast_fusion), channel_id=1, source_target_pairs={{0,1},{1,2},{2,3},{3,4},{4,5},{5,6},{6,7},{7,8},{8,9},{9,10},{10,1... | collective-permute-start | bytes 786440 | tf_op jit(solution)/shard_map/ppermute | solution.py:23
  70.7 16.6 %collective-permute-start.1 = (bf16[2,128,2,512]{1,3,2,0:T(8,128)(2,1)S(1)}, bf16[2,128,2,512]{1,3,2,0:T(8,128)(2,1)S(1)}, u32[]{:S(2)}, u32[]{:S(2)}) collective-permute-start(bf16[2,128,2,512]{1,3,2,0:T(8,128)(2,1)S(1)} %pad_maximum_fusion.1), channel_id=1, source_target_pairs={{0,2},{1,3},{2,4},{3,5},{4,6},{5,7},{6,8},{7,9},{8,10},{9,11},{10,... | collective-permute-start | bytes 1572872 | tf_op jit(solution)/shard_map/ppermute | solution.py:23
  105.1 1.1 copy-start.16
  106.2 9.0 %copy-start.2 = (bf16[1,128,1536]{2,1,0:T(8,128)(2,1)S(1)}, bf16[1,128,1536]{2,1,0:T(8,128)(2,1)}, u32[]{:S(2)}) copy-start(bf16[1,128,1536]{2,1,0:T(8,128)(2,1)} %param.11) | copy-start | bytes 1179652
  107.6 11.0 %copy-start.8 = (f32[1536]{0:T(1024)S(1)}, f32[1536]{0:T(1024)}, u32[]{:S(2)}) copy-start(f32[1536]{0:T(1024)} %param.17) | copy-start | bytes 18436
  118.5 209.3 %copy-start.3 = (bf16[128,1536]{1,0:T(8,128)(2,1)}, bf16[128,1536]{1,0:T(8,128)(2,1)S(1)}, u32[]{:S(2)}) copy-start(bf16[128,1536]{1,0:T(8,128)(2,1)S(1)} %get-tuple-element.41) | copy-start | bytes 1179652
  121.7 11.4 %copy-start.14 = (bf16[1,1536,512]{2,1,0:T(8,128)(2,1)S(1)}, bf16[1,1536,512]{2,1,0:T(8,128)(2,1)}, u32[]{:S(2)}) copy-start(bf16[1,1536,512]{2,1,0:T(8,128)(2,1)} %param.20) | copy-start | bytes 4718596
  121.7 11.5 %copy-start.15 = (bf16[1,256,1536]{2,1,0:T(8,128)(2,1)S(1)}, bf16[1,256,1536]{2,1,0:T(8,128)(2,1)}, u32[]{:S(2)}) copy-start(bf16[1,256,1536]{2,1,0:T(8,128)(2,1)} %param.21) | copy-start | bytes 2359300
  121.7 96.5 %all-to-all-start.3 = ((bf16[32,40,1536]{2,1,0:T(8,128)(2,1)}), bf16[32,40,1536]{2,1,0:T(8,128)(2,1)}, u32[]{:S(2)}, u32[]{:S(2)}) async-start(bf16[32,40,1536]{2,1,0:T(8,128)(2,1)} %bitcast.163), calls=%async_computation.3 | async-start | bytes 7864320 | tf_op jit(solution)/shard_map/all_to_all | solution.py:169
  133.1 90.7 %collective-permute-start.2 = (bf16[1536,512]{1,0:T(8,128)(2,1)S(1)}, bf16[1536,512]{1,0:T(8,128)(2,1)}, u32[]{:S(2)}, u32[]{:S(2)}) collective-permute-start(bf16[1536,512]{1,0:T(8,128)(2,1)S(1)} %bitcast.189), channel_id=1, source_target_pairs={{0,1},{1,0},{2,3},{3,2},{4,5},{5,4},{6,7},{7,6},{8,9},{9,8},{10,11... | collective-permute-start | bytes 4718600 | tf_op jit(solution)/shard_map/ppermute | solution.py:123
  133.2 95.4 %collective-permute-start.3 = (bf16[256,1536]{1,0:T(8,128)(2,1)S(1)}, bf16[256,1536]{1,0:T(8,128)(2,1)}, u32[]{:S(2)}, u32[]{:S(2)}) collective-permute-start(bf16[256,1536]{1,0:T(8,128)(2,1)S(1)} %bitcast.190), channel_id=1, source_target_pairs={{0,1},{1,0},{2,3},{3,2},{4,5},{5,4},{6,7},{7,6},{8,9},{9,8},{10,11... | collective-permute-start | bytes 2359304 | tf_op jit(solution)/shard_map/ppermute | solution.py:123
  327.1 2.2 copy-start.1
Sparse Core Ops, SparseCore 0:
  19.0 78.9 all-gather.2

commit v13 on v12

--- a/solution.py
+++ b/solution.py
@@ -115,10 +115,7 @@
         jnp.zeros((rows, KV_HEADS, ratio), jnp.float32),
         jnp.zeros((rows, KV_HEADS, ratio, HEAD_DIM), jnp.float32),
     )
-    window = local_pairs[None]
-    for bit in range(SHIFTS):
-        earlier = from_behind(window, TENSOR, 2**bit)
-        window = jnp.concatenate([window, earlier], axis=0)
+    window = jnp.stack([local_pairs] + [from_behind(local_pairs, TENSOR, step) for step in range(1, 2**SHIFTS)])
     weights_in, weights_out, window = lax.optimization_barrier((expert_in[0], expert_out[0], window))
     other_in, other_out = lax.ppermute((weights_in, weights_out), "core", [(0, 1), (1, 0)])
     depth = window.shape[0]

time: 337 us -> 336 us (level)
  waiting for transfers between devices: 134 us -> 127 us
  starting transfers between devices: 30.6 us -> 37 us
    ppermute x2 -> x3, waiting for transfers between devices: 17.3 us -> 9.92 us  [from_behind(): lax.ppermute(value, axis, [(source, source + steps) for source in range(f...]
    ppermute x2 -> x3, starting transfers between devices: 5.74 us -> 12.1 us  [from_behind(): lax.ppermute(value, axis, [(source, source + steps) for source in range(f...]
  transfers between devices with their start and end apart: 9 -> 10, of which waited for: 7 -> 7; matrix products, arithmetic and copies ran while one was open for 14% -> 14% of each run, Pallas kernels for 0% -> 0%
where the time goes in v13:
time: 336 us; the launch traced here: 335 us
  waiting for transfers between devices  127 us (38%)
  blocking collectives  96 us (29%)
  starting transfers between devices  37 us (11%)
  matrix products  29.9 us (9%)
  other arithmetic  16.1 us (5%)
  local copies, waits for them, and re-layouts  14.8 us (4%)
  between operations  14.4 us (4%)
    all_to_all x1, blocking collectives, shards(): returned = lax.all_to_all(summed, 'chip', 0, 0, tiled=True)  96 us
    all_to_all x1, waiting for transfers between devices, shards(): arrived = lax.all_to_all(outgoing, 'chip', 0, 0, tiled=True)  84.7 us
    ppermute x3, starting transfers between devices, from_behind(): lax.ppermute(value, axis, [(source, source + steps) for source in range(f...  12.1 us
    all_to_all x1, waiting for transfers between devices, shards(): lax.all_to_all(spread, 'dp', 0, 0, tiled=True).reshape(groups * rows, model)  11.4 us
    all_to_all x1, starting transfers between devices, shards(): arrived = lax.all_to_all(outgoing, 'chip', 0, 0, tiled=True)  11.4 us
    ppermute x3, waiting for transfers between devices, from_behind(): lax.ppermute(value, axis, [(source, source + steps) for source in range(f...  9.92 us
    dot_general x2, matrix products, unit(): jnp.dot(block.reshape(chips * CAP, model), w_in, preferred_element_type=j...  9.12 us
    all_gather x1, waiting for transfers between devices, shards(): piece = lax.all_gather(prefix_cache[0], TENSOR, axis=0, tiled=True)  7.22 us
  transfers between devices with their start and end apart: 10, of which 7 were waited for; matrix products, arithmetic and copies ran while one was open for 14% of the time, Pallas kernels for 0%

profile of v13, /device:TPU:32, one launch (start us, length us, event | category | flops | bytes accessed | tf_op | source)
XLA Modules:
  0.0 335.2 jit_solution(1857095185671947175)
XLA Ops:
  7.2 1.3 fusion.39
  11.0 4.5 %all-to-all-start = ((bf16[4,128,1536]{2,1,0:T(8,128)(2,1)}), bf16[4,128,1536]{2,1,0:T(8,128)(2,1)S(1)}, u32[]{:S(2)}, u32[]{:S(2)}) async-start(bf16[4,128,1536]{2,1,0:T(8,128)(2,1)} %broadcast_in_dim.116), calls=%async_computation | async-start | bytes 3145728 | tf_op jit(solution)/shard_map/all_to_all | solution.py:94
  19.1 1.3 select_reduce_fusion
  23.3 1.4 multiply_cosine_fusion
  24.7 11.4 %all-to-all-done = bf16[4,128,1536]{2,1,0:T(8,128)(2,1)S(1)} async-done(((bf16[4,128,1536]{2,1,0:T(8,128)(2,1)}), bf16[4,128,1536]{2,1,0:T(8,128)(2,1)S(1)}, u32[]{:S(2)}, u32[]{:S(2)}) %all-to-all-start) | async-done | bytes 1572896 | tf_op jit(solution)/shard_map/all_to_all | solution.py:94
  36.1 2.2 convolution_convert_fusion.3
  38.4 2.3 copy.49
  40.6 3.5 %all-to-all-start.1 = ((bf16[4,128,640]{1,2,0:T(8,128)(2,1)}), bf16[4,128,640]{1,2,0:T(8,128)(2,1)S(1)}, u32[]{:S(2)}, u32[]{:S(2)}) async-start(bf16[4,128,640]{1,2,0:T(8,128)(2,1)} %copy.49), calls=%async_computation.1 | async-start | bytes 1310720 | tf_op jit(solution)/shard_map/all_to_all | solution.py:96
  47.6 6.5 %all-to-all-done.1 = bf16[4,128,640]{1,2,0:T(8,128)(2,1)S(1)} async-done(((bf16[4,128,640]{1,2,0:T(8,128)(2,1)}), bf16[4,128,640]{1,2,0:T(8,128)(2,1)S(1)}, u32[]{:S(2)}, u32[]{:S(2)}) %all-to-all-start.1) | async-done | bytes 655392 | tf_op jit(solution)/shard_map/all_to_all | solution.py:96
  54.1 2.5 broadcast_in_dim.124
  56.6 4.9 %all-to-all-start.2 = ((bf16[4,384,1536]{2,1,0:T(8,128)(2,1)}), bf16[4,384,1536]{2,1,0:T(8,128)(2,1)}, u32[]{:S(2)}, u32[]{:S(2)}) async-start(bf16[4,384,1536]{2,1,0:T(8,128)(2,1)} %broadcast_in_dim.124), calls=%async_computation.2 | async-start | bytes 9437184 | tf_op jit(solution)/shard_map/all_to_all | solution.py:92
  61.8 1.9 collective-permute-start
  63.7 3.8 %collective-permute-start.1 = (bf16[128,2,512]{0,2,1:T(8,128)(2,1)S(1)}, bf16[128,2,512]{0,2,1:T(8,128)(2,1)S(1)}, u32[]{:S(2)}, u32[]{:S(2)}) collective-permute-start(bf16[128,2,512]{0,2,1:T(8,128)(2,1)S(1)} %get-tuple-element.31), channel_id=1, source_target_pairs={{0,2},{1,3},{2,4},{3,5},{4,6},{5,7},{6,8},{7,9},{8,10},{9,11},{10,... | collective-permute-start | bytes 786440 | tf_op jit(solution)/shard_map/ppermute | solution.py:23
  67.5 6.4 %collective-permute-start.2 = (bf16[128,2,512]{0,2,1:T(8,128)(2,1)S(1)}, bf16[128,2,512]{0,2,1:T(8,128)(2,1)S(1)}, u32[]{:S(2)}, u32[]{:S(2)}) collective-permute-start(bf16[128,2,512]{0,2,1:T(8,128)(2,1)S(1)} %get-tuple-element.31), channel_id=1, source_target_pairs={{0,3},{1,4},{2,5},{3,6},{4,7},{5,8},{6,9},{7,10},{8,11},{9,12},{10... | collective-permute-start | bytes 786440 | tf_op jit(solution)/shard_map/ppermute | solution.py:23
  74.7 9.5 %collective-permute-done.2 = bf16[128,2,512]{0,2,1:T(8,128)(2,1)S(1)} collective-permute-done((bf16[128,2,512]{0,2,1:T(8,128)(2,1)S(1)}, bf16[128,2,512]{0,2,1:T(8,128)(2,1)S(1)}, u32[]{:S(2)}, u32[]{:S(2)}) %collective-permute-start.2) | collective-permute-done | bytes 262176 | tf_op jit(solution)/shard_map/ppermute | solution.py:23
  86.6 1.5 fusion.5
  88.1 2.6 fusion.29
  90.7 7.2 %all-gather.3.cloned.1.call-done = bf16[1,512,2,512]{3,2,0,1:T(2,128)(2,1)} async-done(((bf16[1,8,2,512]{3,2,0,1:T(2,128)(2,1)}), bf16[1,512,2,512]{3,2,0,1:T(2,128)(2,1)}) %all-gather.3.cloned.1.call-update) | async-done | bytes 1048592 | tf_op jit(solution)/shard_map/all_gather | solution.py:139
  98.0 3.4 %fusion.82 = (bf16[512,1,512]{2,1,0:T(2,128)(2,1)S(1)}, bf16[512,1,512]{2,1,0:T(2,128)(2,1)S(1)}) fusion(bf16[512,2,512]{2,1,0:T(2,128)(2,1)} %bitcast.169), kind=kLoop, calls=%fused_computation.124 | loop fusion | bytes 2097152 | tf_op jit(solution)/shard_map/slice | solution.py:142
  101.3 1.3 copy.54
  102.6 1.3 copy.55
  106.2 1.3 fusion.36
  107.5 6.5 %all-to-all-done.2 = bf16[4,384,1536]{2,1,0:T(8,128)(2,1)} async-done(((bf16[4,384,1536]{2,1,0:T(8,128)(2,1)}), bf16[4,384,1536]{2,1,0:T(8,128)(2,1)}, u32[]{:S(2)}, u32[]{:S(2)}) %all-to-all-start.2) | async-done | bytes 4718624 | tf_op jit(solution)/shard_map/all_to_all | solution.py:92
  114.1 3.2 fusion.42
  117.3 3.2 convolution_convert_fusion
  120.5 11.4 %all-to-all-start.3 = ((bf16[32,40,1536]{2,1,0:T(8,128)(2,1)}), bf16[32,40,1536]{2,1,0:T(8,128)(2,1)}, u32[]{:S(2)}, u32[]{:S(2)}) async-start(bf16[32,40,1536]{2,1,0:T(8,128)(2,1)} %bitcast.166), calls=%async_computation.3 | async-start | bytes 7864320 | tf_op jit(solution)/shard_map/all_to_all | solution.py:166
  132.6 84.7 %all-to-all-done.3 = bf16[32,40,1536]{2,1,0:T(8,128)(2,1)} async-done(((bf16[32,40,1536]{2,1,0:T(8,128)(2,1)}), bf16[32,40,1536]{2,1,0:T(8,128)(2,1)}, u32[]{:S(2)}, u32[]{:S(2)}) %all-to-all-start.3) | async-done | bytes 3932192 | tf_op jit(solution)/shard_map/all_to_all | solution.py:166
  217.2 4.3 %fusion.70 = f32[1280,512]{1,0:T(8,128)S(1)} fusion(bf16[1280,1536]{1,0:T(8,128)(2,1)} %bitcast.53, bf16[1,1536,512]{2,1,0:T(8,128)(2,1)S(1)} %copy-done.12), kind=kOutput, calls=%fused_computation.112 | convolution fusion | flops 2013265920 | bytes 8126464 | tf_op jit(solution)/shard_map/dot_general | solution.py:169
  222.8 4.8 %fusion.84 = f32[1280,512]{1,0:T(8,128)S(1)} fusion(bf16[1280,1536]{1,0:T(8,128)(2,1)} %bitcast.53, bf16[1536,512]{1,0:T(8,128)(2,1)} %collective-permute-done.3), kind=kOutput, calls=%fused_computation.126 | convolution fusion | flops 2013265920 | bytes 8126464 | tf_op jit(solution)/shard_map/dot_general | solution.py:169
  227.6 2.5 add_convert_fusion
  230.1 96.0 %all_to_all.25 = bf16[32,40,1536]{2,1,0:T(8,128)(2,1)S(1)} all-to-all(bf16[32,40,1536]{2,1,0:T(8,128)(2,1)S(1)} %bitcast.171), channel_id=1, replica_groups=mesh['dp'=4,'chip'=32,'core'=2] {'chip'}, dimensions={0} | all-to-all | bytes 7864320 | tf_op jit(solution)/shard_map/all_to_all | solution.py:177
  326.8 1.5 fusion.17
  (83 shorter events, 20.6 us)
Async XLA Ops:
  7.2 29.0 %copy-start = (bf16[1536,640]{1,0:T(8,128)(2,1)S(1)}, bf16[1536,640]{1,0:T(8,128)(2,1)}, u32[]{:S(2)}) copy-start(bf16[1536,640]{1,0:T(8,128)(2,1)} %param.13) | copy-start | bytes 5898244
  7.2 10.1 %copy-start.9 = (s32[1,256]{1,0:T(1,128)S(1)}, s32[1,256]{1,0:T(1,128)}, u32[]{:S(2)}) copy-start(s32[1,256]{1,0:T(1,128)} %param.16) | copy-start | bytes 3076
  7.2 12.0 %copy-start.10 = (f32[1,128,8]{1,2,0:T(8,128)S(1)}, f32[1,128,8]{1,2,0:T(8,128)}, u32[]{:S(2)}) copy-start(f32[1,128,8]{1,2,0:T(8,128)} %param.19) | copy-start | bytes 12292
  11.0 25.2 %all-to-all-start = ((bf16[4,128,1536]{2,1,0:T(8,128)(2,1)}), bf16[4,128,1536]{2,1,0:T(8,128)(2,1)S(1)}, u32[]{:S(2)}, u32[]{:S(2)}) async-start(bf16[4,128,1536]{2,1,0:T(8,128)(2,1)} %broadcast_in_dim.116), calls=%async_computation | async-start | bytes 3145728 | tf_op jit(solution)/shard_map/all_to_all | solution.py:94
  15.4 82.5 %all-gather.3.cloned.1.call-start = ((), (), s32[]{:S(2)}) async-start(), calls=%async_computation.5 | async-start | bytes 1064960 | tf_op jit(solution)/shard_map/all_gather | solution.py:139
  20.5 2.9 copy-start.6
  20.5 0.5 copy-start.11
  22.4 0.9 copy-start.7
  38.4 15.8 %copy-start.4 = (bf16[384,1536]{1,0:T(8,128)(2,1)S(1)}, bf16[384,1536]{1,0:T(8,128)(2,1)}, u32[]{:S(2)}) copy-start(bf16[384,1536]{1,0:T(8,128)(2,1)} %param.14) | copy-start | bytes 3538948
  40.6 13.5 %all-to-all-start.1 = ((bf16[4,128,640]{1,2,0:T(8,128)(2,1)}), bf16[4,128,640]{1,2,0:T(8,128)(2,1)S(1)}, u32[]{:S(2)}, u32[]{:S(2)}) async-start(bf16[4,128,640]{1,2,0:T(8,128)(2,1)} %copy.49), calls=%async_computation.1 | async-start | bytes 1310720 | tf_op jit(solution)/shard_map/all_to_all | solution.py:96
  56.6 57.4 %all-to-all-start.2 = ((bf16[4,384,1536]{2,1,0:T(8,128)(2,1)}), bf16[4,384,1536]{2,1,0:T(8,128)(2,1)}, u32[]{:S(2)}, u32[]{:S(2)}) async-start(bf16[4,384,1536]{2,1,0:T(8,128)(2,1)} %broadcast_in_dim.124), calls=%async_computation.2 | async-start | bytes 9437184 | tf_op jit(solution)/shard_map/all_to_all | solution.py:92
  61.8 12.4 %collective-permute-start = (bf16[128,2,512]{0,2,1:T(8,128)(2,1)S(1)}, bf16[128,2,512]{0,2,1:T(8,128)(2,1)S(1)}, u32[]{:S(2)}, u32[]{:S(2)}) collective-permute-start(bf16[128,2,512]{0,2,1:T(8,128)(2,1)S(1)} %get-tuple-element.31), channel_id=1, source_target_pairs={{0,1},{1,2},{2,3},{3,4},{4,5},{5,6},{6,7},{7,8},{8,9},{9,10},{10,1... | collective-permute-start | bytes 786440 | tf_op jit(solution)/shard_map/ppermute | solution.py:23
  63.7 11.0 %collective-permute-start.1 = (bf16[128,2,512]{0,2,1:T(8,128)(2,1)S(1)}, bf16[128,2,512]{0,2,1:T(8,128)(2,1)S(1)}, u32[]{:S(2)}, u32[]{:S(2)}) collective-permute-start(bf16[128,2,512]{0,2,1:T(8,128)(2,1)S(1)} %get-tuple-element.31), channel_id=1, source_target_pairs={{0,2},{1,3},{2,4},{3,5},{4,6},{5,7},{6,8},{7,9},{8,10},{9,11},{10,... | collective-permute-start | bytes 786440 | tf_op jit(solution)/shard_map/ppermute | solution.py:23
  67.5 16.6 %collective-permute-start.2 = (bf16[128,2,512]{0,2,1:T(8,128)(2,1)S(1)}, bf16[128,2,512]{0,2,1:T(8,128)(2,1)S(1)}, u32[]{:S(2)}, u32[]{:S(2)}) collective-permute-start(bf16[128,2,512]{0,2,1:T(8,128)(2,1)S(1)} %get-tuple-element.31), channel_id=1, source_target_pairs={{0,3},{1,4},{2,5},{3,6},{4,7},{5,8},{6,9},{7,10},{8,11},{9,12},{10... | collective-permute-start | bytes 786440 | tf_op jit(solution)/shard_map/ppermute | solution.py:23
  105.0 1.1 copy-start.14
  106.2 7.9 %copy-start.2 = (bf16[1,128,1536]{2,1,0:T(8,128)(2,1)S(1)}, bf16[1,128,1536]{2,1,0:T(8,128)(2,1)}, u32[]{:S(2)}) copy-start(bf16[1,128,1536]{2,1,0:T(8,128)(2,1)} %param.11) | copy-start | bytes 1179652
  107.5 9.8 %copy-start.8 = (f32[1536]{0:T(1024)S(1)}, f32[1536]{0:T(1024)}, u32[]{:S(2)}) copy-start(f32[1536]{0:T(1024)} %param.17) | copy-start | bytes 18436
  117.3 209.5 %copy-start.3 = (bf16[128,1536]{1,0:T(8,128)(2,1)}, bf16[128,1536]{1,0:T(8,128)(2,1)S(1)}, u32[]{:S(2)}) copy-start(bf16[128,1536]{1,0:T(8,128)(2,1)S(1)} %get-tuple-element.43) | copy-start | bytes 1179652
  120.5 11.4 %copy-start.12 = (bf16[1,1536,512]{2,1,0:T(8,128)(2,1)S(1)}, bf16[1,1536,512]{2,1,0:T(8,128)(2,1)}, u32[]{:S(2)}) copy-start(bf16[1,1536,512]{2,1,0:T(8,128)(2,1)} %param.20) | copy-start | bytes 4718596
  120.5 11.5 %copy-start.13 = (bf16[1,256,1536]{2,1,0:T(8,128)(2,1)S(1)}, bf16[1,256,1536]{2,1,0:T(8,128)(2,1)}, u32[]{:S(2)}) copy-start(bf16[1,256,1536]{2,1,0:T(8,128)(2,1)} %param.21) | copy-start | bytes 2359300
  120.5 96.7 %all-to-all-start.3 = ((bf16[32,40,1536]{2,1,0:T(8,128)(2,1)}), bf16[32,40,1536]{2,1,0:T(8,128)(2,1)}, u32[]{:S(2)}, u32[]{:S(2)}) async-start(bf16[32,40,1536]{2,1,0:T(8,128)(2,1)} %bitcast.166), calls=%async_computation.3 | async-start | bytes 7864320 | tf_op jit(solution)/shard_map/all_to_all | solution.py:166
  132.0 90.8 %collective-permute-start.3 = (bf16[1536,512]{1,0:T(8,128)(2,1)S(1)}, bf16[1536,512]{1,0:T(8,128)(2,1)}, u32[]{:S(2)}, u32[]{:S(2)}) collective-permute-start(bf16[1536,512]{1,0:T(8,128)(2,1)S(1)} %bitcast.195), channel_id=1, source_target_pairs={{0,1},{1,0},{2,3},{3,2},{4,5},{5,4},{6,7},{7,6},{8,9},{9,8},{10,11... | collective-permute-start | bytes 4718600 | tf_op jit(solution)/shard_map/ppermute | solution.py:120
  132.1 95.5 %collective-permute-start.4 = (bf16[256,1536]{1,0:T(8,128)(2,1)S(1)}, bf16[256,1536]{1,0:T(8,128)(2,1)}, u32[]{:S(2)}, u32[]{:S(2)}) collective-permute-start(bf16[256,1536]{1,0:T(8,128)(2,1)S(1)} %bitcast.196), channel_id=1, source_target_pairs={{0,1},{1,0},{2,3},{3,2},{4,5},{5,4},{6,7},{7,6},{8,9},{9,8},{10,11... | collective-permute-start | bytes 2359304 | tf_op jit(solution)/shard_map/ppermute | solution.py:120
  230.1 96.0 %copy-start.5 = (f32[128,32]{0,1:T(8,128)S(1)}, f32[128,32]{0,1:T(8,128)}, u32[]{:S(2)}) copy-start(f32[128,32]{0,1:T(8,128)} %get-tuple-element.16) | copy-start | bytes 49156
  326.1 2.2 copy-start.1
Sparse Core Ops, SparseCore 0:
  19.0 78.9 all-gather.2

commit v14 on v13

--- a/solution.py
+++ b/solution.py
@@ -136,7 +136,13 @@
         jnp.einsum("tgrd,ngd->tgrn", query, suffix_keys, preferred_element_type=jnp.float32) * scale
     )
     carry = merge_block(start_carry, scores, suffix_values, visible[:, None, None, :])
-    piece = lax.all_gather(prefix_cache[0], TENSOR, axis=0, tiled=True)
+    own_cache = prefix_cache[0]
+    other_cache = lax.ppermute(own_cache, "core", [(0, 1), (1, 0)])
+    low_core = lax.axis_index("core") == 0
+    pair = jnp.where(
+        low_core, jnp.concatenate([own_cache, other_cache], axis=0), jnp.concatenate([other_cache, own_cache], axis=0)
+    )
+    piece = lax.all_gather(pair, "chip", axis=0, tiled=True)
     piece, carry = lax.optimization_barrier((piece, carry))
     count = piece.shape[0]
     cached_keys = piece[:, 0].reshape(count, KV_HEADS, HEAD_DIM)

time: 336 us -> 354 us (1.054)
  waiting for transfers between devices: 127 us -> 148 us
  starting transfers between devices: 37 us -> 33.2 us
    all_gather x1, waiting for transfers between devices: 7.22 us -> 37.4 us  [shards(): piece = lax.all_gather(pair, 'chip', axis=0, tiled=True)]
    all_to_all x1, waiting for transfers between devices: 6.55 us -> 0.01 us  [shards(): lax.all_to_all(out_spread, 'dp', 0, 0, tiled=True)]
    all_to_all x1, starting transfers between devices: 11.4 us -> 7.55 us  [shards(): arrived = lax.all_to_all(outgoing, 'chip', 0, 0, tiled=True)]
  transfers between devices with their start and end apart: 10 -> 11, of which waited for: 7 -> 6; matrix products, arithmetic and copies ran while one was open for 14% -> 13% of each run, Pallas kernels for 0% -> 0%
where the time goes in v14:
time: 354 us; the launch traced here: 353 us
  waiting for transfers between devices  148 us (42%)
  blocking collectives  95.6 us (27%)
  starting transfers between devices  33.2 us (9%)
  matrix products  29.9 us (8%)
  other arithmetic  18.2 us (5%)
  between operations  14.5 us (4%)
  local copies, waits for them, and re-layouts  14.3 us (4%)
    all_to_all x1, blocking collectives, shards(): returned = lax.all_to_all(summed, 'chip', 0, 0, tiled=True)  95.6 us
    all_to_all x1, waiting for transfers between devices, shards(): arrived = lax.all_to_all(outgoing, 'chip', 0, 0, tiled=True)  83.6 us
    all_gather x1, waiting for transfers between devices, shards(): piece = lax.all_gather(pair, 'chip', axis=0, tiled=True)  37.4 us
    all_to_all x1, waiting for transfers between devices, shards(): lax.all_to_all(spread, 'dp', 0, 0, tiled=True).reshape(groups * rows, model)  12.2 us
    ppermute x3, starting transfers between devices, from_behind(): lax.ppermute(value, axis, [(source, source + steps) for source in range(f...  12.1 us
    ppermute x3, waiting for transfers between devices, from_behind(): lax.ppermute(value, axis, [(source, source + steps) for source in range(f...  9.61 us
    dot_general x2, matrix products, unit(): jnp.dot(block.reshape(chips * CAP, model), w_in, preferred_element_type=j...  9.12 us
    all_to_all x1, starting transfers between devices, shards(): arrived = lax.all_to_all(outgoing, 'chip', 0, 0, tiled=True)  7.55 us
  transfers between devices with their start and end apart: 11, of which 6 were waited for; matrix products, arithmetic and copies ran while one was open for 13% of the time, Pallas kernels for 0%

profile of v14, /device:TPU:32, one launch (start us, length us, event | category | flops | bytes accessed | tf_op | source)
XLA Modules:
  0.0 353.2 jit_solution(17177311306848053382)
XLA Ops:
  11.0 4.5 %all-to-all-start = ((bf16[4,128,1536]{2,1,0:T(8,128)(2,1)}), bf16[4,128,1536]{2,1,0:T(8,128)(2,1)S(1)}, u32[]{:S(2)}, u32[]{:S(2)}) async-start(bf16[4,128,1536]{2,1,0:T(8,128)(2,1)} %broadcast_in_dim.116), calls=%async_computation | async-start | bytes 3145728 | tf_op jit(solution)/shard_map/all_to_all | solution.py:94
  18.4 1.3 select_reduce_fusion
  19.7 1.4 fusion.65
  22.5 1.4 multiply_cosine_fusion
  23.9 12.2 %all-to-all-done = bf16[4,128,1536]{2,1,0:T(8,128)(2,1)S(1)} async-done(((bf16[4,128,1536]{2,1,0:T(8,128)(2,1)}), bf16[4,128,1536]{2,1,0:T(8,128)(2,1)S(1)}, u32[]{:S(2)}, u32[]{:S(2)}) %all-to-all-start) | async-done | bytes 1572896 | tf_op jit(solution)/shard_map/all_to_all | solution.py:94
  36.1 2.2 convolution_convert_fusion.3
  38.4 2.3 copy.47
  40.6 3.5 all-to-all-start.1
  47.9 1.5 broadcast_select_fusion
  49.4 4.7 %all-to-all-done.1 = bf16[4,128,640]{1,2,0:T(8,128)(2,1)S(1)} async-done(((bf16[4,128,640]{1,2,0:T(8,128)(2,1)}), bf16[4,128,640]{1,2,0:T(8,128)(2,1)S(1)}, u32[]{:S(2)}, u32[]{:S(2)}) %all-to-all-start.1) | async-done | bytes 655392 | tf_op jit(solution)/shard_map/all_to_all | solution.py:96
  54.1 2.5 broadcast_in_dim.124
  56.6 4.9 %all-to-all-start.2 = ((bf16[4,384,1536]{2,1,0:T(8,128)(2,1)}), bf16[4,384,1536]{2,1,0:T(8,128)(2,1)}, u32[]{:S(2)}, u32[]{:S(2)}) async-start(bf16[4,384,1536]{2,1,0:T(8,128)(2,1)} %broadcast_in_dim.124), calls=%async_computation.2 | async-start | bytes 9437184 | tf_op jit(solution)/shard_map/all_to_all | solution.py:92
  61.8 1.9 collective-permute-start.1
  63.7 3.8 %collective-permute-start.2 = (bf16[128,2,512]{0,2,1:T(8,128)(2,1)S(1)}, bf16[128,2,512]{0,2,1:T(8,128)(2,1)S(1)}, u32[]{:S(2)}, u32[]{:S(2)}) collective-permute-start(bf16[128,2,512]{0,2,1:T(8,128)(2,1)S(1)} %get-tuple-element.31), channel_id=1, source_target_pairs={{0,2},{1,3},{2,4},{3,5},{4,6},{5,7},{6,8},{7,9},{8,10},{9,11},{10,... | collective-permute-start | bytes 786440 | tf_op jit(solution)/shard_map/ppermute | solution.py:23
  67.5 6.4 %collective-permute-start.3 = (bf16[128,2,512]{0,2,1:T(8,128)(2,1)S(1)}, bf16[128,2,512]{0,2,1:T(8,128)(2,1)S(1)}, u32[]{:S(2)}, u32[]{:S(2)}) collective-permute-start(bf16[128,2,512]{0,2,1:T(8,128)(2,1)S(1)} %get-tuple-element.31), channel_id=1, source_target_pairs={{0,3},{1,4},{2,5},{3,6},{4,7},{5,8},{6,9},{7,10},{8,11},{9,12},{10... | collective-permute-start | bytes 786440 | tf_op jit(solution)/shard_map/ppermute | solution.py:23
  74.7 9.1 %collective-permute-done.3 = bf16[128,2,512]{0,2,1:T(8,128)(2,1)S(1)} collective-permute-done((bf16[128,2,512]{0,2,1:T(8,128)(2,1)S(1)}, bf16[128,2,512]{0,2,1:T(8,128)(2,1)S(1)}, u32[]{:S(2)}, u32[]{:S(2)}) %collective-permute-start.3) | collective-permute-done | bytes 262176 | tf_op jit(solution)/shard_map/ppermute | solution.py:23
  86.3 1.5 fusion.5
  87.8 2.6 fusion.29
  90.4 37.4 %all-gather.2.cloned.1.call-done = bf16[512,2,512]{2,1,0:T(2,128)(2,1)} async-done(((bf16[16,2,512]{2,1,0:T(2,128)(2,1)}), bf16[512,2,512]{2,1,0:T(2,128)(2,1)}) %all-gather.2.cloned.1.call-update) | async-done | bytes 1048592 | tf_op jit(solution)/shard_map/all_gather | solution.py:145
  127.8 3.4 fusion.82
  131.2 1.3 copy.52
  132.5 1.3 copy.53
  136.1 1.3 fusion.36
  137.4 3.2 fusion.42
  140.7 3.2 convolution_convert_fusion
  143.9 7.5 %all-to-all-start.3 = ((bf16[32,40,1536]{2,1,0:T(8,128)(2,1)}), bf16[32,40,1536]{2,1,0:T(8,128)(2,1)}, u32[]{:S(2)}, u32[]{:S(2)}) async-start(bf16[32,40,1536]{2,1,0:T(8,128)(2,1)} %bitcast.165), calls=%async_computation.3 | async-start | bytes 7864320 | tf_op jit(solution)/shard_map/all_to_all | solution.py:172
  152.1 83.6 %all-to-all-done.3 = bf16[32,40,1536]{2,1,0:T(8,128)(2,1)} async-done(((bf16[32,40,1536]{2,1,0:T(8,128)(2,1)}), bf16[32,40,1536]{2,1,0:T(8,128)(2,1)}, u32[]{:S(2)}, u32[]{:S(2)}) %all-to-all-start.3) | async-done | bytes 3932192 | tf_op jit(solution)/shard_map/all_to_all | solution.py:172
  235.6 4.3 %fusion.70 = f32[1280,512]{1,0:T(8,128)S(1)} fusion(bf16[1280,1536]{1,0:T(8,128)(2,1)} %bitcast.52, bf16[1,1536,512]{2,1,0:T(8,128)(2,1)S(1)} %copy-done.11), kind=kOutput, calls=%fused_computation.113 | convolution fusion | flops 2013265920 | bytes 8126464 | tf_op jit(solution)/shard_map/dot_general | solution.py:175
  241.2 4.8 %fusion.84 = f32[1280,512]{1,0:T(8,128)S(1)} fusion(bf16[1280,1536]{1,0:T(8,128)(2,1)} %bitcast.52, bf16[1536,512]{1,0:T(8,128)(2,1)} %collective-permute-done.4), kind=kOutput, calls=%fused_computation.127 | convolution fusion | flops 2013265920 | bytes 8126464 | tf_op jit(solution)/shard_map/dot_general | solution.py:175
  246.0 2.5 add_convert_fusion
  248.6 95.6 %all_to_all.25 = bf16[32,40,1536]{2,1,0:T(8,128)(2,1)S(1)} all-to-all(bf16[32,40,1536]{2,1,0:T(8,128)(2,1)S(1)} %bitcast.169), channel_id=1, replica_groups=mesh['dp'=4,'chip'=32,'core'=2] {'chip'}, dimensions={0} | all-to-all | bytes 7864320 | tf_op jit(solution)/shard_map/all_to_all | solution.py:183
  344.9 1.5 fusion.17
  (84 shorter events, 19.9 us)
Async XLA Ops:
  7.2 29.0 %copy-start = (bf16[1536,640]{1,0:T(8,128)(2,1)S(1)}, bf16[1536,640]{1,0:T(8,128)(2,1)}, u32[]{:S(2)}) copy-start(bf16[1536,640]{1,0:T(8,128)(2,1)} %param.13) | copy-start | bytes 5898244
  7.2 9.4 %copy-start.9 = (s32[1,256]{1,0:T(1,128)S(1)}, s32[1,256]{1,0:T(1,128)}, u32[]{:S(2)}) copy-start(s32[1,256]{1,0:T(1,128)} %param.16) | copy-start | bytes 3076
  7.2 11.2 %copy-start.10 = (f32[1,128,8]{1,2,0:T(8,128)S(1)}, f32[1,128,8]{1,2,0:T(8,128)}, u32[]{:S(2)}) copy-start(f32[1,128,8]{1,2,0:T(8,128)} %param.19) | copy-start | bytes 12292
  11.0 25.2 %all-to-all-start = ((bf16[4,128,1536]{2,1,0:T(8,128)(2,1)}), bf16[4,128,1536]{2,1,0:T(8,128)(2,1)S(1)}, u32[]{:S(2)}, u32[]{:S(2)}) async-start(bf16[4,128,1536]{2,1,0:T(8,128)(2,1)} %broadcast_in_dim.116), calls=%async_computation | async-start | bytes 3145728 | tf_op jit(solution)/shard_map/all_to_all | solution.py:94
  15.4 32.5 %collective-permute-start = (bf16[8,2,512]{2,1,0:T(2,128)(2,1)}, bf16[8,2,512]{2,1,0:T(2,128)(2,1)}, u32[]{:S(2)}, u32[]{:S(2)}) collective-permute-start(bf16[8,2,512]{2,1,0:T(2,128)(2,1)} %bitcast.1), channel_id=1, source_target_pairs={{0,1},{1,0},{2,3},{3,2},{4,5},{5,4},{6,7},{7,6},{8,9},{9,8},{10,11... | collective-permute-start | bytes 49160 | tf_op jit(solution)/shard_map/ppermute | solution.py:140
  18.4 4.1 %copy-start.7 = (s32[256]{0:T(256)}, s32[256]{0:T(256)S(1)}, u32[]{:S(2)}) copy-start(s32[256]{0:T(256)S(1)} %add_bitcast_fusion.1) | copy-start | bytes 3076
  19.7 2.8 copy-start.6
  38.4 15.8 %copy-start.4 = (bf16[384,1536]{1,0:T(8,128)(2,1)S(1)}, bf16[384,1536]{1,0:T(8,128)(2,1)}, u32[]{:S(2)}) copy-start(bf16[384,1536]{1,0:T(8,128)(2,1)} %param.14) | copy-start | bytes 3538948
  40.6 13.5 %all-to-all-start.1 = ((bf16[4,128,640]{1,2,0:T(8,128)(2,1)}), bf16[4,128,640]{1,2,0:T(8,128)(2,1)S(1)}, u32[]{:S(2)}, u32[]{:S(2)}) async-start(bf16[4,128,640]{1,2,0:T(8,128)(2,1)} %copy.47), calls=%async_computation.1 | async-start | bytes 1310720 | tf_op jit(solution)/shard_map/all_to_all | solution.py:96
  44.1 83.7 %all-gather.2.cloned.1.call-start = ((), (), s32[]{:S(2)}) async-start(), calls=%async_computation.5 | async-start | bytes 1081344 | tf_op jit(solution)/shard_map/all_gather | solution.py:145
  56.6 80.8 %all-to-all-start.2 = ((bf16[4,384,1536]{2,1,0:T(8,128)(2,1)}), bf16[4,384,1536]{2,1,0:T(8,128)(2,1)}, u32[]{:S(2)}, u32[]{:S(2)}) async-start(bf16[4,384,1536]{2,1,0:T(8,128)(2,1)} %broadcast_in_dim.124), calls=%async_computation.2 | async-start | bytes 9437184 | tf_op jit(solution)/shard_map/all_to_all | solution.py:92
  61.8 12.4 %collective-permute-start.1 = (bf16[128,2,512]{0,2,1:T(8,128)(2,1)S(1)}, bf16[128,2,512]{0,2,1:T(8,128)(2,1)S(1)}, u32[]{:S(2)}, u32[]{:S(2)}) collective-permute-start(bf16[128,2,512]{0,2,1:T(8,128)(2,1)S(1)} %get-tuple-element.31), channel_id=1, source_target_pairs={{0,1},{1,2},{2,3},{3,4},{4,5},{5,6},{6,7},{7,8},{8,9},{9,10},{10,1... | collective-permute-start | bytes 786440 | tf_op jit(solution)/shard_map/ppermute | solution.py:23
  63.7 11.0 %collective-permute-start.2 = (bf16[128,2,512]{0,2,1:T(8,128)(2,1)S(1)}, bf16[128,2,512]{0,2,1:T(8,128)(2,1)S(1)}, u32[]{:S(2)}, u32[]{:S(2)}) collective-permute-start(bf16[128,2,512]{0,2,1:T(8,128)(2,1)S(1)} %get-tuple-element.31), channel_id=1, source_target_pairs={{0,2},{1,3},{2,4},{3,5},{4,6},{5,7},{6,8},{7,9},{8,10},{9,11},{10,... | collective-permute-start | bytes 786440 | tf_op jit(solution)/shard_map/ppermute | solution.py:23
  67.5 16.3 %collective-permute-start.3 = (bf16[128,2,512]{0,2,1:T(8,128)(2,1)S(1)}, bf16[128,2,512]{0,2,1:T(8,128)(2,1)S(1)}, u32[]{:S(2)}, u32[]{:S(2)}) collective-permute-start(bf16[128,2,512]{0,2,1:T(8,128)(2,1)S(1)} %get-tuple-element.31), channel_id=1, source_target_pairs={{0,3},{1,4},{2,5},{3,6},{4,7},{5,8},{6,9},{7,10},{8,11},{9,12},{10... | collective-permute-start | bytes 786440 | tf_op jit(solution)/shard_map/ppermute | solution.py:23
  134.9 1.1 copy-start.13
  136.1 1.4 copy-start.2
  137.4 3.3 copy-start.8
  140.7 204.2 %copy-start.3 = (bf16[128,1536]{1,0:T(8,128)(2,1)}, bf16[128,1536]{1,0:T(8,128)(2,1)S(1)}, u32[]{:S(2)}) copy-start(bf16[128,1536]{1,0:T(8,128)(2,1)S(1)} %get-tuple-element.43) | copy-start | bytes 1179652
  143.9 7.6 %copy-start.11 = (bf16[1,1536,512]{2,1,0:T(8,128)(2,1)S(1)}, bf16[1,1536,512]{2,1,0:T(8,128)(2,1)}, u32[]{:S(2)}) copy-start(bf16[1,1536,512]{2,1,0:T(8,128)(2,1)} %param.20) | copy-start | bytes 4718596
  143.9 7.7 %copy-start.12 = (bf16[1,256,1536]{2,1,0:T(8,128)(2,1)S(1)}, bf16[1,256,1536]{2,1,0:T(8,128)(2,1)}, u32[]{:S(2)}) copy-start(bf16[1,256,1536]{2,1,0:T(8,128)(2,1)} %param.21) | copy-start | bytes 2359300
  143.9 91.8 %all-to-all-start.3 = ((bf16[32,40,1536]{2,1,0:T(8,128)(2,1)}), bf16[32,40,1536]{2,1,0:T(8,128)(2,1)}, u32[]{:S(2)}, u32[]{:S(2)}) async-start(bf16[32,40,1536]{2,1,0:T(8,128)(2,1)} %bitcast.165), calls=%async_computation.3 | async-start | bytes 7864320 | tf_op jit(solution)/shard_map/all_to_all | solution.py:172
  151.5 89.7 %collective-permute-start.4 = (bf16[1536,512]{1,0:T(8,128)(2,1)S(1)}, bf16[1536,512]{1,0:T(8,128)(2,1)}, u32[]{:S(2)}, u32[]{:S(2)}) collective-permute-start(bf16[1536,512]{1,0:T(8,128)(2,1)S(1)} %bitcast.192), channel_id=1, source_target_pairs={{0,1},{1,0},{2,3},{3,2},{4,5},{5,4},{6,7},{7,6},{8,9},{9,8},{10,11... | collective-permute-start | bytes 4718600 | tf_op jit(solution)/shard_map/ppermute | solution.py:120
  151.6 94.5 %collective-permute-start.5 = (bf16[256,1536]{1,0:T(8,128)(2,1)S(1)}, bf16[256,1536]{1,0:T(8,128)(2,1)}, u32[]{:S(2)}, u32[]{:S(2)}) collective-permute-start(bf16[256,1536]{1,0:T(8,128)(2,1)S(1)} %bitcast.193), channel_id=1, source_target_pairs={{0,1},{1,0},{2,3},{3,2},{4,5},{5,4},{6,7},{7,6},{8,9},{9,8},{10,11... | collective-permute-start | bytes 2359304 | tf_op jit(solution)/shard_map/ppermute | solution.py:120
  248.5 95.6 %copy-start.5 = (f32[128,32]{0,1:T(8,128)S(1)}, f32[128,32]{0,1:T(8,128)}, u32[]{:S(2)}) copy-start(f32[128,32]{0,1:T(8,128)} %get-tuple-element.16) | copy-start | bytes 49156
  344.2 2.2 copy-start.1
Sparse Core Ops, SparseCore 0:
  49.6 78.2 all-gather.1

commit v15 on v13

--- a/solution.py
+++ b/solution.py
@@ -171,8 +171,17 @@
         produced = jnp.dot(activated, w_out, preferred_element_type=jnp.float32).astype(jnp.bfloat16)
         return produced.reshape(chips, CAP, model)
 
-    own_part = unit(arrived, expert_in[0], expert_out[0])
-    partner = unit(arrived, other_in, other_out)
+    both_in = jnp.concatenate([expert_in[0], other_in], axis=1)
+    inner_both = jnp.dot(arrived.reshape(chips * CAP, model), both_in, preferred_element_type=jnp.float32)
+    width = expert_in.shape[2]
+
+    def finish(inner, w_out):
+        activated = (jax.nn.silu(inner[:, :unit_ff]) * inner[:, unit_ff:]).astype(jnp.bfloat16)
+        produced = jnp.dot(activated, w_out, preferred_element_type=jnp.float32).astype(jnp.bfloat16)
+        return produced.reshape(chips, CAP, model)
+
+    own_part = finish(inner_both[:, :width], expert_out[0])
+    partner = finish(inner_both[:, width:], other_out)
     summed = (own_part.astype(jnp.float32) + partner.astype(jnp.float32)).astype(jnp.bfloat16)
     returned = lax.all_to_all(summed, "chip", 0, 0, tiled=True)
     returned = returned.reshape(chips * CAP, model)

time: 336 us -> 334 us (level)
    dot_general x4 -> x3, matrix products: 12.9 us -> 10.6 us  [the longest x1 6.88 us: shards(): jnp.dot(arrived.reshape(chips * CAP, model), both_in, preferred_element_t...]
  transfers between devices with their start and end apart: 10 -> 10, of which waited for: 7 -> 8; matrix products, arithmetic and copies ran while one was open for 14% -> 13% of each run, Pallas kernels for 0% -> 0%
where the time goes in v15:
time: 334 us; the launch traced here: 333 us
  waiting for transfers between devices  127 us (38%)
  blocking collectives  96 us (29%)
  starting transfers between devices  37 us (11%)
  matrix products  27.6 us (8%)
  other arithmetic  16.1 us (5%)
  local copies, waits for them, and re-layouts  14.8 us (4%)
  between operations  14.4 us (4%)
    all_to_all x1, blocking collectives, shards(): returned = lax.all_to_all(summed, 'chip', 0, 0, tiled=True)  96 us
    all_to_all x1, waiting for transfers between devices, shards(): arrived = lax.all_to_all(outgoing, 'chip', 0, 0, tiled=True)  81.6 us
    ppermute x3, starting transfers between devices, from_behind(): lax.ppermute(value, axis, [(source, source + steps) for source in range(f...  12.1 us
    all_to_all x1, waiting for transfers between devices, shards(): lax.all_to_all(spread, 'dp', 0, 0, tiled=True).reshape(groups * rows, model)  11.4 us
    all_to_all x1, starting transfers between devices, shards(): arrived = lax.all_to_all(outgoing, 'chip', 0, 0, tiled=True)  11.4 us
    ppermute x3, waiting for transfers between devices, from_behind(): lax.ppermute(value, axis, [(source, source + steps) for source in range(f...  9.92 us
    all_gather x1, waiting for transfers between devices, shards(): piece = lax.all_gather(prefix_cache[0], TENSOR, axis=0, tiled=True)  7.22 us
    dot_general x1, matrix products, shards(): jnp.dot(arrived.reshape(chips * CAP, model), both_in, preferred_element_t...  6.88 us
  transfers between devices with their start and end apart: 10, of which 8 were waited for; matrix products, arithmetic and copies ran while one was open for 13% of the time, Pallas kernels for 0%

profile of v15, /device:TPU:32, one launch (start us, length us, event | category | flops | bytes accessed | tf_op | source)
XLA Modules:
  0.0 332.9 jit_solution(2400521975396106447)
XLA Ops:
  7.2 1.3 fusion.43
  11.0 4.5 %all-to-all-start = ((bf16[4,128,1536]{2,1,0:T(8,128)(2,1)}), bf16[4,128,1536]{2,1,0:T(8,128)(2,1)S(1)}, u32[]{:S(2)}, u32[]{:S(2)}) async-start(bf16[4,128,1536]{2,1,0:T(8,128)(2,1)} %broadcast_in_dim.116), calls=%async_computation | async-start | bytes 3145728 | tf_op jit(solution)/shard_map/all_to_all | solution.py:94
  19.1 1.3 select_reduce_fusion
  23.3 1.4 multiply_cosine_fusion
  24.7 11.4 %all-to-all-done = bf16[4,128,1536]{2,1,0:T(8,128)(2,1)S(1)} async-done(((bf16[4,128,1536]{2,1,0:T(8,128)(2,1)}), bf16[4,128,1536]{2,1,0:T(8,128)(2,1)S(1)}, u32[]{:S(2)}, u32[]{:S(2)}) %all-to-all-start) | async-done | bytes 1572896 | tf_op jit(solution)/shard_map/all_to_all | solution.py:94
  36.1 2.2 convolution_convert_fusion.3
  38.4 2.3 copy.49
  40.6 3.5 %all-to-all-start.1 = ((bf16[4,128,640]{1,2,0:T(8,128)(2,1)}), bf16[4,128,640]{1,2,0:T(8,128)(2,1)S(1)}, u32[]{:S(2)}, u32[]{:S(2)}) async-start(bf16[4,128,640]{1,2,0:T(8,128)(2,1)} %copy.49), calls=%async_computation.1 | async-start | bytes 1310720 | tf_op jit(solution)/shard_map/all_to_all | solution.py:96
  47.6 6.5 %all-to-all-done.1 = bf16[4,128,640]{1,2,0:T(8,128)(2,1)S(1)} async-done(((bf16[4,128,640]{1,2,0:T(8,128)(2,1)}), bf16[4,128,640]{1,2,0:T(8,128)(2,1)S(1)}, u32[]{:S(2)}, u32[]{:S(2)}) %all-to-all-start.1) | async-done | bytes 655392 | tf_op jit(solution)/shard_map/all_to_all | solution.py:96
  54.1 2.5 broadcast_in_dim.124
  56.6 4.9 %all-to-all-start.2 = ((bf16[4,384,1536]{2,1,0:T(8,128)(2,1)}), bf16[4,384,1536]{2,1,0:T(8,128)(2,1)}, u32[]{:S(2)}, u32[]{:S(2)}) async-start(bf16[4,384,1536]{2,1,0:T(8,128)(2,1)} %broadcast_in_dim.124), calls=%async_computation.2 | async-start | bytes 9437184 | tf_op jit(solution)/shard_map/all_to_all | solution.py:92
  61.8 1.9 collective-permute-start
  63.7 3.8 %collective-permute-start.1 = (bf16[128,2,512]{0,2,1:T(8,128)(2,1)S(1)}, bf16[128,2,512]{0,2,1:T(8,128)(2,1)S(1)}, u32[]{:S(2)}, u32[]{:S(2)}) collective-permute-start(bf16[128,2,512]{0,2,1:T(8,128)(2,1)S(1)} %get-tuple-element.31), channel_id=1, source_target_pairs={{0,2},{1,3},{2,4},{3,5},{4,6},{5,7},{6,8},{7,9},{8,10},{9,11},{10,... | collective-permute-start | bytes 786440 | tf_op jit(solution)/shard_map/ppermute | solution.py:23
  67.5 6.4 %collective-permute-start.2 = (bf16[128,2,512]{0,2,1:T(8,128)(2,1)S(1)}, bf16[128,2,512]{0,2,1:T(8,128)(2,1)S(1)}, u32[]{:S(2)}, u32[]{:S(2)}) collective-permute-start(bf16[128,2,512]{0,2,1:T(8,128)(2,1)S(1)} %get-tuple-element.31), channel_id=1, source_target_pairs={{0,3},{1,4},{2,5},{3,6},{4,7},{5,8},{6,9},{7,10},{8,11},{9,12},{10... | collective-permute-start | bytes 786440 | tf_op jit(solution)/shard_map/ppermute | solution.py:23
  74.7 9.5 %collective-permute-done.2 = bf16[128,2,512]{0,2,1:T(8,128)(2,1)S(1)} collective-permute-done((bf16[128,2,512]{0,2,1:T(8,128)(2,1)S(1)}, bf16[128,2,512]{0,2,1:T(8,128)(2,1)S(1)}, u32[]{:S(2)}, u32[]{:S(2)}) %collective-permute-start.2) | collective-permute-done | bytes 262176 | tf_op jit(solution)/shard_map/ppermute | solution.py:23
  86.6 1.5 fusion.5
  88.1 2.6 fusion.33
  90.7 7.2 %all-gather.3.cloned.1.call-done = bf16[1,512,2,512]{3,2,0,1:T(2,128)(2,1)} async-done(((bf16[1,8,2,512]{3,2,0,1:T(2,128)(2,1)}), bf16[1,512,2,512]{3,2,0,1:T(2,128)(2,1)}) %all-gather.3.cloned.1.call-update) | async-done | bytes 1048592 | tf_op jit(solution)/shard_map/all_gather | solution.py:139
  98.0 3.4 %fusion.85 = (bf16[512,1,512]{2,1,0:T(2,128)(2,1)S(1)}, bf16[512,1,512]{2,1,0:T(2,128)(2,1)S(1)}) fusion(bf16[512,2,512]{2,1,0:T(2,128)(2,1)} %bitcast.165), kind=kLoop, calls=%fused_computation.127 | loop fusion | bytes 2097152 | tf_op jit(solution)/shard_map/slice | solution.py:142
  101.3 1.3 copy.54
  102.6 1.3 copy.55
  106.2 1.3 fusion.40
  107.5 6.5 %all-to-all-done.2 = bf16[4,384,1536]{2,1,0:T(8,128)(2,1)} async-done(((bf16[4,384,1536]{2,1,0:T(8,128)(2,1)}), bf16[4,384,1536]{2,1,0:T(8,128)(2,1)}, u32[]{:S(2)}, u32[]{:S(2)}) %all-to-all-start.2) | async-done | bytes 4718624 | tf_op jit(solution)/shard_map/all_to_all | solution.py:92
  114.1 3.2 fusion.46
  117.3 3.2 convolution_convert_fusion
  120.5 11.4 %all-to-all-start.3 = ((bf16[32,40,1536]{2,1,0:T(8,128)(2,1)}), bf16[32,40,1536]{2,1,0:T(8,128)(2,1)}, u32[]{:S(2)}, u32[]{:S(2)}) async-start(bf16[32,40,1536]{2,1,0:T(8,128)(2,1)} %bitcast.162), calls=%async_computation.3 | async-start | bytes 7864320 | tf_op jit(solution)/shard_map/all_to_all | solution.py:166
  132.6 3.0 collective-permute-done.3
  135.6 81.6 %all-to-all-done.3 = bf16[32,40,1536]{2,1,0:T(8,128)(2,1)} async-done(((bf16[32,40,1536]{2,1,0:T(8,128)(2,1)}), bf16[32,40,1536]{2,1,0:T(8,128)(2,1)}, u32[]{:S(2)}, u32[]{:S(2)}) %all-to-all-start.3) | async-done | bytes 3932192 | tf_op jit(solution)/shard_map/all_to_all | solution.py:166
  217.2 6.9 %fusion.8 = f32[1280,1024]{1,0:T(8,128)S(1)} fusion(bf16[1280,1536]{1,0:T(8,128)(2,1)} %bitcast.53, bf16[1536,512]{1,0:T(8,128)(2,1)} %collective-permute-done.3, bf16[1536,512]{1,0:T(8,128)(2,1)S(1)} %bitcast.192), kind=kOutput, calls=%fused_computation.15 | convolution fusion | flops 4032823296 | bytes 12320768 | tf_op jit(solution)/shard_map/dot_general | solution.py:175
  225.4 2.5 add_convert_fusion
  227.9 96.0 %all_to_all.25 = bf16[32,40,1536]{2,1,0:T(8,128)(2,1)S(1)} all-to-all(bf16[32,40,1536]{2,1,0:T(8,128)(2,1)S(1)} %bitcast.167), channel_id=1, replica_groups=mesh['dp'=4,'chip'=32,'core'=2] {'chip'}, dimensions={0} | all-to-all | bytes 7864320 | tf_op jit(solution)/shard_map/all_to_all | solution.py:186
  324.6 1.5 fusion.21
  (82 shorter events, 20.6 us)
Async XLA Ops:
  7.2 29.0 %copy-start = (bf16[1536,640]{1,0:T(8,128)(2,1)S(1)}, bf16[1536,640]{1,0:T(8,128)(2,1)}, u32[]{:S(2)}) copy-start(bf16[1536,640]{1,0:T(8,128)(2,1)} %param.13) | copy-start | bytes 5898244
  7.2 10.1 %copy-start.9 = (s32[1,256]{1,0:T(1,128)S(1)}, s32[1,256]{1,0:T(1,128)}, u32[]{:S(2)}) copy-start(s32[1,256]{1,0:T(1,128)} %param.16) | copy-start | bytes 3076
  7.2 12.0 %copy-start.10 = (f32[1,128,8]{1,2,0:T(8,128)S(1)}, f32[1,128,8]{1,2,0:T(8,128)}, u32[]{:S(2)}) copy-start(f32[1,128,8]{1,2,0:T(8,128)} %param.19) | copy-start | bytes 12292
  11.0 25.2 %all-to-all-start = ((bf16[4,128,1536]{2,1,0:T(8,128)(2,1)}), bf16[4,128,1536]{2,1,0:T(8,128)(2,1)S(1)}, u32[]{:S(2)}, u32[]{:S(2)}) async-start(bf16[4,128,1536]{2,1,0:T(8,128)(2,1)} %broadcast_in_dim.116), calls=%async_computation | async-start | bytes 3145728 | tf_op jit(solution)/shard_map/all_to_all | solution.py:94
  15.4 82.5 %all-gather.3.cloned.1.call-start = ((), (), s32[]{:S(2)}) async-start(), calls=%async_computation.5 | async-start | bytes 1064960 | tf_op jit(solution)/shard_map/all_gather | solution.py:139
  20.5 2.9 copy-start.6
  20.5 0.5 copy-start.11
  22.4 0.9 copy-start.7
  38.4 15.8 %copy-start.4 = (bf16[384,1536]{1,0:T(8,128)(2,1)S(1)}, bf16[384,1536]{1,0:T(8,128)(2,1)}, u32[]{:S(2)}) copy-start(bf16[384,1536]{1,0:T(8,128)(2,1)} %param.14) | copy-start | bytes 3538948
  40.6 13.5 %all-to-all-start.1 = ((bf16[4,128,640]{1,2,0:T(8,128)(2,1)}), bf16[4,128,640]{1,2,0:T(8,128)(2,1)S(1)}, u32[]{:S(2)}, u32[]{:S(2)}) async-start(bf16[4,128,640]{1,2,0:T(8,128)(2,1)} %copy.49), calls=%async_computation.1 | async-start | bytes 1310720 | tf_op jit(solution)/shard_map/all_to_all | solution.py:96
  56.6 57.4 %all-to-all-start.2 = ((bf16[4,384,1536]{2,1,0:T(8,128)(2,1)}), bf16[4,384,1536]{2,1,0:T(8,128)(2,1)}, u32[]{:S(2)}, u32[]{:S(2)}) async-start(bf16[4,384,1536]{2,1,0:T(8,128)(2,1)} %broadcast_in_dim.124), calls=%async_computation.2 | async-start | bytes 9437184 | tf_op jit(solution)/shard_map/all_to_all | solution.py:92
  61.8 12.4 %collective-permute-start = (bf16[128,2,512]{0,2,1:T(8,128)(2,1)S(1)}, bf16[128,2,512]{0,2,1:T(8,128)(2,1)S(1)}, u32[]{:S(2)}, u32[]{:S(2)}) collective-permute-start(bf16[128,2,512]{0,2,1:T(8,128)(2,1)S(1)} %get-tuple-element.31), channel_id=1, source_target_pairs={{0,1},{1,2},{2,3},{3,4},{4,5},{5,6},{6,7},{7,8},{8,9},{9,10},{10,1... | collective-permute-start | bytes 786440 | tf_op jit(solution)/shard_map/ppermute | solution.py:23
  63.7 11.0 %collective-permute-start.1 = (bf16[128,2,512]{0,2,1:T(8,128)(2,1)S(1)}, bf16[128,2,512]{0,2,1:T(8,128)(2,1)S(1)}, u32[]{:S(2)}, u32[]{:S(2)}) collective-permute-start(bf16[128,2,512]{0,2,1:T(8,128)(2,1)S(1)} %get-tuple-element.31), channel_id=1, source_target_pairs={{0,2},{1,3},{2,4},{3,5},{4,6},{5,7},{6,8},{7,9},{8,10},{9,11},{10,... | collective-permute-start | bytes 786440 | tf_op jit(solution)/shard_map/ppermute | solution.py:23
  67.5 16.6 %collective-permute-start.2 = (bf16[128,2,512]{0,2,1:T(8,128)(2,1)S(1)}, bf16[128,2,512]{0,2,1:T(8,128)(2,1)S(1)}, u32[]{:S(2)}, u32[]{:S(2)}) collective-permute-start(bf16[128,2,512]{0,2,1:T(8,128)(2,1)S(1)} %get-tuple-element.31), channel_id=1, source_target_pairs={{0,3},{1,4},{2,5},{3,6},{4,7},{5,8},{6,9},{7,10},{8,11},{9,12},{10... | collective-permute-start | bytes 786440 | tf_op jit(solution)/shard_map/ppermute | solution.py:23
  105.0 1.1 copy-start.14
  106.2 7.9 %copy-start.2 = (bf16[1,128,1536]{2,1,0:T(8,128)(2,1)S(1)}, bf16[1,128,1536]{2,1,0:T(8,128)(2,1)}, u32[]{:S(2)}) copy-start(bf16[1,128,1536]{2,1,0:T(8,128)(2,1)} %param.11) | copy-start | bytes 1179652
  107.5 9.8 %copy-start.8 = (f32[1536]{0:T(1024)S(1)}, f32[1536]{0:T(1024)}, u32[]{:S(2)}) copy-start(f32[1536]{0:T(1024)} %param.17) | copy-start | bytes 18436
  117.3 207.3 %copy-start.3 = (bf16[128,1536]{1,0:T(8,128)(2,1)}, bf16[128,1536]{1,0:T(8,128)(2,1)S(1)}, u32[]{:S(2)}) copy-start(bf16[128,1536]{1,0:T(8,128)(2,1)S(1)} %get-tuple-element.43) | copy-start | bytes 1179652
  120.5 11.4 %copy-start.12 = (bf16[1,1536,512]{2,1,0:T(8,128)(2,1)S(1)}, bf16[1,1536,512]{2,1,0:T(8,128)(2,1)}, u32[]{:S(2)}) copy-start(bf16[1,1536,512]{2,1,0:T(8,128)(2,1)} %param.20) | copy-start | bytes 4718596
  120.5 11.5 %copy-start.13 = (bf16[1,256,1536]{2,1,0:T(8,128)(2,1)S(1)}, bf16[1,256,1536]{2,1,0:T(8,128)(2,1)}, u32[]{:S(2)}) copy-start(bf16[1,256,1536]{2,1,0:T(8,128)(2,1)} %param.21) | copy-start | bytes 2359300
  120.5 96.7 %all-to-all-start.3 = ((bf16[32,40,1536]{2,1,0:T(8,128)(2,1)}), bf16[32,40,1536]{2,1,0:T(8,128)(2,1)}, u32[]{:S(2)}, u32[]{:S(2)}) async-start(bf16[32,40,1536]{2,1,0:T(8,128)(2,1)} %bitcast.162), calls=%async_computation.3 | async-start | bytes 7864320 | tf_op jit(solution)/shard_map/all_to_all | solution.py:166
  132.0 3.6 %collective-permute-start.3 = (bf16[1536,512]{1,0:T(8,128)(2,1)S(1)}, bf16[1536,512]{1,0:T(8,128)(2,1)}, u32[]{:S(2)}, u32[]{:S(2)}) collective-permute-start(bf16[1536,512]{1,0:T(8,128)(2,1)S(1)} %bitcast.191), channel_id=1, source_target_pairs={{0,1},{1,0},{2,3},{3,2},{4,5},{5,4},{6,7},{7,6},{8,9},{9,8},{10,11... | collective-permute-start | bytes 4718600 | tf_op jit(solution)/shard_map/ppermute | solution.py:120
  132.1 93.3 %collective-permute-start.4 = (bf16[256,1536]{1,0:T(8,128)(2,1)S(1)}, bf16[256,1536]{1,0:T(8,128)(2,1)}, u32[]{:S(2)}, u32[]{:S(2)}) collective-permute-start(bf16[256,1536]{1,0:T(8,128)(2,1)S(1)} %bitcast.193), channel_id=1, source_target_pairs={{0,1},{1,0},{2,3},{3,2},{4,5},{5,4},{6,7},{7,6},{8,9},{9,8},{10,11... | collective-permute-start | bytes 2359304 | tf_op jit(solution)/shard_map/ppermute | solution.py:120
  227.9 96.0 %copy-start.5 = (f32[128,32]{0,1:T(8,128)S(1)}, f32[128,32]{0,1:T(8,128)}, u32[]{:S(2)}) copy-start(f32[128,32]{0,1:T(8,128)} %get-tuple-element.16) | copy-start | bytes 49156
  323.9 2.2 copy-start.1
Sparse Core Ops, SparseCore 0:
  19.0 78.9 all-gather.2
